TPU v7x, 32 devices: a whole 2x2x4 slice. The times are simulated.
32 devices in a mesh: dp: 16 (over z, x, core), tensor: 2 (over y).
Axes of the slice: x: 2, y: 2, z: 4, core: 2. Of those that a mesh axis runs over, the one named last changes fastest.
Arguments:
- inputs: float32 [64, 320, 1024], P(('dp', 'tensor')), may hold values from -6 to 6
- key_mask: int32 [64, 256], P('dp'), may hold values 0 or 1
- ln1_gain: float32 [1024], P('dp'), may hold values from 0.1 to 1.9
- ln1_bias: float32 [1024], P('dp'), may hold values from -1.8 to 1.8
- w_qkv: float32 [3, 1024, 1024], P(None, 'dp', 'tensor'), may hold values from -0.1875 to 0.1875
- qv_bias: float32 [2, 1024], P(None, 'dp'), may hold values from -0.6 to 0.6
- w_proj: float32 [1024, 1024], P('tensor', 'dp'), may hold values from -3.5 to 3.5
- proj_bias: float32 [1024], P('dp'), may hold values from -1.8 to 1.8
- ln2_gain: float32 [1024], P('dp'), may hold values from 0.1 to 1.9
- ln2_bias: float32 [1024], P('dp'), may hold values from -1.8 to 1.8
- w_fc1: float32 [1024, 4096], P('dp', 'tensor'), may hold values from -0.1875 to 0.1875
- fc1_bias: float32 [4096], P('dp'), may hold values from -3 to 3
- w_fc2: float32 [4096, 1024], P('tensor', 'dp'), may hold values from -0.09375 to 0.09375
- fc2_bias: float32 [1024], P('dp'), may hold values from -1.8 to 1.8
- out_grad: float32 [64, 320, 1024], P(('dp', 'tensor')), may hold values from -6 to 6
Outputs:
- activations: float32 [64, 320, 1024], P(('dp', 'tensor'))
- input_grad: float32 [64, 320, 1024], P(('dp', 'tensor'))
- ln1_gain_grad: float32 [1024], P('dp')
- ln1_bias_grad: float32 [1024], P('dp')
- w_qkv_grad: float32 [3, 1024, 1024], P(None, 'dp', 'tensor')
- qv_bias_grad: float32 [2, 1024], P(None, 'dp')
- w_proj_grad: float32 [1024, 1024], P('tensor', 'dp')
- proj_bias_grad: float32 [1024], P('dp')
- ln2_gain_grad: float32 [1024], P('dp')
- ln2_bias_grad: float32 [1024], P('dp')
- w_fc1_grad: float32 [1024, 4096], P('dp', 'tensor')
- fc1_bias_grad: float32 [4096], P('dp')
- w_fc2_grad: float32 [4096, 1024], P('tensor', 'dp')
- fc2_bias_grad: float32 [1024], P('dp')
All inputs are finite; a program needn't handle non-finite values. No bound on the sum of `key_mask` on one device may be relied on, other than what follows from the above.
Results may differ from a plain program's by a relative error of at most 0.015.
Values may be sent and summed in bfloat16 or wider, within the bound.
No kernel may reach another device: no remote copies, remote signals or barrier semaphores. Data moves between devices by JAX's collectives and lax.ppermute only.
A program may use at most 192 MiB of HBM per device.

v0:
```python
import jax
import jax.numpy as jnp
from jax import lax
from jax.experimental import pallas as pl
from jax.experimental.pallas import tpu as pltpu
from jax.sharding import PartitionSpec as P

HEAD_DIM = 64
norm_eps = 1e-06
masked_score = -1e30
AXES = ("dp", "tensor")
LOW = jnp.bfloat16
F32 = jnp.float32
TILE = 128
Y_BIT, CORE_BIT, X_BIT, Z_SHIFT = 1, 2, 4, 3
ANY = pl.BlockSpec(memory_space=pltpu.HBM)


def mm(left, right):
    return lax.dot_general(left, right, (((1,), (0,)), ((), ())), preferred_element_type=F32)


def mm_nt(left, right):
    return lax.dot_general(left, right, (((1,), (1,)), ((), ())), preferred_element_type=F32)


def mm_tn(left, right):
    return lax.dot_general(left, right, (((0,), (0,)), ((), ())), preferred_element_type=F32)


def whole(*shape):
    return pl.BlockSpec(shape, lambda t, me: (0,) * len(shape))


def call(body, grid, ins, outs, shapes, scratch, flops, moved, name, room=32):
    return pl.pallas_call(
        body,
        grid_spec=pltpu.PrefetchScalarGridSpec(
            num_scalar_prefetch=1,
            grid=grid,
            in_specs=ins,
            out_specs=outs,
            scratch_shapes=scratch,
        ),
        out_shape=shapes,
        compiler_params=pltpu.CompilerParams(
            dimension_semantics=("arbitrary",) * len(grid), vmem_limit_bytes=room << 20
        ),
        cost_estimate=pl.CostEstimate(flops=1, bytes_accessed=1, transcendentals=0),
        name=name,
    )


def places(me, core_flip, first, second):
    owner = ((me >> 1) & 1) ^ core_flip
    off_y = jnp.where(owner == 0, first, second)
    off_x = jnp.where(owner == 0, second, first)
    return off_y, off_x


def dp_of(me, core_flip, off_x, off_z):
    core = ((me >> 1) & 1) ^ core_flip
    return (((me >> Z_SHIFT) ^ off_z) << 2) | ((((me >> 2) & 1) ^ off_x) << 1) | core


def fetch(me, pieces, store, sems, start, width):
    for index, piece in enumerate(pieces):
        core_flip, first, second = index >> 2, (index >> 1) & 1, index & 1
        off_y, off_x = places(me, core_flip, first, second)
        y_at = (me & 1) ^ off_y
        depth, rows, _ = piece.shape
        for off_z in range(depth):
            row = pl.multiple_of(dp_of(me, core_flip, off_x, off_z) * rows, rows)
            pltpu.make_async_copy(
                piece.at[off_z, :, pl.ds(start, width)],
                store.at[y_at, pl.ds(row, rows), :],
                sems.at[y_at],
            ).start()


def arrived(store, sems, y_at):
    pltpu.make_async_copy(store.at[y_at], store.at[y_at], sems.at[y_at]).wait()


def normed(rows, gain, shift):
    center = rows - jnp.mean(rows, axis=-1, keepdims=True)
    spread = jnp.mean(center * center, axis=-1, keepdims=True)
    return center * lax.rsqrt(spread + norm_eps) * gain + shift


def qkv_call(me, rows_in, pieces):
    count, width = rows_in.shape
    half = width // 2
    span = 3 * half

    def body(me_ref, x_ref, *refs):
        parts, refs = refs[:8], refs[8:]
        norm_ref, turn_ref, out_ref, table_ref, store, sems, vectors, vector_sems = refs
        step = pl.program_id(0)

        @pl.when(step == 0)
        def _():
            fetch(me_ref[0], parts, vectors, vector_sems, span, TILE)
            fetch(me_ref[0], parts, store, sems, 0, span)
            for y_at in range(2):
                arrived(vectors, vector_sems, y_at)
            table_ref[...] = vectors[0].astype(F32).T[: table_ref.shape[0]]

            @pl.loop(0, count // TILE)
            def _(i):
                at = pl.ds(pl.multiple_of(i * TILE, TILE), TILE)
                value = normed(x_ref[at, :], table_ref[0:1, :], table_ref[1:2, :])
                norm_ref[at, :] = value.astype(LOW)
                turn_ref[:, at] = value.T.astype(LOW)

        for y_at in range(2):

            @pl.when(step == 3 * y_at)
            def _():
                arrived(store, sems, y_at)

        y_at, kind = step // 3, step % 3
        col = pl.multiple_of(kind * half, half)
        own = pl.ds(pl.multiple_of(y_at * half, half), half)
        product = mm(norm_ref[...], store[y_at, :, pl.ds(col, half)])
        bias = jnp.where(kind == 0, table_ref[2:3, own], table_ref[3:4, own])
        bias = jnp.where(kind == 1, 0.0, bias)
        out_ref[...] = (product + bias).astype(LOW)

    return call(
        body,
        (6,),
        [whole(count, width)] + [ANY] * 8,
        [
            whole(count, width),
            whole(width, count),
            pl.BlockSpec((count, half), lambda t, me: (0, t)),
            whole(16, width),
        ],
        [
            jax.ShapeDtypeStruct((count, width), LOW),
            jax.ShapeDtypeStruct((width, count), LOW),
            jax.ShapeDtypeStruct((count, 2 * span), LOW),
            jax.ShapeDtypeStruct((16, width), F32),
        ],
        [
            pltpu.VMEM((2, width, span), LOW),
            pltpu.SemaphoreType.DMA((2,)),
            pltpu.VMEM((2, width, TILE), LOW),
            pltpu.SemaphoreType.DMA((2,)),
        ],
        2 * count * width * 2 * span,
        count * width * 16 + width * span * 4,
        "qkv",
        60,
    )(me, rows_in, *pieces)


def head_halves(shape):
    lane = lax.broadcasted_iota(jnp.int32, shape, 1)
    return lane < HEAD_DIM, lane >= HEAD_DIM


def attend_call(me, qkv, visible):
    images, _, seq = visible.shape
    count, full = qkv.shape
    half = full // 6

    def body(me_ref, qkv_ref, seen_ref, out_ref):
        seen = seen_ref[0] > 0

        @pl.loop(0, half // (2 * TILE))
        def _(pair):
            for part in range(2):
                col = pl.multiple_of((2 * pair + part) * TILE, TILE)
                query = qkv_ref[:, pl.ds(col, TILE)] * jnp.asarray(HEAD_DIM**-0.5, LOW)
                key = qkv_ref[:, pl.ds(half + col, TILE)]
                value = qkv_ref[:, pl.ds(2 * half + col, TILE)]
                lanes = head_halves(query.shape)
                mixed = []
                for keep in lanes:
                    scores = jnp.where(seen, mm_nt(jnp.where(keep, query, 0), key), masked_score)
                    exps = jnp.exp(scores - jnp.max(scores, axis=-1, keepdims=True))
                    total = jnp.sum(exps, axis=-1, keepdims=True)
                    mixed.append(mm(exps.astype(LOW), value) * (1.0 / total))
                out_ref[:, pl.ds(col, TILE)] = jnp.where(lanes[0], mixed[0], mixed[1]).astype(LOW)

    return call(
        body,
        (images, 2),
        [
            pl.BlockSpec((seq, 3 * half), lambda i, y, me: (i, y)),
            pl.BlockSpec((1, 1, seq), lambda i, y, me: (i, 0, 0)),
        ],
        pl.BlockSpec((seq, half), lambda i, y, me: (i, y)),
        jax.ShapeDtypeStruct((count, 2 * half), LOW),
        [],
        4 * count * seq * 2 * half * 4,
        count * full * 3,
        "attend",
    )(me, qkv, visible)


def project_call(me, mixed, rows_in, table, pieces):
    count, width = rows_in.shape
    half = width // 2

    def body(me_ref, mixed_ref, x_ref, table_ref, *refs):
        parts, (mid_ref, norm_ref, turn_ref, store, sems) = refs[:8], refs[8:]
        fetch(me_ref[0], parts, store, sems, 2 * width, half)
        arrived(store, sems, 0)
        mid_ref[...] = mm_nt(mixed_ref[:, :half], store[0])
        arrived(store, sems, 1)
        mid_ref[...] += mm_nt(mixed_ref[:, half:], store[1])

        @pl.loop(0, count // TILE)
        def _(i):
            at = pl.ds(pl.multiple_of(i * TILE, TILE), TILE)
            middle = x_ref[at, :] + (mid_ref[at, :] + table_ref[4:5, :])
            mid_ref[at, :] = middle
            value = normed(middle, table_ref[5:6, :], table_ref[6:7, :])
            norm_ref[at, :] = value.astype(LOW)
            turn_ref[:, at] = value.T.astype(LOW)

    return call(
        body,
        (1,),
        [whole(count, width), whole(count, width), whole(*table.shape)] + [ANY] * 8,
        [whole(count, width), whole(count, width), whole(width, count)],
        [
            jax.ShapeDtypeStruct((count, width), F32),
            jax.ShapeDtypeStruct((count, width), LOW),
            jax.ShapeDtypeStruct((width, count), LOW),
        ],
        [pltpu.VMEM((2, width, half), LOW), pltpu.SemaphoreType.DMA((2,))],
        2 * count * width * width,
        count * width * 14 + width * width * 2,
        "project",
    )(me, mixed, rows_in, table, *pieces)


def expand_call(me, normed_two, bias, pieces):
    count, width = normed_two.shape
    span = bias.shape[1] // 2
    chunk = span // 4

    def body(me_ref, norm_ref, bias_ref, *refs):
        parts, (hid_ref, slope_ref, store, sems) = refs[:8], refs[8:]
        step = pl.program_id(0)

        @pl.when(step == 0)
        def _():
            fetch(me_ref[0], parts, store, sems, 0, span)

        for y_at in range(2):

            @pl.when(step == 4 * y_at)
            def _():
                arrived(store, sems, y_at)

        y_at, col = step // 4, pl.multiple_of(step % 4 * chunk, chunk)
        pre = mm(norm_ref[...], store[y_at, :, pl.ds(col, chunk)]) + bias_ref[...]
        below = 0.5 + 0.5 * lax.erf(pre * 0.5**0.5)
        hid_ref[...] = (pre * below).astype(LOW)
        slope_ref[...] = (below + pre * jnp.exp(pre * pre * -0.5) * 0.3989422804014327).astype(LOW)

    out = pl.BlockSpec((count, chunk), lambda t, me: (0, t))
    return call(
        body,
        (8,),
        [whole(count, width), pl.BlockSpec((1, chunk), lambda t, me: (0, t))] + [ANY] * 8,
        [out, out],
        [jax.ShapeDtypeStruct((count, 2 * span), LOW)] * 2,
        [pltpu.VMEM((2, width, span), LOW), pltpu.SemaphoreType.DMA((2,))],
        2 * count * width * 2 * span,
        count * span * 8 + width * span * 4,
        "expand",
    )(me, normed_two, bias, *pieces)


def contract_call(me, hidden, slope, out_low, middle, table, pieces):
    count, width = middle.shape
    span = hidden.shape[1] // 2
    chunk = span // 4

    def body(me_ref, hid_ref, slope_ref, low_ref, mid_ref, table_ref, *refs):
        parts, (act_ref, pre_ref, sum_ref, store, sems) = refs[:8], refs[8:]
        step = pl.program_id(0)

        @pl.when(step == 0)
        def _():
            fetch(me_ref[0], parts, store, sems, 0, span)
            act_ref[...] = mid_ref[...] + table_ref[7:8, :]

        for y_at in range(2):

            @pl.when(step == 4 * y_at)
            def _():
                arrived(store, sems, y_at)

        y_at, col = step // 4, pl.multiple_of(step % 4 * chunk, chunk)
        weight = store[y_at, :, pl.ds(col, chunk)]
        act_ref[...] += mm_nt(hid_ref[...], weight)
        pre = mm(low_ref[...], weight) * slope_ref[...].astype(F32)
        pre_ref[...] = pre.astype(LOW)
        sum_ref[...] = jnp.sum(pre, axis=0, keepdims=True)

    part = pl.BlockSpec((count, chunk), lambda t, me: (0, t))
    return call(
        body,
        (8,),
        [part, part, whole(count, width), whole(count, width), whole(*table.shape)] + [ANY] * 8,
        [whole(count, width), part, pl.BlockSpec((1, chunk), lambda t, me: (0, t))],
        [
            jax.ShapeDtypeStruct((count, width), F32),
            jax.ShapeDtypeStruct((count, 2 * span), LOW),
            jax.ShapeDtypeStruct((1, 2 * span), F32),
        ],
        [pltpu.VMEM((2, width, span), LOW), pltpu.SemaphoreType.DMA((2,))],
        4 * count * width * 2 * span,
        count * span * 12 + width * span * 4,
        "contract",
    )(me, hidden, slope, out_low, middle, table, *pieces)


def norm_back_call(me, low, start, gain_row, rows_in, base, table, pieces, keep_low, name):
    count, width = rows_in.shape
    span = low.shape[1] // 2
    chunk = span // 2

    def body(me_ref, low_ref, x_ref, base_ref, table_ref, *refs):
        parts, outs = refs[:8], refs[8:]
        if keep_low:
            grad_ref, vec_ref, out_low_ref, turn_ref, store, sems = outs
        else:
            grad_ref, vec_ref, store, sems = outs
        step = pl.program_id(0)

        @pl.when(step == 0)
        def _():
            fetch(me_ref[0], parts, store, sems, start, span)

        for y_at in range(2):

            @pl.when(step == 2 * y_at)
            def _():
                arrived(store, sems, y_at)

        y_at, col = step // 2, pl.multiple_of(step % 2 * chunk, chunk)
        product = mm_nt(low_ref[...], store[y_at, :, pl.ds(col, chunk)])

        @pl.when(step == 0)
        def _():
            grad_ref[...] = product

        @pl.when(step > 0)
        def _():
            grad_ref[...] += product

        @pl.when(step == 3)
        def _():
            vec_ref[...] = jnp.zeros_like(vec_ref)

            @pl.loop(0, count // TILE)
            def _(i):
                at = pl.ds(pl.multiple_of(i * TILE, TILE), TILE)
                back = grad_ref[at, :]
                rows = x_ref[at, :]
                center = rows - jnp.mean(rows, axis=-1, keepdims=True)
                spread = jnp.mean(center * center, axis=-1, keepdims=True)
                scale = lax.rsqrt(spread + norm_eps)
                unit = center * scale
                inner = back * table_ref[gain_row : gain_row + 1, :]
                along = jnp.mean(inner * unit, axis=-1, keepdims=True)
                level = jnp.mean(inner, axis=-1, keepdims=True)
                grad = base_ref[at, :] + scale * (inner - level - unit * along)
                grad_ref[at, :] = grad
                vec_ref[0:1, :] += jnp.sum(back * unit, axis=0, keepdims=True)
                vec_ref[1:2, :] += jnp.sum(back, axis=0, keepdims=True)
                vec_ref[2:3, :] += jnp.sum(grad, axis=0, keepdims=True)
                if keep_low:
                    out_low_ref[at, :] = grad.astype(LOW)
                    turn_ref[:, at] = grad.T.astype(LOW)

    outs = [whole(count, width), whole(8, width)]
    shapes = [jax.ShapeDtypeStruct((count, width), F32), jax.ShapeDtypeStruct((8, width), F32)]
    if keep_low:
        outs += [whole(count, width), whole(width, count)]
        shapes += [
            jax.ShapeDtypeStruct((count, width), LOW),
            jax.ShapeDtypeStruct((width, count), LOW),
        ]
    return call(
        body,
        (4,),
        [
            pl.BlockSpec((count, chunk), lambda t, me: (0, t)),
            whole(count, width),
            whole(count, width),
            whole(*table.shape),
        ]
        + [ANY] * 8,
        outs,
        shapes,
        [pltpu.VMEM((2, width, span), LOW), pltpu.SemaphoreType.DMA((2,))],
        2 * count * width * 2 * span,
        count * width * 16 + width * span * 4 + count * span * 4,
        name,
        32 if keep_low else 60,
    )(me, low, rows_in, base, table, *pieces)


def mixed_back_call(me, middle_low, pieces):
    count, width = middle_low.shape
    half = width // 2

    def body(me_ref, low_ref, *refs):
        parts, (out_ref, store, sems) = refs[:8], refs[8:]
        step = pl.program_id(0)

        @pl.when(step == 0)
        def _():
            fetch(me_ref[0], parts, store, sems, 2 * width, half)

        for y_at in range(2):

            @pl.when(step == y_at)
            def _():
                arrived(store, sems, y_at)

        out_ref[...] = mm(low_ref[...], store[step]).astype(LOW)

    return call(
        body,
        (2,),
        [whole(count, width)] + [ANY] * 8,
        pl.BlockSpec((count, half), lambda t, me: (0, t)),
        jax.ShapeDtypeStruct((count, width), LOW),
        [pltpu.VMEM((2, width, half), LOW), pltpu.SemaphoreType.DMA((2,))],
        2 * count * width * width,
        count * width * 4 + width * width * 2,
        "mixed_back",
    )(me, middle_low, *pieces)


def attend_back_call(me, qkv, grads, visible):
    images, seq, _ = visible.shape
    count, full = qkv.shape
    half = full // 6
    scale = HEAD_DIM**-0.5

    def body(me_ref, qkv_ref, grad_ref, seen_ref, out_ref, sum_ref):
        seen = seen_ref[0] > 0
        @pl.loop(0, half // (2 * TILE))
        def _(pair):
            for part in range(2):
                col = pl.multiple_of((2 * pair + part) * TILE, TILE)
                query = qkv_ref[:, pl.ds(col, TILE)] * jnp.asarray(scale, LOW)
                key = qkv_ref[:, pl.ds(half + col, TILE)]
                value = qkv_ref[:, pl.ds(2 * half + col, TILE)]
                grad = grad_ref[:, pl.ds(col, TILE)]
                lanes = head_halves(query.shape)
                parts = []
                for keep in lanes:
                    scores = jnp.where(seen, mm_nt(jnp.where(keep, key, 0), query), masked_score)
                    exps = jnp.exp(scores - jnp.max(scores, axis=0, keepdims=True))
                    probs = exps * (1.0 / jnp.sum(exps, axis=0, keepdims=True))
                    prob_grad = mm_nt(jnp.where(keep, value, 0), grad)
                    row_dot = jnp.sum(probs * prob_grad, axis=0, keepdims=True)
                    score_grad = (probs * (prob_grad - row_dot)).astype(LOW)
                    parts.append(
                        (
                            mm_tn(key, score_grad).T * scale,
                            mm(score_grad, query),
                            mm(probs.astype(LOW), grad),
                        )
                    )
                for at in range(3):
                    merged = jnp.where(lanes[0], parts[0][at], parts[1][at])
                    put = at * half + col
                    out_ref[:, pl.ds(put, TILE)] = merged.astype(LOW)
                    sum_ref[0, 0, :, pl.ds(put, TILE)] = jnp.sum(merged, axis=0, keepdims=True)

    return call(
        body,
        (images, 2),
        [
            pl.BlockSpec((seq, 3 * half), lambda i, y, me: (i, y)),
            pl.BlockSpec((seq, half), lambda i, y, me: (i, y)),
            pl.BlockSpec((1, seq, 1), lambda i, y, me: (i, 0, 0)),
        ],
        [
            pl.BlockSpec((seq, 3 * half), lambda i, y, me: (i, y)),
            pl.BlockSpec((1, 1, 1, 3 * half), lambda i, y, me: (i, y, 0, 0)),
        ],
        [
            jax.ShapeDtypeStruct((count, full), LOW),
            jax.ShapeDtypeStruct((images, 2, 1, 3 * half), F32),
        ],
        [],
        10 * count * seq * 2 * half * 4,
        count * full * 5,
        "attend_back",
    )(me, qkv, grads, visible)


def weight_grad_call(me, turned, right, depth, core_flip, received, name):
    width, count = turned.shape
    span = right.shape[1] // 2
    chunk = next(c for c in (1024, 768, 512, 384, 256, 128) if span % c == 0)
    parts = span // chunk
    steps = 2 * parts
    rows = width // (4 * depth)
    quarter = width // 4

    def body(me_ref, turn_ref, right_ref, *refs):
        if core_flip:
            (far_ref, lefts, ready, sems) = refs
        else:
            (got_ref, kept_ref, sent_ref, lefts, ready, sems, got, got_sems) = refs
        step = pl.program_id(0)
        slot = step % 2
        owner = ((me_ref[0] >> 1) & 1) ^ core_flip

        def spot(off_y, off_x):
            return jnp.where(owner == 0, off_y, off_x), jnp.where(owner == 0, off_x, off_y)

        def fetched(at, off_x):
            first, second = spot(1 - at // parts, off_x)
            col = pl.multiple_of(at % parts * chunk, chunk)
            return pltpu.make_async_copy(
                got_ref.at[first, second, :, :, pl.ds(col, chunk)],
                got.at[at, off_x],
                got_sems.at[at, off_x],
            )

        def leaving(target, at, off_x):
            col = pl.multiple_of(at % parts * chunk, chunk)
            return pltpu.make_async_copy(
                ready.at[at % 2, off_x],
                target.at[:, :, pl.ds(col, chunk)],
                sems.at[at % 2, off_x],
            )

        @pl.when(step == 0)
        def _():
            if not core_flip:
                for at in range(steps):
                    for off_x in range(2):
                        fetched(at, off_x).start()
            for off_x in range(2):
                for off_z in range(depth):
                    row = pl.multiple_of(dp_of(me_ref[0], core_flip, off_x, off_z) * rows, rows)
                    put = off_x * quarter + off_z * rows
                    lefts[put : put + rows, :] = turn_ref[pl.ds(row, rows), :]

        product = mm(lefts[...], right_ref[...]).reshape(2, depth, rows, chunk)

        @pl.when(step >= 2)
        def _():
            for off_x in range(2):
                some = far_ref.at[0, 0] if core_flip else kept_ref.at[0]
                leaving(some, step, off_x).wait()

        for off_x in range(2):
            total = product[off_x]
            if not core_flip:
                fetched(step, off_x).wait()
                total = total + got[step, off_x].astype(F32)
            ready[slot, off_x] = total.astype(LOW)
            first, second = spot(1 - step // parts, off_x)
            if core_flip:
                leaving(far_ref.at[first, second], step, off_x).start()
            else:
                for at, target in enumerate((kept_ref, sent_ref)):

                    @pl.when(first == at)
                    def _():
                        leaving(target.at[second], step, off_x).start()

        @pl.when(step == steps - 1)
        def _():
            for back in range(min(2, steps)):
                for off_x in range(2):
                    some = far_ref.at[0, 0] if core_flip else kept_ref.at[0]
                    leaving(some, step - back, off_x).wait()

    def right_at(t, me):
        return 0, ((me[0] & 1) ^ (1 - t // parts)) * parts + t % parts

    ins = [whole(width, count), pl.BlockSpec((count, chunk), right_at)]
    scratch = [
        pltpu.VMEM((2 * quarter, count), LOW),
        pltpu.VMEM((2, 2, depth, rows, chunk), LOW),
        pltpu.SemaphoreType.DMA((2, 2)),
    ]
    if core_flip:
        outs = ANY
        shapes = jax.ShapeDtypeStruct((2, 2, depth, rows, span), LOW)
        extra = ()
    else:
        ins = ins + [ANY]
        outs = [ANY, ANY]
        shapes = [jax.ShapeDtypeStruct((2, depth, rows, span), LOW)] * 2
        extra = (received,)
        scratch += [
            pltpu.VMEM((steps, 2, depth, rows, chunk), LOW),
            pltpu.SemaphoreType.DMA((steps, 2)),
        ]
    return call(
        body,
        (steps,),
        ins,
        outs,
        shapes,
        scratch,
        2 * count * width * span,
        count * (width + span * 2) * 2 + width * span * 4,
        name,
    )(me, turned, right, *extra)


def swap(value, size, bits, other=None):
    other = bits if other is None else other
    return lax.ppermute(
        value, AXES, [(i, i ^ (other if i & CORE_BIT else bits)) for i in range(size)]
    )


def after(value, *others):
    return lax.optimization_barrier((value, *others))[0]


def along_depth(piece, size, steps):
    return [piece] + [swap(piece, size, k << Z_SHIFT) for k in steps]


def along_first(value, size):
    return swap(value, size, Y_BIT, X_BIT)


def along_second(value, size):
    return swap(value, size, X_BIT, Y_BIT)


def along_core(value, size):
    return swap(value, size, CORE_BIT)


class Scatter:
    def __init__(self, turned, right, size, depth, name):
        self.size, self.depth, self.name = size, depth, name
        self.turned, self.right = turned, right

    def far(self, me):
        self.me = me
        self.sent = weight_grad_call(
            me, self.turned, self.right, self.depth, 1, None, self.name + "_far"
        )
        self.received = swap(self.sent, self.size, CORE_BIT)
        return self.sent

    def near(self, *others):
        right = after(self.right, *others)
        self.kept, self.sent = weight_grad_call(
            self.me, self.turned, right, self.depth, 0, self.received, self.name + "_near"
        )
        self.received = swap(self.sent, self.size, Y_BIT, X_BIT)
        return self.kept

    def second(self, *others):
        kept = after(self.kept, *others)
        total = (kept.astype(F32) + self.received.astype(F32)).astype(LOW)
        self.kept = total[0]
        self.received = swap(total[1], self.size, X_BIT, Y_BIT)
        return self.kept

    def third(self, *others):
        kept = after(self.kept, *others)
        total = (kept.astype(F32) + self.received.astype(F32)).astype(LOW)
        self.kept = total[0]
        self.received = [
            swap(total[k], self.size, k << Z_SHIFT) for k in range(1, self.depth)
        ]
        return self.kept

    def last(self, *others):
        result = after(self.kept, *others).astype(F32)
        for value in self.received:
            result = result + value.astype(F32)
        return result


def shards(
    inputs,
    key_mask,
    ln1_gain,
    ln1_bias,
    w_qkv,
    qv_bias,
    w_proj,
    proj_bias,
    ln2_gain,
    ln2_bias,
    w_fc1,
    fc1_bias,
    w_fc2,
    fc2_bias,
    out_grad,
):
    tensor_rank = lax.axis_index("tensor")
    dp_rank = lax.axis_index("dp")
    dp_size = lax.axis_size("dp")
    size = 2 * dp_size
    depth = dp_size // 4
    own_images, seq, width = inputs.shape
    count = own_images * seq
    half = w_qkv.shape[2]
    rows = ln1_gain.shape[0]
    me = jnp.reshape(dp_rank * 2 + tensor_rank, (1,)).astype(jnp.int32)

    vectors = jnp.concatenate(
        [
            jnp.stack([ln1_gain, ln1_bias, qv_bias[0], qv_bias[1]]),
            jnp.stack([proj_bias, ln2_gain, ln2_bias, fc2_bias]),
            fc1_bias.reshape(4, rows),
        ]
    )
    vectors = jnp.pad(vectors, ((0, TILE - vectors.shape[0]), (0, 0))).T
    piece_one = jnp.concatenate([w_qkv[0], w_qkv[1], w_qkv[2], vectors], axis=1).astype(LOW)
    piece_two = jnp.concatenate([w_fc1, w_proj.T], axis=1).astype(LOW)
    piece_three = w_fc2.T.astype(LOW)

    held_one = jnp.stack(along_depth(piece_one, size, range(1, depth)))
    grad_in = out_grad.reshape(count, width)
    out_low = grad_in.astype(LOW)
    out_turned = out_low.T
    held_one, piece_two, out_low, out_turned = lax.optimization_barrier(
        (held_one, piece_two, out_low, out_turned)
    )
    first_one = along_first(held_one, size)
    second_one = along_second(held_one, size)
    far_one = [along_core(held_one, size)]
    deep_two = along_depth(piece_two, size, range(1, depth - 1))
    first_one, second_one, far_own, *deep_two = lax.optimization_barrier(
        (first_one, second_one, *far_one, *deep_two)
    )
    both_one = along_second(first_one, size)
    far_one = [far_own, along_core(second_one, size), along_core(first_one, size)]
    plane_one = [held_one, second_one, first_one]
    deep_two += along_depth(deep_two[0], size, [depth - 1])[1:]
    far_one += [along_core(both_one, size)]
    both_one, piece_three, *deep_two = lax.optimization_barrier((both_one, piece_three, *deep_two))
    pieces_one = plane_one + [both_one] + far_one
    held_two = jnp.stack(deep_two)
    first_two = along_first(held_two, size)
    second_two = along_second(held_two, size)
    far_two = [along_core(held_two, size)]
    deep_three = along_depth(piece_three, size, range(1, depth - 1))

    rows_in = inputs.reshape(count, width)
    own_mask = lax.dynamic_slice_in_dim(key_mask, tensor_rank * own_images, own_images, 0)
    visible = jnp.concatenate(
        [jnp.ones((own_images, seq - key_mask.shape[1]), jnp.int32), own_mask], axis=1
    )
    visible_rows = after(visible, held_one)[:, :, None]
    visible = visible[:, None, :]

    normed_one, turned_one, qkv, table = qkv_call(me, rows_in, pieces_one)
    fc1_full = table[8:12].reshape(4, dp_size, rows).transpose(1, 0, 2).reshape(1, 4 * width)
    mixed = attend_call(me, qkv, visible)
    mixed, fc1_full, first_two, second_two, *deep_three, far_own = lax.optimization_barrier(
        (mixed, fc1_full, first_two, second_two, *deep_three, *far_two)
    )
    both_two = along_second(first_two, size)
    far_two = [far_own, along_core(second_two, size), along_core(first_two, size)]
    plane_two = [held_two, second_two, first_two]
    deep_three += along_depth(deep_three[0], size, [depth - 1])[1:]
    far_two += [along_core(both_two, size)]
    both_two, *deep_three = lax.optimization_barrier((both_two, *deep_three))
    pieces_two = plane_two + [both_two] + far_two
    held_three = jnp.stack(deep_three)
    first_three = along_first(held_three, size)
    second_three = along_second(held_three, size)
    far_three = [along_core(held_three, size)]
    middle, normed_two, turned_two = project_call(me, mixed, rows_in, table, pieces_two)
    normed_two, first_three, second_three, far_own = lax.optimization_barrier(
        (normed_two, first_three, second_three, *far_three)
    )
    both_three = along_second(first_three, size)
    far_three = [far_own, along_core(second_three, size), along_core(first_three, size)]
    plane_three = [held_three, second_three, first_three]
    hidden, slope = expand_call(me, normed_two, fc1_full, pieces_two)
    hidden, both_three = lax.optimization_barrier((hidden, both_three))
    pieces_three = plane_three + [both_three] + far_three + [along_core(both_three, size)]
    fc2 = Scatter(out_turned, hidden, size, depth, "fc2_grad")
    done = fc2.far(me)
    outputs, pre_low, fc1_sum = contract_call(
        me, after(hidden, done), slope, out_low, middle, table, pieces_three
    )
    done = fc2.near(pre_low)
    middle_grad, vec_two, middle_low, turned_mid = norm_back_call(
        me, after(pre_low, done), 0, 5, middle, grad_in, table, pieces_two, True, "norm_two_back"
    )
    fc1 = Scatter(turned_two, after(pre_low, middle_low), size, depth, "fc1_grad")
    done = fc1.far(me)
    done = fc2.second(done)
    mixed_grad = mixed_back_call(me, after(middle_low, done), pieces_two)
    proj = Scatter(turned_mid, after(mixed, mixed_grad), size, depth, "proj_grad")
    done = proj.far(me)
    done = fc2.third(done)
    done = fc1.near(done)
    qkv_low, qkv_sum = attend_back_call(me, qkv, after(mixed_grad, done), visible_rows)
    fc2_grad = fc2.last(qkv_low)
    done = fc1.second(fc2_grad)
    done = proj.near(done)
    qkv_out = Scatter(turned_one, after(qkv_low, done), size, depth, "qkv_grad")
    done = qkv_out.far(me)
    done = qkv_out.near(done)
    done = fc1.third(proj.second(done))
    input_grad, vec_one = norm_back_call(
        me,
        after(qkv_low, done),
        0,
        0,
        rows_in,
        middle_grad,
        table,
        pieces_one,
        False,
        "norm_one_back",
    )

    qkv_sum = jnp.sum(qkv_sum, axis=(0, 2)).reshape(2, 3, half)
    sums = jnp.concatenate(
        [
            vec_one[:2],
            qkv_sum[:, 0].reshape(1, width),
            qkv_sum[:, 2].reshape(1, width),
            vec_two[2:3],
            vec_two[:2],
            jnp.sum(grad_in, axis=0, keepdims=True),
            fc1_sum.reshape(4, width),
        ]
    )
    fc1_grad = fc1.last(input_grad)
    done = qkv_out.second(fc1_grad)
    done = proj.third(done)
    sums = after(sums, done)
    for bits in (CORE_BIT, X_BIT, Y_BIT):
        sums = sums + swap(sums, size, bits)
    done = qkv_out.third(sums)
    proj_grad = proj.last(done)
    sums = sum(along_depth(after(sums, qkv_out.received[0]), size, range(1, depth)))
    qkv_grad = qkv_out.last()
    mine = lax.dynamic_slice_in_dim(sums[:8], dp_rank * rows, rows, 1)
    fc1_mine = lax.dynamic_slice_in_dim(sums[8:].reshape(-1), dp_rank * 4 * rows, 4 * rows, 0)
    return (
        outputs.reshape(inputs.shape),
        input_grad.reshape(inputs.shape),
        mine[0],
        mine[1],
        qkv_grad.reshape(rows, 3, half).transpose(1, 0, 2),
        mine[2:4],
        proj_grad.T,
        mine[4],
        mine[5],
        mine[6],
        fc1_grad,
        fc1_mine,
        fc2_grad.T,
        mine[7],
    )


def solution(mesh):
    placed = (
        P(("dp", "tensor"), None, None),
        P("dp", None),
        P("dp"),
        P("dp"),
        P(None, "dp", "tensor"),
        P(None, "dp"),
        P("tensor", "dp"),
        P("dp"),
        P("dp"),
        P("dp"),
        P("dp", "tensor"),
        P("dp"),
        P("tensor", "dp"),
        P("dp"),
        P(("dp", "tensor"), None, None),
    )
    return jax.shard_map(
        shards,
        mesh=mesh,
        in_specs=placed,
        out_specs=(
            P(("dp", "tensor"), None, None),
            P(("dp", "tensor"), None, None),
            P("dp"),
            P("dp"),
            P(None, "dp", "tensor"),
            P(None, "dp"),
            P("tensor", "dp"),
            P("dp"),
            P("dp"),
            P("dp"),
            P("dp", "tensor"),
            P("dp"),
            P("tensor", "dp"),
            P("dp"),
        ),
        check_vma=False,
    )
```

profile of v0, /device:TPU:0, one launch (start us, length us, event | category | flops | bytes accessed | tf_op | source)
XLA Modules:
  0.0 410.1 jit_solution(15840941431121150143)
XLA Ops:
  3.5 3.1 collective-permute-start
  6.6 2.6 collective-permute-start.1
  10.3 3.2 fusion.2
  13.5 2.2 collective-permute-done
  15.7 9.1 %collective-permute-done.1 = bf16[64,1664]{1,0:T(8,128)(2,1)S(1)} collective-permute-done((bf16[64,1664]{1,0:T(8,128)(2,1)S(1)}, bf16[64,1664]{1,0:T(8,128)(2,1)S(1)}, u32[]{:S(2)}, u32[]{:S(2)}) %collective-permute-start.1) | collective-permute-done | bytes 213024 | tf_op jit(solution)/shard_map/ppermute | solution.py:625
  27.9 3.8 collective-permute-start.6
  32.7 14.3 %collective-permute-done.6 = bf16[64,2560]{1,0:T(8,128)(2,1)S(1)} collective-permute-done((bf16[64,2560]{1,0:T(8,128)(2,1)S(1)}, bf16[64,2560]{1,0:T(8,128)(2,1)S(1)}, u32[]{:S(2)}, u32[]{:S(2)}) %collective-permute-start.6) | collective-permute-done | bytes 327712 | tf_op jit(solution)/shard_map/ppermute | solution.py:625
  47.0 2.5 collective-permute-done.7
  51.0 2.5 collective-permute-start.9
  54.2 8.8 %collective-permute-done.9 = bf16[64,2560]{1,0:T(8,128)(2,1)S(1)} collective-permute-done((bf16[64,2560]{1,0:T(8,128)(2,1)S(1)}, bf16[64,2560]{1,0:T(8,128)(2,1)S(1)}, u32[]{:S(2)}, u32[]{:S(2)}) %collective-permute-start.9) | collective-permute-done | bytes 327712 | tf_op jit(solution)/shard_map/ppermute | solution.py:625
  65.9 3.7 collective-permute-done.10.refs_5_
  69.6 6.1 %collective-permute-start.15 = (bf16[64,2048]{1,0:T(8,128)(2,1)}, bf16[64,2048]{1,0:T(8,128)(2,1)}, u32[]{:S(2)}, u32[]{:S(2)}) collective-permute-start(bf16[64,2048]{1,0:T(8,128)(2,1)} %convert_bitcast_fusion), channel_id=1, source_target_pairs={{0,8},{1,9},{2,10},{3,11},{4,12},{5,13},{6,14},{7,15},{8,0},{9,1},... | collective-permute-start | bytes 786440 | tf_op jit(solution)/shard_map/ppermute | solution.py:625
  75.7 2.2 collective-permute-start.16
  78.0 13.1 %qkv.1 = (bf16[640,1024]{1,0:T(8,128)(2,1)}, bf16[1024,640]{1,0:T(8,128)(2,1)}, bf16[640,3072]{1,0:T(8,128)(2,1)}, f32[16,1024]{1,0:T(8,128)}) custom-call(s32[1]{0:T(128)} %bitcast.me_ref, f32[640,1024]{1,0:T(8,128)} %bitcast.121, bf16[4,64,1664]{2,1,0:T(8,128)(2,1)} %copy-done.52, bf16[4,64,1664]{2,1,0:T(8,128)(2,1)} %copy-done.54, ...), custom_call_target="tpu_custom_call" | custom-call | flops 1 | bytes 1 | tf_op jit(solution)/shard_map/qkv/pallas_call | solution.py:130
  93.2 11.7 %attend.1.mixed_ref.right_ref = bf16[640,1024]{1,0:T(8,128)(2,1)S(1)} custom-call(s32[1]{0:T(128)} %bitcast.me_ref, bf16[640,3072]{1,0:T(8,128)(2,1)S(1)} %copy-done.23, s32[2,1,320]{2,1,0:T(1,128)S(1)} %broadcast_in_dim.10.seen_ref), custom_call_target="tpu_custom_call" | custom-call | flops 1 | bytes 1 | tf_op jit(solution)/shard_map/attend/pallas_call | solution.py:188
  108.4 15.5 %collective-permute-done.18.refs_3_ = bf16[4,64,2560]{2,1,0:T(8,128)(2,1)S(1)} collective-permute-done((bf16[4,64,2560]{2,1,0:T(8,128)(2,1)S(1)}, bf16[4,64,2560]{2,1,0:T(8,128)(2,1)S(1)}, u32[]{:S(2)}, u32[]{:S(2)}) %collective-permute-start.18) | collective-permute-done | bytes 1310752 | tf_op jit(solution)/shard_map/ppermute | solution.py:625
  127.0 2.5 copy-done.4
  129.5 5.1 %project.1 = (f32[640,1024]{1,0:T(8,128)S(1)}, bf16[640,1024]{1,0:T(8,128)(2,1)S(1)}, bf16[1024,640]{1,0:T(8,128)(2,1)S(1)}) custom-call(s32[1]{0:T(128)} %bitcast.me_ref, bf16[640,1024]{1,0:T(8,128)(2,1)S(1)} %copy-done.20, f32[640,1024]{1,0:T(8,128)S(1)} %bitcast.123, f32[16,1024]{1,0:T(8,128)S(1)} %copy-done.46, ...), custom_call_target="tpu_custom_call" | custom-call | flops 1 | bytes 1 | tf_op jit(solution)/shard_map/project/pallas_call | solution.py:225
  138.2 13.0 %collective-permute-done.23.refs_2_ = bf16[4,64,2048]{2,1,0:T(8,128)(2,1)} collective-permute-done((bf16[4,64,2048]{2,1,0:T(8,128)(2,1)S(1)}, bf16[4,64,2048]{2,1,0:T(8,128)(2,1)}, u32[]{:S(2)}, u32[]{:S(2)}) %collective-permute-start.23) | collective-permute-done | bytes 1048608 | tf_op jit(solution)/shard_map/ppermute | solution.py:625
  154.1 2.5 copy.56.turn_ref
  163.2 13.0 %expand.1 = (bf16[640,4096]{1,0:T(8,128)(2,1)S(1)}, bf16[640,4096]{1,0:T(8,128)(2,1)S(1)}) custom-call(s32[1]{0:T(128)} %bitcast.me_ref, bf16[640,1024]{1,0:T(8,128)(2,1)S(1)} %copy-done.45, f32[1,4096]{1,0:T(1,128)S(1)} %reshape.119.bias_ref, bf16[4,64,2560]{2,1,0:T(8,128)(2,1)S(1)} %pad_maximum_fusion.refs_0_, ...), custom_call_target="tpu_custom_call" | custom-call | flops 1 | bytes 1 | tf_op jit(solution)/shard_map/expand/pallas_call | solution.py:268
  176.2 2.3 copy-done.32
  178.6 5.9 %fc2_grad_far.1 = bf16[2,2,4,64,2048]{4,3,2,1,0:T(8,128)(2,1)} custom-call(s32[1]{0:T(128)} %bitcast.me_ref, bf16[1024,640]{1,0:T(8,128)(2,1)S(1)} %copy-done.26, bf16[640,4096]{1,0:T(8,128)(2,1)S(1)} %get-tuple-element.146.right_ref.hid_ref), custom_call_target="tpu_custom_call" | custom-call | flops 1 | bytes 1 | tf_op jit(solution)/shard_map/fc2_grad_far/pallas_call | solution.py:610
  185.6 9.3 %collective-permute-done.27.refs_5_ = bf16[4,64,2048]{2,1,0:T(8,128)(2,1)S(1)} collective-permute-done((bf16[4,64,2048]{2,1,0:T(8,128)(2,1)S(1)}, bf16[4,64,2048]{2,1,0:T(8,128)(2,1)S(1)}, u32[]{:S(2)}, u32[]{:S(2)}) %collective-permute-start.27) | collective-permute-done | bytes 1048608 | tf_op jit(solution)/shard_map/ppermute | solution.py:625
  196.5 16.5 %contract.1 = (f32[640,1024]{1,0:T(8,128)}, bf16[640,4096]{1,0:T(8,128)(2,1)S(1)}, f32[1,4096]{1,0:T(1,128)S(1)}) custom-call(s32[1]{0:T(128)} %bitcast.me_ref, bf16[640,4096]{1,0:T(8,128)(2,1)S(1)} %get-tuple-element.146.right_ref.hid_ref, bf16[640,4096]{1,0:T(8,128)(2,1)} %copy-done.32, bf16[640,1024]{1,0:T(8,128)(2,1)S(1)} %copy-done.25, ...), custom_call_target="tpu_custom_call" | custom-call | flops 1 | bytes 1 | tf_op jit(solution)/shard_map/contract/pallas_call | solution.py:309
  213.0 7.8 %fc2_grad_near.1 = (bf16[2,4,64,2048]{3,2,1,0:T(8,128)(2,1)S(1)}, bf16[2,4,64,2048]{3,2,1,0:T(8,128)(2,1)}) custom-call(s32[1]{0:T(128)} %bitcast.me_ref, bf16[1024,640]{1,0:T(8,128)(2,1)S(1)} %copy-done.26, bf16[640,4096]{1,0:T(8,128)(2,1)S(1)} %get-tuple-element.146.right_ref.hid_ref, bf16[2,2,4,64,2048]{4,3,2,1,0:T(8,128)(2,1)} %collective-permute-done.30.refs_0_), custom_call_target="tpu_custom_call" | custom-call | flops 1 | bytes 1 | tf_op jit(solution)/shard_map/fc2_grad_near/pallas_call | solution.py:610
  225.9 13.1 %norm_two_back.1 = (f32[640,1024]{1,0:T(8,128)S(1)}, f32[8,1024]{1,0:T(8,128)S(1)}, bf16[640,1024]{1,0:T(8,128)(2,1)S(1)}, bf16[1024,640]{1,0:T(8,128)(2,1)S(1)}) custom-call(s32[1]{0:T(128)} %bitcast.me_ref, bf16[640,4096]{1,0:T(8,128)(2,1)} %copy-done.2, f32[640,1024]{1,0:T(8,128)S(1)} %copy-done.28, f32[640,1024]{1,0:T(8,128)S(1)} %bitcast.125, ...), custom_call_target="tpu_custom_call" | custom-call | flops 1 | bytes 1 | tf_op jit(solution)/shard_map/norm_two_back/pallas_call | solution.py:393
  240.7 6.0 %fc1_grad_far.1 = bf16[2,2,4,64,2048]{4,3,2,1,0:T(8,128)(2,1)} custom-call(s32[1]{0:T(128)} %bitcast.me_ref, bf16[1024,640]{1,0:T(8,128)(2,1)S(1)} %copy-done.37, bf16[640,4096]{1,0:T(8,128)(2,1)S(1)} %bitcast.120), custom_call_target="tpu_custom_call" | custom-call | flops 1 | bytes 1 | tf_op jit(solution)/shard_map/fc1_grad_far/pallas_call | solution.py:610
  251.0 3.1 mixed_back.1.grad_ref
  255.8 8.6 %collective-permute-done.32 = bf16[4,64,2048]{2,1,0:T(8,128)(2,1)S(1)} collective-permute-done((bf16[4,64,2048]{2,1,0:T(8,128)(2,1)S(1)}, bf16[4,64,2048]{2,1,0:T(8,128)(2,1)S(1)}, u32[]{:S(2)}, u32[]{:S(2)}) %collective-permute-start.32) | collective-permute-done | bytes 1048608 | tf_op jit(solution)/shard_map/ppermute | solution.py:625
  265.7 6.1 %fc1_grad_near.1 = (bf16[2,4,64,2048]{3,2,1,0:T(8,128)(2,1)S(1)}, bf16[2,4,64,2048]{3,2,1,0:T(8,128)(2,1)}) custom-call(s32[1]{0:T(128)} %bitcast.me_ref, bf16[1024,640]{1,0:T(8,128)(2,1)S(1)} %copy-done.37, bf16[640,4096]{1,0:T(8,128)(2,1)S(1)} %bitcast.120, bf16[2,2,4,64,2048]{4,3,2,1,0:T(8,128)(2,1)S(1)} %collective-permute-done.33.refs_0_), custom_call_target="tpu_custom_call" | custom-call | flops 1 | bytes 1 | tf_op jit(solution)/shard_map/fc1_grad_near/pallas_call | solution.py:610
  274.5 2.1 collective-permute-start.36
  280.7 21.1 %attend_back.1 = (bf16[640,3072]{1,0:T(8,128)(2,1)S(1)}, f32[2,2,1,1536]{3,2,1,0:T(1,128)S(1)}) custom-call(s32[1]{0:T(128)} %bitcast.me_ref, bf16[640,3072]{1,0:T(8,128)(2,1)S(1)} %copy-done.24, bf16[640,1024]{1,0:T(8,128)(2,1)S(1)} %copy-done.31, s32[2,320,1]{2,1,0:T(8,128)S(1)} %copy-done.43), custom_call_target="tpu_custom_call" | custom-call | flops 1 | bytes 1 | tf_op jit(solution)/shard_map/attend_back/pallas_call | solution.py:484
  301.8 2.6 convert_add_fusion.1
  304.5 2.4 add_convert_fusion
  310.4 4.2 %qkv_grad_far.1 = bf16[2,2,4,64,1536]{4,3,2,1,0:T(8,128)(2,1)S(1)} custom-call(s32[1]{0:T(128)} %bitcast.me_ref, bf16[1024,640]{1,0:T(8,128)(2,1)S(1)} %copy-done.35, bf16[640,3072]{1,0:T(8,128)(2,1)S(1)} %get-tuple-element.175.right_ref.low_ref), custom_call_target="tpu_custom_call" | custom-call | flops 1 | bytes 1 | tf_op jit(solution)/shard_map/qkv_grad_far/pallas_call | solution.py:610
  317.9 2.6 collective-permute-done.39.refs_0_
  320.5 4.9 %qkv_grad_near.1 = (bf16[2,4,64,1536]{3,2,1,0:T(8,128)(2,1)S(1)}, bf16[2,4,64,1536]{3,2,1,0:T(8,128)(2,1)S(1)}) custom-call(s32[1]{0:T(128)} %bitcast.me_ref, bf16[1024,640]{1,0:T(8,128)(2,1)S(1)} %copy-done.35, bf16[640,3072]{1,0:T(8,128)(2,1)S(1)} %get-tuple-element.175.right_ref.low_ref, bf16[2,2,4,64,1536]{4,3,2,1,0:T(8,128)(2,1)S(1)} %collective-permute-done.39.refs_0_), custom_call_target="tpu_custom_call" | custom-call | flops 1 | bytes 1 | tf_op jit(solution)/shard_map/qkv_grad_near/pallas_call | solution.py:610
  325.4 6.2 %collective-permute-done.40 = bf16[2,4,64,512]{3,2,1,0:T(8,128)(2,1)S(1)} collective-permute-done((bf16[2,4,64,512]{3,2,1,0:T(8,128)(2,1)S(1)}, bf16[2,4,64,512]{3,2,1,0:T(8,128)(2,1)S(1)}, u32[]{:S(2)}, u32[]{:S(2)}) %collective-permute-start.40) | collective-permute-done | bytes 524320 | tf_op jit(solution)/shard_map/ppermute | solution.py:625
  333.6 3.6 collective-permute-done.41
  338.5 2.5 collective-permute-start.43
  344.2 15.2 %norm_one_back.1 = (f32[640,1024]{1,0:T(8,128)}, f32[8,1024]{1,0:T(8,128)}) custom-call(s32[1]{0:T(128)} %bitcast.me_ref, bf16[640,3072]{1,0:T(8,128)(2,1)} %copy-done.3, f32[640,1024]{1,0:T(8,128)} %bitcast.122, f32[640,1024]{1,0:T(8,128)} %copy-done.40, f32[16,1024]{1,0:T(8,128)} %get-tuple-element.112.table_ref, bf16[4,64,1664]{2,1,0:T(8,128)(2,1)} %copy-done.52, ...), custom_call_target="tpu_custom_call" | custom-call | flops 1 | bytes 1 | tf_op jit(solution)/shard_map/norm_one_back/pallas_call | solution.py:393
  359.4 2.1 collective-permute-start.46
  371.2 8.0 %collective-permute-done.48 = f32[12,1024]{1,0:T(8,128)S(1)} collective-permute-done((f32[12,1024]{1,0:T(8,128)S(1)}, f32[12,1024]{1,0:T(8,128)S(1)}, u32[]{:S(2)}, u32[]{:S(2)}) %collective-permute-start.48) | collective-permute-done | bytes 49184 | tf_op jit(solution)/shard_map/ppermute | solution.py:625
  382.5 2.4 collective-permute-start.59
  387.3 2.4 collective-permute-start.56
  389.7 2.6 collective-permute-done.58
  399.3 5.7 %collective-permute-done.55 = bf16[64,1536]{1,0:T(8,128)(2,1)S(1)} collective-permute-done((bf16[64,1536]{1,0:T(8,128)(2,1)S(1)}, bf16[64,1536]{1,0:T(8,128)(2,1)S(1)}, u32[]{:S(2)}, u32[]{:S(2)}) %collective-permute-start.55) | collective-permute-done | bytes 196640 | tf_op jit(solution)/shard_map/ppermute | solution.py:625
  (289 shorter events, 98.6 us)
Async XLA Ops:
  3.5 12.2 %collective-permute-start = (bf16[64,1664]{1,0:T(8,128)(2,1)S(1)}, bf16[64,1664]{1,0:T(8,128)(2,1)S(1)}, u32[]{:S(2)}, u32[]{:S(2)}) collective-permute-start(bf16[64,1664]{1,0:T(8,128)(2,1)S(1)} %pad_maximum_fusion.4), channel_id=1, source_target_pairs={{0,8},{1,9},{2,10},{3,11},{4,12},{5,13},{6,14},{7,15},{8,0},{9,1},... | collective-permute-start | bytes 638984 | tf_op jit(solution)/shard_map/ppermute | solution.py:625
  6.6 18.2 %collective-permute-start.1 = (bf16[64,1664]{1,0:T(8,128)(2,1)S(1)}, bf16[64,1664]{1,0:T(8,128)(2,1)S(1)}, u32[]{:S(2)}, u32[]{:S(2)}) collective-permute-start(bf16[64,1664]{1,0:T(8,128)(2,1)S(1)} %pad_maximum_fusion.4), channel_id=1, source_target_pairs={{0,16},{1,17},{2,18},{3,19},{4,20},{5,21},{6,22},{7,23},{8,24},{9,... | collective-permute-start | bytes 638984 | tf_op jit(solution)/shard_map/ppermute | solution.py:625
  9.2 15.6 %collective-permute-start.2 = (bf16[64,1664]{1,0:T(8,128)(2,1)S(1)}, bf16[64,1664]{1,0:T(8,128)(2,1)S(1)}, u32[]{:S(2)}, u32[]{:S(2)}) collective-permute-start(bf16[64,1664]{1,0:T(8,128)(2,1)S(1)} %pad_maximum_fusion.4), channel_id=1, source_target_pairs={{0,24},{1,25},{2,26},{3,27},{4,28},{5,29},{6,30},{7,31},{8,16},{9,... | collective-permute-start | bytes 638984 | tf_op jit(solution)/shard_map/ppermute | solution.py:625
  24.8 24.6 %collective-permute-start.3 = (bf16[4,64,1664]{2,1,0:T(8,128)(2,1)S(1)}, bf16[4,64,1664]{2,1,0:T(8,128)(2,1)S(1)}, u32[]{:S(2)}, u32[]{:S(2)}) collective-permute-start(bf16[4,64,1664]{2,1,0:T(8,128)(2,1)S(1)} %pad_maximum_fusion.2.refs_0_), channel_id=1, source_target_pairs={{0,1},{1,0},{2,6},{3,7},{4,5},{5,4},{6,2},{7,3},{8,9},{9,8},{10,14... | collective-permute-start | bytes 2555912 | tf_op jit(solution)/shard_map/ppermute | solution.py:625
  26.4 23.1 %collective-permute-start.4 = (bf16[4,64,1664]{2,1,0:T(8,128)(2,1)S(1)}, bf16[4,64,1664]{2,1,0:T(8,128)(2,1)S(1)}, u32[]{:S(2)}, u32[]{:S(2)}) collective-permute-start(bf16[4,64,1664]{2,1,0:T(8,128)(2,1)S(1)} %pad_maximum_fusion.2.refs_0_), channel_id=1, source_target_pairs={{0,4},{1,5},{2,3},{3,2},{4,0},{5,1},{6,7},{7,6},{8,12},{9,13},{10,... | collective-permute-start | bytes 2555912 | tf_op jit(solution)/shard_map/ppermute | solution.py:625
  27.9 21.6 %collective-permute-start.5 = (bf16[4,64,1664]{2,1,0:T(8,128)(2,1)S(1)}, bf16[4,64,1664]{2,1,0:T(8,128)(2,1)S(1)}, u32[]{:S(2)}, u32[]{:S(2)}) collective-permute-start(bf16[4,64,1664]{2,1,0:T(8,128)(2,1)S(1)} %pad_maximum_fusion.2.refs_0_), channel_id=1, source_target_pairs={{0,2},{1,3},{2,0},{3,1},{4,6},{5,7},{6,4},{7,5},{8,10},{9,11},{10,... | collective-permute-start | bytes 2555912 | tf_op jit(solution)/shard_map/ppermute | solution.py:625
  27.9 19.0 %collective-permute-start.6 = (bf16[64,2560]{1,0:T(8,128)(2,1)S(1)}, bf16[64,2560]{1,0:T(8,128)(2,1)S(1)}, u32[]{:S(2)}, u32[]{:S(2)}) collective-permute-start(bf16[64,2560]{1,0:T(8,128)(2,1)S(1)} %pad_maximum_fusion.3), channel_id=1, source_target_pairs={{0,8},{1,9},{2,10},{3,11},{4,12},{5,13},{6,14},{7,15},{8,0},{9,1},... | collective-permute-start | bytes 983048 | tf_op jit(solution)/shard_map/ppermute | solution.py:625
  31.7 17.8 %collective-permute-start.7 = (bf16[64,2560]{1,0:T(8,128)(2,1)S(1)}, bf16[64,2560]{1,0:T(8,128)(2,1)S(1)}, u32[]{:S(2)}, u32[]{:S(2)}) collective-permute-start(bf16[64,2560]{1,0:T(8,128)(2,1)S(1)} %pad_maximum_fusion.3), channel_id=1, source_target_pairs={{0,16},{1,17},{2,18},{3,19},{4,20},{5,21},{6,22},{7,23},{8,24},{9,... | collective-permute-start | bytes 983048 | tf_op jit(solution)/shard_map/ppermute | solution.py:625
  50.5 12.7 %collective-permute-start.8 = (bf16[4,64,1664]{2,1,0:T(8,128)(2,1)S(1)}, bf16[4,64,1664]{2,1,0:T(8,128)(2,1)S(1)}, u32[]{:S(2)}, u32[]{:S(2)}) collective-permute-start(bf16[4,64,1664]{2,1,0:T(8,128)(2,1)S(1)} %collective-permute-done.3.refs_2_), channel_id=1, source_target_pairs={{0,4},{1,5},{2,3},{3,2},{4,0},{5,1},{6,7},{7,6},{8,12},{9,13},{10,... | collective-permute-start | bytes 2555912 | tf_op jit(solution)/shard_map/ppermute | solution.py:625
  51.0 14.8 %collective-permute-start.11 = (bf16[4,64,1664]{2,1,0:T(8,128)(2,1)S(1)}, bf16[4,64,1664]{2,1,0:T(8,128)(2,1)S(1)}, u32[]{:S(2)}, u32[]{:S(2)}) collective-permute-start(bf16[4,64,1664]{2,1,0:T(8,128)(2,1)S(1)} %collective-permute-done.3.refs_2_), channel_id=1, source_target_pairs={{0,2},{1,3},{2,0},{3,1},{4,6},{5,7},{6,4},{7,5},{8,10},{9,11},{10,... | collective-permute-start | bytes 2555912 | tf_op jit(solution)/shard_map/ppermute | solution.py:625
  51.0 12.0 %collective-permute-start.9 = (bf16[64,2560]{1,0:T(8,128)(2,1)S(1)}, bf16[64,2560]{1,0:T(8,128)(2,1)S(1)}, u32[]{:S(2)}, u32[]{:S(2)}) collective-permute-start(bf16[64,2560]{1,0:T(8,128)(2,1)S(1)} %pad_maximum_fusion.3), channel_id=1, source_target_pairs={{0,24},{1,25},{2,26},{3,27},{4,28},{5,29},{6,30},{7,31},{8,16},{9,... | collective-permute-start | bytes 983048 | tf_op jit(solution)/shard_map/ppermute | solution.py:625
  63.4 42.8 %collective-permute-start.13 = (bf16[4,64,2560]{2,1,0:T(8,128)(2,1)S(1)}, bf16[4,64,2560]{2,1,0:T(8,128)(2,1)S(1)}, u32[]{:S(2)}, u32[]{:S(2)}) collective-permute-start(bf16[4,64,2560]{2,1,0:T(8,128)(2,1)S(1)} %pad_maximum_fusion.refs_0_), channel_id=1, source_target_pairs={{0,1},{1,0},{2,6},{3,7},{4,5},{5,4},{6,2},{7,3},{8,9},{9,8},{10,14... | collective-permute-start | bytes 3932168 | tf_op jit(solution)/shard_map/ppermute | solution.py:625
  64.0 42.3 %collective-permute-start.14 = (bf16[4,64,2560]{2,1,0:T(8,128)(2,1)S(1)}, bf16[4,64,2560]{2,1,0:T(8,128)(2,1)}, u32[]{:S(2)}, u32[]{:S(2)}) collective-permute-start(bf16[4,64,2560]{2,1,0:T(8,128)(2,1)S(1)} %pad_maximum_fusion.refs_0_), channel_id=1, source_target_pairs={{0,4},{1,5},{2,3},{3,2},{4,0},{5,1},{6,7},{7,6},{8,12},{9,13},{10,... | collective-permute-start | bytes 3932168 | tf_op jit(solution)/shard_map/ppermute | solution.py:625
  65.3 40.9 %collective-permute-start.17 = (bf16[4,64,2560]{2,1,0:T(8,128)(2,1)S(1)}, bf16[4,64,2560]{2,1,0:T(8,128)(2,1)}, u32[]{:S(2)}, u32[]{:S(2)}) collective-permute-start(bf16[4,64,2560]{2,1,0:T(8,128)(2,1)S(1)} %pad_maximum_fusion.refs_0_), channel_id=1, source_target_pairs={{0,2},{1,3},{2,0},{3,1},{4,6},{5,7},{6,4},{7,5},{8,10},{9,11},{10,... | collective-permute-start | bytes 3932168 | tf_op jit(solution)/shard_map/ppermute | solution.py:625
  69.6 36.6 %collective-permute-start.15 = (bf16[64,2048]{1,0:T(8,128)(2,1)}, bf16[64,2048]{1,0:T(8,128)(2,1)}, u32[]{:S(2)}, u32[]{:S(2)}) collective-permute-start(bf16[64,2048]{1,0:T(8,128)(2,1)} %convert_bitcast_fusion), channel_id=1, source_target_pairs={{0,8},{1,9},{2,10},{3,11},{4,12},{5,13},{6,14},{7,15},{8,0},{9,1},... | collective-permute-start | bytes 786440 | tf_op jit(solution)/shard_map/ppermute | solution.py:625
  75.7 30.5 %collective-permute-start.16 = (bf16[64,2048]{1,0:T(8,128)(2,1)}, bf16[64,2048]{1,0:T(8,128)(2,1)}, u32[]{:S(2)}, u32[]{:S(2)}) collective-permute-start(bf16[64,2048]{1,0:T(8,128)(2,1)} %convert_bitcast_fusion), channel_id=1, source_target_pairs={{0,16},{1,17},{2,18},{3,19},{4,20},{5,21},{6,22},{7,23},{8,24},{9,... | collective-permute-start | bytes 786440 | tf_op jit(solution)/shard_map/ppermute | solution.py:625
  106.3 17.7 %collective-permute-start.18 = (bf16[4,64,2560]{2,1,0:T(8,128)(2,1)S(1)}, bf16[4,64,2560]{2,1,0:T(8,128)(2,1)S(1)}, u32[]{:S(2)}, u32[]{:S(2)}) collective-permute-start(bf16[4,64,2560]{2,1,0:T(8,128)(2,1)S(1)} %collective-permute-done.13.refs_2_), channel_id=1, source_target_pairs={{0,4},{1,5},{2,3},{3,2},{4,0},{5,1},{6,7},{7,6},{8,12},{9,13},{10,... | collective-permute-start | bytes 3932168 | tf_op jit(solution)/shard_map/ppermute | solution.py:625
  106.9 19.9 %collective-permute-start.20 = (bf16[4,64,2560]{2,1,0:T(8,128)(2,1)}, bf16[4,64,2560]{2,1,0:T(8,128)(2,1)S(1)}, u32[]{:S(2)}, u32[]{:S(2)}) collective-permute-start(bf16[4,64,2560]{2,1,0:T(8,128)(2,1)} %collective-permute-done.14.refs_1_), channel_id=1, source_target_pairs={{0,2},{1,3},{2,0},{3,1},{4,6},{5,7},{6,4},{7,5},{8,10},{9,11},{10,... | collective-permute-start | bytes 3932168 | tf_op jit(solution)/shard_map/ppermute | solution.py:625
  106.9 17.1 %collective-permute-start.19 = (bf16[64,2048]{1,0:T(8,128)(2,1)}, bf16[64,2048]{1,0:T(8,128)(2,1)S(1)}, u32[]{:S(2)}, u32[]{:S(2)}) collective-permute-start(bf16[64,2048]{1,0:T(8,128)(2,1)} %convert_bitcast_fusion), channel_id=1, source_target_pairs={{0,24},{1,25},{2,26},{3,27},{4,28},{5,29},{6,30},{7,31},{8,16},{9,... | collective-permute-start | bytes 786440 | tf_op jit(solution)/shard_map/ppermute | solution.py:625
  108.3 18.5 %collective-permute-start.21 = (bf16[4,64,2560]{2,1,0:T(8,128)(2,1)S(1)}, bf16[4,64,2560]{2,1,0:T(8,128)(2,1)S(1)}, u32[]{:S(2)}, u32[]{:S(2)}) collective-permute-start(bf16[4,64,2560]{2,1,0:T(8,128)(2,1)S(1)} %collective-permute-done.13.refs_2_), channel_id=1, source_target_pairs={{0,2},{1,3},{2,0},{3,1},{4,6},{5,7},{6,4},{7,5},{8,10},{9,11},{10,... | collective-permute-start | bytes 3932168 | tf_op jit(solution)/shard_map/ppermute | solution.py:625
  125.7 25.5 %collective-permute-start.23 = (bf16[4,64,2048]{2,1,0:T(8,128)(2,1)S(1)}, bf16[4,64,2048]{2,1,0:T(8,128)(2,1)}, u32[]{:S(2)}, u32[]{:S(2)}) collective-permute-start(bf16[4,64,2048]{2,1,0:T(8,128)(2,1)S(1)} %pad_maximum_fusion.1.refs_0_), channel_id=1, source_target_pairs={{0,1},{1,0},{2,6},{3,7},{4,5},{5,4},{6,2},{7,3},{8,9},{9,8},{10,14... | collective-permute-start | bytes 3145736 | tf_op jit(solution)/shard_map/ppermute | solution.py:625
  126.2 24.9 %collective-permute-start.24 = (bf16[4,64,2048]{2,1,0:T(8,128)(2,1)S(1)}, bf16[4,64,2048]{2,1,0:T(8,128)(2,1)S(1)}, u32[]{:S(2)}, u32[]{:S(2)}) collective-permute-start(bf16[4,64,2048]{2,1,0:T(8,128)(2,1)S(1)} %pad_maximum_fusion.1.refs_0_), channel_id=1, source_target_pairs={{0,4},{1,5},{2,3},{3,2},{4,0},{5,1},{6,7},{7,6},{8,12},{9,13},{10,... | collective-permute-start | bytes 3145736 | tf_op jit(solution)/shard_map/ppermute | solution.py:625
  126.8 24.4 %collective-permute-start.25 = (bf16[4,64,2048]{2,1,0:T(8,128)(2,1)S(1)}, bf16[4,64,2048]{2,1,0:T(8,128)(2,1)S(1)}, u32[]{:S(2)}, u32[]{:S(2)}) collective-permute-start(bf16[4,64,2048]{2,1,0:T(8,128)(2,1)S(1)} %pad_maximum_fusion.1.refs_0_), channel_id=1, source_target_pairs={{0,2},{1,3},{2,0},{3,1},{4,6},{5,7},{6,4},{7,5},{8,10},{9,11},{10,... | collective-permute-start | bytes 3145736 | tf_op jit(solution)/shard_map/ppermute | solution.py:625
  153.2 25.4 %collective-permute-start.26 = (bf16[4,64,2048]{2,1,0:T(8,128)(2,1)}, bf16[4,64,2048]{2,1,0:T(8,128)(2,1)}, u32[]{:S(2)}, u32[]{:S(2)}) collective-permute-start(bf16[4,64,2048]{2,1,0:T(8,128)(2,1)} %collective-permute-done.23.refs_2_), channel_id=1, source_target_pairs={{0,4},{1,5},{2,3},{3,2},{4,0},{5,1},{6,7},{7,6},{8,12},{9,13},{10,... | collective-permute-start | bytes 3145736 | tf_op jit(solution)/shard_map/ppermute | solution.py:625
  184.5 28.5 %collective-permute-start.30 = (bf16[2,2,4,64,2048]{4,3,2,1,0:T(8,128)(2,1)}, bf16[2,2,4,64,2048]{4,3,2,1,0:T(8,128)(2,1)}, u32[]{:S(2)}, u32[]{:S(2)}) collective-permute-start(bf16[2,2,4,64,2048]{4,3,2,1,0:T(8,128)(2,1)} %fc2_grad_far.1), channel_id=1, source_target_pairs={{0,2},{1,3},{2,0},{3,1},{4,6},{5,7},{6,4},{7,5},{8,10},{9,11},{10,... | collective-permute-start | bytes 12582920 | tf_op jit(solution)/shard_map/ppermute | solution.py:625
  184.6 10.4 %collective-permute-start.28 = (bf16[4,64,2048]{2,1,0:T(8,128)(2,1)}, bf16[4,64,2048]{2,1,0:T(8,128)(2,1)S(1)}, u32[]{:S(2)}, u32[]{:S(2)}) collective-permute-start(bf16[4,64,2048]{2,1,0:T(8,128)(2,1)} %collective-permute-done.23.refs_2_), channel_id=1, source_target_pairs={{0,2},{1,3},{2,0},{3,1},{4,6},{5,7},{6,4},{7,5},{8,10},{9,11},{10,... | collective-permute-start | bytes 3145736 | tf_op jit(solution)/shard_map/ppermute | solution.py:625
  185.2 11.3 %collective-permute-start.29 = (bf16[4,64,2048]{2,1,0:T(8,128)(2,1)}, bf16[4,64,2048]{2,1,0:T(8,128)(2,1)S(1)}, u32[]{:S(2)}, u32[]{:S(2)}) collective-permute-start(bf16[4,64,2048]{2,1,0:T(8,128)(2,1)} %collective-permute-done.26.refs_3_), channel_id=1, source_target_pairs={{0,2},{1,3},{2,0},{3,1},{4,6},{5,7},{6,4},{7,5},{8,10},{9,11},{10,... | collective-permute-start | bytes 3145736 | tf_op jit(solution)/shard_map/ppermute | solution.py:625
  222.1 26.4 %collective-permute-start.31 = (bf16[2,4,64,2048]{3,2,1,0:T(8,128)(2,1)}, bf16[2,4,64,2048]{3,2,1,0:T(8,128)(2,1)S(1)}, u32[]{:S(2)}, u32[]{:S(2)}) collective-permute-start(bf16[2,4,64,2048]{3,2,1,0:T(8,128)(2,1)} %get-tuple-element.153), channel_id=1, source_target_pairs={{0,1},{1,0},{2,6},{3,7},{4,5},{5,4},{6,2},{7,3},{8,9},{9,8},{10,14... | collective-permute-start | bytes 6291464 | tf_op jit(solution)/shard_map/ppermute | solution.py:625
  246.6 19.1 %collective-permute-start.33 = (bf16[2,2,4,64,2048]{4,3,2,1,0:T(8,128)(2,1)}, bf16[2,2,4,64,2048]{4,3,2,1,0:T(8,128)(2,1)S(1)}, u32[]{:S(2)}, u32[]{:S(2)}) collective-permute-start(bf16[2,2,4,64,2048]{4,3,2,1,0:T(8,128)(2,1)} %fc1_grad_far.1), channel_id=1, source_target_pairs={{0,2},{1,3},{2,0},{3,1},{4,6},{5,7},{6,4},{7,5},{8,10},{9,11},{10,... | collective-permute-start | bytes 12582920 | tf_op jit(solution)/shard_map/ppermute | solution.py:625
  249.5 14.9 %collective-permute-start.32 = (bf16[4,64,2048]{2,1,0:T(8,128)(2,1)S(1)}, bf16[4,64,2048]{2,1,0:T(8,128)(2,1)S(1)}, u32[]{:S(2)}, u32[]{:S(2)}) collective-permute-start(bf16[4,64,2048]{2,1,0:T(8,128)(2,1)S(1)} %get-tuple-element.222), channel_id=1, source_target_pairs={{0,4},{1,5},{2,3},{3,2},{4,0},{5,1},{6,7},{7,6},{8,12},{9,13},{10,... | collective-permute-start | bytes 3145736 | tf_op jit(solution)/shard_map/ppermute | solution.py:625
  271.9 32.6 %collective-permute-start.37 = (bf16[2,4,64,2048]{3,2,1,0:T(8,128)(2,1)}, bf16[2,4,64,2048]{3,2,1,0:T(8,128)(2,1)}, u32[]{:S(2)}, u32[]{:S(2)}) collective-permute-start(bf16[2,4,64,2048]{3,2,1,0:T(8,128)(2,1)} %get-tuple-element.165), channel_id=1, source_target_pairs={{0,1},{1,0},{2,6},{3,7},{4,5},{5,4},{6,2},{7,3},{8,9},{9,8},{10,14... | collective-permute-start | bytes 6291464 | tf_op jit(solution)/shard_map/ppermute | solution.py:625
  272.3 29.5 %collective-permute-start.34 = (bf16[64,2048]{1,0:T(8,128)(2,1)}, bf16[64,2048]{1,0:T(8,128)(2,1)}, u32[]{:S(2)}, u32[]{:S(2)}) collective-permute-start(bf16[64,2048]{1,0:T(8,128)(2,1)} %get-tuple-element.230), channel_id=1, source_target_pairs={{0,8},{1,9},{2,10},{3,11},{4,12},{5,13},{6,14},{7,15},{8,0},{9,1},... | collective-permute-start | bytes 786440 | tf_op jit(solution)/shard_map/ppermute | solution.py:625
  273.2 28.6 %collective-permute-start.35 = (bf16[64,2048]{1,0:T(8,128)(2,1)}, bf16[64,2048]{1,0:T(8,128)(2,1)}, u32[]{:S(2)}, u32[]{:S(2)}) collective-permute-start(bf16[64,2048]{1,0:T(8,128)(2,1)} %get-tuple-element.232), channel_id=1, source_target_pairs={{0,16},{1,17},{2,18},{3,19},{4,20},{5,21},{6,22},{7,23},{8,24},{9,... | collective-permute-start | bytes 786440 | tf_op jit(solution)/shard_map/ppermute | solution.py:625
  274.5 27.3 %collective-permute-start.36 = (bf16[64,2048]{1,0:T(8,128)(2,1)}, bf16[64,2048]{1,0:T(8,128)(2,1)}, u32[]{:S(2)}, u32[]{:S(2)}) collective-permute-start(bf16[64,2048]{1,0:T(8,128)(2,1)} %get-tuple-element.231), channel_id=1, source_target_pairs={{0,24},{1,25},{2,26},{3,27},{4,28},{5,29},{6,30},{7,31},{8,16},{9,... | collective-permute-start | bytes 786440 | tf_op jit(solution)/shard_map/ppermute | solution.py:625
  277.6 29.6 %collective-permute-start.38 = (bf16[2,2,4,64,512]{4,3,2,1,0:T(8,128)(2,1)}, bf16[2,2,4,64,512]{4,3,2,1,0:T(8,128)(2,1)S(1)}, u32[]{:S(2)}, u32[]{:S(2)}) collective-permute-start(bf16[2,2,4,64,512]{4,3,2,1,0:T(8,128)(2,1)} %copy-done.51), channel_id=1, source_target_pairs={{0,2},{1,3},{2,0},{3,1},{4,6},{5,7},{6,4},{7,5},{8,10},{9,11},{10,... | collective-permute-start | bytes 3145736 | tf_op jit(solution)/shard_map/ppermute | solution.py:625
  315.2 21.9 %collective-permute-start.41 = (bf16[4,64,2048]{2,1,0:T(8,128)(2,1)S(1)}, bf16[4,64,2048]{2,1,0:T(8,128)(2,1)S(1)}, u32[]{:S(2)}, u32[]{:S(2)}) collective-permute-start(bf16[4,64,2048]{2,1,0:T(8,128)(2,1)S(1)} %get-tuple-element.221), channel_id=1, source_target_pairs={{0,4},{1,5},{2,3},{3,2},{4,0},{5,1},{6,7},{7,6},{8,12},{9,13},{10,... | collective-permute-start | bytes 3145736 | tf_op jit(solution)/shard_map/ppermute | solution.py:625
  316.8 14.8 %collective-permute-start.40 = (bf16[2,4,64,512]{3,2,1,0:T(8,128)(2,1)S(1)}, bf16[2,4,64,512]{3,2,1,0:T(8,128)(2,1)S(1)}, u32[]{:S(2)}, u32[]{:S(2)}) collective-permute-start(bf16[2,4,64,512]{3,2,1,0:T(8,128)(2,1)S(1)} %get-tuple-element.173), channel_id=1, source_target_pairs={{0,1},{1,0},{2,6},{3,7},{4,5},{5,4},{6,2},{7,3},{8,9},{9,8},{10,14... | collective-permute-start | bytes 1572872 | tf_op jit(solution)/shard_map/ppermute | solution.py:625
  332.5 31.2 %collective-permute-start.45 = (bf16[2,4,64,1536]{3,2,1,0:T(8,128)(2,1)S(1)}, bf16[2,4,64,1536]{3,2,1,0:T(8,128)(2,1)}, u32[]{:S(2)}, u32[]{:S(2)}) collective-permute-start(bf16[2,4,64,1536]{3,2,1,0:T(8,128)(2,1)S(1)} %get-tuple-element.184), channel_id=1, source_target_pairs={{0,1},{1,0},{2,6},{3,7},{4,5},{5,4},{6,2},{7,3},{8,9},{9,8},{10,14... | collective-permute-start | bytes 4718600 | tf_op jit(solution)/shard_map/ppermute | solution.py:625
  338.5 23.1 %collective-permute-start.42 = (bf16[64,2048]{1,0:T(8,128)(2,1)}, bf16[64,2048]{1,0:T(8,128)(2,1)}, u32[]{:S(2)}, u32[]{:S(2)}) collective-permute-start(bf16[64,2048]{1,0:T(8,128)(2,1)} %get-tuple-element.226), channel_id=1, source_target_pairs={{0,8},{1,9},{2,10},{3,11},{4,12},{5,13},{6,14},{7,15},{8,0},{9,1},... | collective-permute-start | bytes 786440 | tf_op jit(solution)/shard_map/ppermute | solution.py:625
  338.5 23.1 %collective-permute-start.43 = (bf16[64,2048]{1,0:T(8,128)(2,1)}, bf16[64,2048]{1,0:T(8,128)(2,1)}, u32[]{:S(2)}, u32[]{:S(2)}) collective-permute-start(bf16[64,2048]{1,0:T(8,128)(2,1)} %get-tuple-element.228), channel_id=1, source_target_pairs={{0,16},{1,17},{2,18},{3,19},{4,20},{5,21},{6,22},{7,23},{8,24},{9,... | collective-permute-start | bytes 786440 | tf_op jit(solution)/shard_map/ppermute | solution.py:625
  341.1 20.5 %collective-permute-start.44 = (bf16[64,2048]{1,0:T(8,128)(2,1)}, bf16[64,2048]{1,0:T(8,128)(2,1)}, u32[]{:S(2)}, u32[]{:S(2)}) collective-permute-start(bf16[64,2048]{1,0:T(8,128)(2,1)} %get-tuple-element.227), channel_id=1, source_target_pairs={{0,24},{1,25},{2,26},{3,27},{4,28},{5,29},{6,30},{7,31},{8,16},{9,... | collective-permute-start | bytes 786440 | tf_op jit(solution)/shard_map/ppermute | solution.py:625
  365.7 19.3 %collective-permute-start.50 = (bf16[4,64,1536]{2,1,0:T(8,128)(2,1)S(1)}, bf16[4,64,1536]{2,1,0:T(8,128)(2,1)S(1)}, u32[]{:S(2)}, u32[]{:S(2)}) collective-permute-start(bf16[4,64,1536]{2,1,0:T(8,128)(2,1)S(1)} %get-tuple-element.224), channel_id=1, source_target_pairs={{0,4},{1,5},{2,3},{3,2},{4,0},{5,1},{6,7},{7,6},{8,12},{9,13},{10,... | collective-permute-start | bytes 2359304 | tf_op jit(solution)/shard_map/ppermute | solution.py:625
  369.1 10.1 %collective-permute-start.48 = (f32[12,1024]{1,0:T(8,128)S(1)}, f32[12,1024]{1,0:T(8,128)S(1)}, u32[]{:S(2)}, u32[]{:S(2)}) collective-permute-start(f32[12,1024]{1,0:T(8,128)S(1)} %add.109), channel_id=1, source_target_pairs={{0,4},{1,5},{2,6},{3,7},{4,0},{5,1},{6,2},{7,3},{8,12},{9,13},{10,... | collective-permute-start | bytes 147464 | tf_op jit(solution)/shard_map/ppermute | solution.py:625
  386.4 18.6 %collective-permute-start.55 = (bf16[64,1536]{1,0:T(8,128)(2,1)S(1)}, bf16[64,1536]{1,0:T(8,128)(2,1)S(1)}, u32[]{:S(2)}, u32[]{:S(2)}) collective-permute-start(bf16[64,1536]{1,0:T(8,128)(2,1)S(1)} %get-tuple-element.236), channel_id=1, source_target_pairs={{0,16},{1,17},{2,18},{3,19},{4,20},{5,21},{6,22},{7,23},{8,24},{9,... | collective-permute-start | bytes 589832 | tf_op jit(solution)/shard_map/ppermute | solution.py:625
  387.3 17.7 %collective-permute-start.56 = (bf16[64,1536]{1,0:T(8,128)(2,1)S(1)}, bf16[64,1536]{1,0:T(8,128)(2,1)S(1)}, u32[]{:S(2)}, u32[]{:S(2)}) collective-permute-start(bf16[64,1536]{1,0:T(8,128)(2,1)S(1)} %get-tuple-element.235), channel_id=1, source_target_pairs={{0,24},{1,25},{2,26},{3,27},{4,28},{5,29},{6,30},{7,31},{8,16},{9,... | collective-permute-start | bytes 589832 | tf_op jit(solution)/shard_map/ppermute | solution.py:625
  394.9 11.4 %collective-permute-start.52 = (f32[12,1024]{1,0:T(8,128)S(1)}, f32[12,1024]{1,0:T(8,128)S(1)}, u32[]{:S(2)}, u32[]{:S(2)}) collective-permute-start(f32[12,1024]{1,0:T(8,128)S(1)} %add.111), channel_id=1, source_target_pairs={{0,8},{1,9},{2,10},{3,11},{4,12},{5,13},{6,14},{7,15},{8,0},{9,1},... | collective-permute-start | bytes 147464 | tf_op jit(solution)/shard_map/ppermute | solution.py:625
  395.3 12.9 %collective-permute-start.53 = (f32[12,1024]{1,0:T(8,128)S(1)}, f32[12,1024]{1,0:T(8,128)S(1)}, u32[]{:S(2)}, u32[]{:S(2)}) collective-permute-start(f32[12,1024]{1,0:T(8,128)S(1)} %add.111), channel_id=1, source_target_pairs={{0,16},{1,17},{2,18},{3,19},{4,20},{5,21},{6,22},{7,23},{8,24},{9,... | collective-permute-start | bytes 147464 | tf_op jit(solution)/shard_map/ppermute | solution.py:625
  397.1 11.1 %collective-permute-start.54 = (f32[12,1024]{1,0:T(8,128)S(1)}, f32[12,1024]{1,0:T(8,128)S(1)}, u32[]{:S(2)}, u32[]{:S(2)}) collective-permute-start(f32[12,1024]{1,0:T(8,128)S(1)} %add.111), channel_id=1, source_target_pairs={{0,24},{1,25},{2,26},{3,27},{4,28},{5,29},{6,30},{7,31},{8,16},{9,... | collective-permute-start | bytes 147464 | tf_op jit(solution)/shard_map/ppermute | solution.py:625
  (78 other events, 719.2 us)
where the time goes:
time: 411 us; the launch traced here: 410 us
  Pallas kernels  150 us (36%)
  waiting for transfers between devices  123 us (30%)
  starting transfers between devices  68.5 us (17%)
  local copies, waits for them, and re-layouts  46.7 us (11%)
  other arithmetic  20.5 us (5%)
    ppermute x60, waiting for transfers between devices, swap(): lax.ppermute(value, AXES, [(i, i ^ (other if i & CORE_BIT else bits)) for...  123 us
    ppermute x60, starting transfers between devices, swap(): lax.ppermute(value, AXES, [(i, i ^ (other if i & CORE_BIT else bits)) for...  68.5 us
    pallas_call x8, Pallas kernels, weight_grad_call(): call(body, (steps,), ins, outs, shapes, scratch, 2 * count * width * span...  38.3 us
    unnamed x138, local copies, waits for them, and re-layouts  33.5 us
    pallas_call x2, Pallas kernels, norm_back_call(): call(body, (4,), [pl.BlockSpec((count, chunk), lambda t, me: (0, t)), who...  28.4 us
    pallas_call x1, Pallas kernels, attend_back_call(): call(body, (images, 2), [pl.BlockSpec((seq, 3 * half), lambda i, y, me: (...  21.1 us
    pallas_call x1, Pallas kernels, contract_call(): call(body, (8,), [part, part, whole(count, width), whole(count, width), w...  16.5 us
    pallas_call x1, Pallas kernels, qkv_call(): call(body, (6,), [whole(count, width)] + [ANY] * 8, [whole(count, width),...  13.1 us
  transfers between devices with their start and end apart: 60, of which 22 were waited for; matrix products, arithmetic and copies ran while one was open for 7% of the time, Pallas kernels for 30%

commit v1 on v0

--- a/solution.py
+++ b/solution.py
@@ -275,6 +275,7 @@
         2 * count * width * 2 * span,
         count * span * 8 + width * span * 4,
         "expand",
+        60,
     )(me, normed_two, bias, *pieces)
 
 
@@ -768,14 +769,17 @@
 
     normed_one, turned_one, qkv, table = qkv_call(me, rows_in, pieces_one)
     fc1_full = table[8:12].reshape(4, dp_size, rows).transpose(1, 0, 2).reshape(1, 4 * width)
-    mixed = attend_call(me, qkv, visible)
-    mixed, fc1_full, first_two, second_two, *deep_three, far_own = lax.optimization_barrier(
-        (mixed, fc1_full, first_two, second_two, *deep_three, *far_two)
+    qkv, first_two, second_two, *deep_three, far_own = lax.optimization_barrier(
+        (qkv, first_two, second_two, *deep_three, *far_two)
     )
     both_two = along_second(first_two, size)
     far_two = [far_own, along_core(second_two, size), along_core(first_two, size)]
     plane_two = [held_two, second_two, first_two]
     deep_three += along_depth(deep_three[0], size, [depth - 1])[1:]
+    mixed = attend_call(me, qkv, visible)
+    mixed, fc1_full, both_two, *far_two = lax.optimization_barrier(
+        (mixed, fc1_full, both_two, *far_two)
+    )
     far_two += [along_core(both_two, size)]
     both_two, *deep_three = lax.optimization_barrier((both_two, *deep_three))
     pieces_two = plane_two + [both_two] + far_two
@@ -791,33 +795,35 @@
     far_three = [far_own, along_core(second_three, size), along_core(first_three, size)]
     plane_three = [held_three, second_three, first_three]
     hidden, slope = expand_call(me, normed_two, fc1_full, pieces_two)
-    hidden, both_three = lax.optimization_barrier((hidden, both_three))
-    pieces_three = plane_three + [both_three] + far_three + [along_core(both_three, size)]
-    fc2 = Scatter(out_turned, hidden, size, depth, "fc2_grad")
+    hidden, both_three, *far_three = lax.optimization_barrier((hidden, both_three, *far_three))
+    far_three += [along_core(both_three, size)]
+    pieces_three = plane_three + [both_three] + far_three
+    fc2 = Scatter(out_turned, after(hidden, far_three[3]), size, depth, "fc2_grad")
     done = fc2.far(me)
     outputs, pre_low, fc1_sum = contract_call(
         me, after(hidden, done), slope, out_low, middle, table, pieces_three
     )
-    done = fc2.near(pre_low)
+    fc1 = Scatter(turned_two, pre_low, size, depth, "fc1_grad")
+    done = fc1.far(me)
+    done = fc2.near(done)
     middle_grad, vec_two, middle_low, turned_mid = norm_back_call(
         me, after(pre_low, done), 0, 5, middle, grad_in, table, pieces_two, True, "norm_two_back"
     )
-    fc1 = Scatter(turned_two, after(pre_low, middle_low), size, depth, "fc1_grad")
-    done = fc1.far(me)
-    done = fc2.second(done)
-    mixed_grad = mixed_back_call(me, after(middle_low, done), pieces_two)
+    mixed_grad = mixed_back_call(me, middle_low, pieces_two)
     proj = Scatter(turned_mid, after(mixed, mixed_grad), size, depth, "proj_grad")
     done = proj.far(me)
+    done = fc2.second(done)
+    done = proj.near(done)
+    done = fc1.near(done)
     done = fc2.third(done)
-    done = fc1.near(done)
     qkv_low, qkv_sum = attend_back_call(me, qkv, after(mixed_grad, done), visible_rows)
-    fc2_grad = fc2.last(qkv_low)
-    done = fc1.second(fc2_grad)
-    done = proj.near(done)
-    qkv_out = Scatter(turned_one, after(qkv_low, done), size, depth, "qkv_grad")
+    landed = after(qkv_low, proj.received, *fc2.received)
+    qkv_out = Scatter(turned_one, landed, size, depth, "qkv_grad")
     done = qkv_out.far(me)
+    done = proj.second(done)
+    done = fc1.second(done)
     done = qkv_out.near(done)
-    done = fc1.third(proj.second(done))
+    done = fc1.third(done)
     input_grad, vec_one = norm_back_call(
         me,
         after(qkv_low, done),
@@ -843,15 +849,19 @@
             fc1_sum.reshape(4, width),
         ]
     )
-    fc1_grad = fc1.last(input_grad)
-    done = qkv_out.second(fc1_grad)
+    done = qkv_out.second(input_grad, *fc1.received)
     done = proj.third(done)
     sums = after(sums, done)
-    for bits in (CORE_BIT, X_BIT, Y_BIT):
+    sums = sums + along_core(sums, size)
+    done = qkv_out.third(sums)
+    fc1_grad = fc1.last(done)
+    fc2_grad = fc2.last(done)
+    proj_grad = proj.last(done)
+    sums = after(sums, done)
+    for bits in (X_BIT, Y_BIT):
         sums = sums + swap(sums, size, bits)
-    done = qkv_out.third(sums)
-    proj_grad = proj.last(done)
-    sums = sum(along_depth(after(sums, qkv_out.received[0]), size, range(1, depth)))
+    sums = after(sums, *qkv_out.received)
+    sums = sum(along_depth(sums, size, range(1, depth)))
     qkv_grad = qkv_out.last()
     mine = lax.dynamic_slice_in_dim(sums[:8], dp_rank * rows, rows, 1)
     fc1_mine = lax.dynamic_slice_in_dim(sums[8:].reshape(-1), dp_rank * 4 * rows, 4 * rows, 0)

time: 411 us -> 393 us (0.956)
  waiting for transfers between devices: 123 us -> 92.9 us
  starting transfers between devices: 68.5 us -> 88.4 us
  local copies, waits for them, and re-layouts: 46.7 us -> 35.7 us
    ppermute x60, waiting for transfers between devices: 123 us -> 92.9 us  [swap(): lax.ppermute(value, AXES, [(i, i ^ (other if i & CORE_BIT else bits)) for...]
    ppermute x60, starting transfers between devices: 68.5 us -> 88.4 us  [swap(): lax.ppermute(value, AXES, [(i, i ^ (other if i & CORE_BIT else bits)) for...]
    unnamed x138 -> x144, local copies, waits for them, and re-layouts: 33.5 us -> 22.1 us
    add x3 -> x1, other arithmetic: 4.79 us -> 0.09 us  [last(): result = result + value.astype(F32)]
  transfers between devices with their start and end apart: 60 -> 60, of which waited for: 22 -> 17; matrix products, arithmetic and copies ran while one was open for 7% -> 8% of each run, Pallas kernels for 30% -> 36%
where the time goes in v1:
time: 393 us; the launch traced here: 392 us
  Pallas kernels  153 us (39%)
  waiting for transfers between devices  92.9 us (24%)
  starting transfers between devices  88.4 us (22%)
  local copies, waits for them, and re-layouts  35.7 us (9%)
  other arithmetic  20.7 us (5%)
    ppermute x60, waiting for transfers between devices, swap(): lax.ppermute(value, AXES, [(i, i ^ (other if i & CORE_BIT else bits)) for...  92.9 us
    ppermute x60, starting transfers between devices, swap(): lax.ppermute(value, AXES, [(i, i ^ (other if i & CORE_BIT else bits)) for...  88.4 us
    pallas_call x8, Pallas kernels, weight_grad_call(): call(body, (steps,), ins, outs, shapes, scratch, 2 * count * width * span...  36 us
    pallas_call x2, Pallas kernels, norm_back_call(): call(body, (4,), [pl.BlockSpec((count, chunk), lambda t, me: (0, t)), who...  29 us
    unnamed x144, local copies, waits for them, and re-layouts  22.1 us
    pallas_call x1, Pallas kernels, attend_back_call(): call(body, (images, 2), [pl.BlockSpec((seq, 3 * half), lambda i, y, me: (...  21.1 us
    pallas_call x1, Pallas kernels, contract_call(): call(body, (8,), [part, part, whole(count, width), whole(count, width), w...  16.8 us
    pallas_call x1, Pallas kernels, expand_call(): call(body, (8,), [whole(count, width), pl.BlockSpec((1, chunk), lambda t,...  16.1 us
  transfers between devices with their start and end apart: 60, of which 17 were waited for; matrix products, arithmetic and copies ran while one was open for 8% of the time, Pallas kernels for 36%

profile of v1, /device:TPU:0, one launch (start us, length us, event | category | flops | bytes accessed | tf_op | source)
XLA Modules:
  0.0 392.1 jit_solution(13051590626559484804)
XLA Ops:
  3.5 3.1 collective-permute-start
  6.6 2.6 collective-permute-start.1
  10.3 3.1 fusion.2
  13.4 2.3 collective-permute-done
  15.7 9.1 %collective-permute-done.1 = bf16[64,1664]{1,0:T(8,128)(2,1)S(1)} collective-permute-done((bf16[64,1664]{1,0:T(8,128)(2,1)S(1)}, bf16[64,1664]{1,0:T(8,128)(2,1)S(1)}, u32[]{:S(2)}, u32[]{:S(2)}) %collective-permute-start.1) | collective-permute-done | bytes 213024 | tf_op jit(solution)/shard_map/ppermute | solution.py:626
  27.9 3.8 collective-permute-start.6
  32.7 14.3 %collective-permute-done.6 = bf16[64,2560]{1,0:T(8,128)(2,1)S(1)} collective-permute-done((bf16[64,2560]{1,0:T(8,128)(2,1)S(1)}, bf16[64,2560]{1,0:T(8,128)(2,1)S(1)}, u32[]{:S(2)}, u32[]{:S(2)}) %collective-permute-start.6) | collective-permute-done | bytes 327712 | tf_op jit(solution)/shard_map/ppermute | solution.py:626
  47.0 2.5 collective-permute-done.7
  50.1 2.5 collective-permute-start.9
  53.3 8.8 %collective-permute-done.9 = bf16[64,2560]{1,0:T(8,128)(2,1)S(1)} collective-permute-done((bf16[64,2560]{1,0:T(8,128)(2,1)S(1)}, bf16[64,2560]{1,0:T(8,128)(2,1)S(1)}, u32[]{:S(2)}, u32[]{:S(2)}) %collective-permute-start.9) | collective-permute-done | bytes 327712 | tf_op jit(solution)/shard_map/ppermute | solution.py:626
  65.0 3.7 collective-permute-done.10.refs_5_
  68.7 6.1 %collective-permute-start.15 = (bf16[64,2048]{1,0:T(8,128)(2,1)}, bf16[64,2048]{1,0:T(8,128)(2,1)}, u32[]{:S(2)}, u32[]{:S(2)}) collective-permute-start(bf16[64,2048]{1,0:T(8,128)(2,1)} %convert_bitcast_fusion), channel_id=1, source_target_pairs={{0,8},{1,9},{2,10},{3,11},{4,12},{5,13},{6,14},{7,15},{8,0},{9,1},... | collective-permute-start | bytes 786440 | tf_op jit(solution)/shard_map/ppermute | solution.py:626
  74.8 2.2 collective-permute-start.16
  77.0 13.1 %qkv.1 = (bf16[640,1024]{1,0:T(8,128)(2,1)}, bf16[1024,640]{1,0:T(8,128)(2,1)}, bf16[640,3072]{1,0:T(8,128)(2,1)}, f32[16,1024]{1,0:T(8,128)}) custom-call(s32[1]{0:T(128)} %bitcast.me_ref, f32[640,1024]{1,0:T(8,128)} %bitcast.122, bf16[4,64,1664]{2,1,0:T(8,128)(2,1)} %copy-done.48, bf16[4,64,1664]{2,1,0:T(8,128)(2,1)} %copy-done.50, ...), custom_call_target="tpu_custom_call" | custom-call | flops 1 | bytes 1 | tf_op jit(solution)/shard_map/qkv/pallas_call | solution.py:130
  90.1 3.8 collective-permute-done.13.refs_2_
  95.0 2.5 collective-permute-start.21
  101.3 11.7 %attend.1.mixed_ref.right_ref = bf16[640,1024]{1,0:T(8,128)(2,1)S(1)} custom-call(s32[1]{0:T(128)} %bitcast.me_ref, bf16[640,3072]{1,0:T(8,128)(2,1)S(1)} %copy-done.15, s32[2,1,320]{2,1,0:T(1,128)S(1)} %broadcast_in_dim.10.seen_ref), custom_call_target="tpu_custom_call" | custom-call | flops 1 | bytes 1 | tf_op jit(solution)/shard_map/attend/pallas_call | solution.py:188
  116.9 5.3 %project.1 = (f32[640,1024]{1,0:T(8,128)S(1)}, bf16[640,1024]{1,0:T(8,128)(2,1)S(1)}, bf16[1024,640]{1,0:T(8,128)(2,1)S(1)}) custom-call(s32[1]{0:T(128)} %bitcast.me_ref, bf16[640,1024]{1,0:T(8,128)(2,1)S(1)} %attend.1.mixed_ref.right_ref, f32[640,1024]{1,0:T(8,128)S(1)} %bitcast.124, f32[16,1024]{1,0:T(8,128)S(1)} %copy-done.39, ...), custom_call_target="tpu_custom_call" | custom-call | flops 1 | bytes 1 | tf_op jit(solution)/shard_map/project/pallas_call | solution.py:225
  125.9 14.7 %collective-permute-done.23.refs_2_ = bf16[4,64,2048]{2,1,0:T(8,128)(2,1)} collective-permute-done((bf16[4,64,2048]{2,1,0:T(8,128)(2,1)S(1)}, bf16[4,64,2048]{2,1,0:T(8,128)(2,1)}, u32[]{:S(2)}, u32[]{:S(2)}) %collective-permute-start.23) | collective-permute-done | bytes 1048608 | tf_op jit(solution)/shard_map/ppermute | solution.py:626
  143.3 16.1 %expand.1 = (bf16[640,4096]{1,0:T(8,128)(2,1)}, bf16[640,4096]{1,0:T(8,128)(2,1)}) custom-call(s32[1]{0:T(128)} %bitcast.me_ref, bf16[640,1024]{1,0:T(8,128)(2,1)} %copy-done.38, f32[1,4096]{1,0:T(1,128)} %reshape.119.bias_ref, bf16[4,64,2560]{2,1,0:T(8,128)(2,1)} %copy-done.6, bf16[4,64,2560]{2,1,0:T(8,128)(2,1)} %collective-permute-done.14.refs_1_, ...), custom_call_target="tpu_custom_call" | custom-call | flops 1 | bytes 1 | tf_op jit(solution)/shard_map/expand/pallas_call | solution.py:268
  162.2 2.3 collective-permute-done.29.refs_7_
  164.4 2.5 copy-done.3
  166.9 5.9 %fc2_grad_far.1 = bf16[2,2,4,64,2048]{4,3,2,1,0:T(8,128)(2,1)} custom-call(s32[1]{0:T(128)} %bitcast.me_ref, bf16[1024,640]{1,0:T(8,128)(2,1)S(1)} %copy.56.turn_ref, bf16[640,4096]{1,0:T(8,128)(2,1)S(1)} %copy-done.3), custom_call_target="tpu_custom_call" | custom-call | flops 1 | bytes 1 | tf_op jit(solution)/shard_map/fc2_grad_far/pallas_call | solution.py:611
  174.8 16.8 %contract.1 = (f32[640,1024]{1,0:T(8,128)}, bf16[640,4096]{1,0:T(8,128)(2,1)S(1)}, f32[1,4096]{1,0:T(1,128)S(1)}) custom-call(s32[1]{0:T(128)} %bitcast.me_ref, bf16[640,4096]{1,0:T(8,128)(2,1)S(1)} %copy-done.4, bf16[640,4096]{1,0:T(8,128)(2,1)} %get-tuple-element.155.slope_ref, bf16[640,1024]{1,0:T(8,128)(2,1)S(1)} %copy-done.17, ...), custom_call_target="tpu_custom_call" | custom-call | flops 1 | bytes 1 | tf_op jit(solution)/shard_map/contract/pallas_call | solution.py:310
  191.7 5.9 %fc1_grad_far.1 = bf16[2,2,4,64,2048]{4,3,2,1,0:T(8,128)(2,1)} custom-call(s32[1]{0:T(128)} %bitcast.me_ref, bf16[1024,640]{1,0:T(8,128)(2,1)S(1)} %copy-done.26, bf16[640,4096]{1,0:T(8,128)(2,1)S(1)} %get-tuple-element.174.right_ref.low_ref), custom_call_target="tpu_custom_call" | custom-call | flops 1 | bytes 1 | tf_op jit(solution)/shard_map/fc1_grad_far/pallas_call | solution.py:611
  197.7 6.1 %fc2_grad_near.1 = (bf16[2,4,64,2048]{3,2,1,0:T(8,128)(2,1)S(1)}, bf16[2,4,64,2048]{3,2,1,0:T(8,128)(2,1)S(1)}) custom-call(s32[1]{0:T(128)} %bitcast.me_ref, bf16[1024,640]{1,0:T(8,128)(2,1)S(1)} %copy.56.turn_ref, bf16[640,4096]{1,0:T(8,128)(2,1)S(1)} %copy-done.4, bf16[2,2,4,64,2048]{4,3,2,1,0:T(8,128)(2,1)} %collective-permute-done.30.refs_0_), custom_call_target="tpu_custom_call" | custom-call | flops 1 | bytes 1 | tf_op jit(solution)/shard_map/fc2_grad_near/pallas_call | solution.py:611
  207.0 13.9 %norm_two_back.1 = (f32[640,1024]{1,0:T(8,128)S(1)}, f32[8,1024]{1,0:T(8,128)S(1)}, bf16[640,1024]{1,0:T(8,128)(2,1)S(1)}, bf16[1024,640]{1,0:T(8,128)(2,1)S(1)}) custom-call(s32[1]{0:T(128)} %bitcast.me_ref, bf16[640,4096]{1,0:T(8,128)(2,1)} %copy-done.2, f32[640,1024]{1,0:T(8,128)S(1)} %copy-done.20, f32[640,1024]{1,0:T(8,128)S(1)} %bitcast.126, ...), custom_call_target="tpu_custom_call" | custom-call | flops 1 | bytes 1 | tf_op jit(solution)/shard_map/norm_two_back/pallas_call | solution.py:394
  222.4 3.3 mixed_back.1.grad_ref
  227.5 3.7 collective-permute-done.31
  231.3 2.5 add_convert_fusion.1
  236.7 5.6 %fc1_grad_near.1 = (bf16[2,4,64,2048]{3,2,1,0:T(8,128)(2,1)S(1)}, bf16[2,4,64,2048]{3,2,1,0:T(8,128)(2,1)}) custom-call(s32[1]{0:T(128)} %bitcast.me_ref, bf16[1024,640]{1,0:T(8,128)(2,1)S(1)} %copy-done.27, bf16[640,4096]{1,0:T(8,128)(2,1)S(1)} %bitcast.121, bf16[2,2,4,64,2048]{4,3,2,1,0:T(8,128)(2,1)} %collective-permute-done.33.refs_0_), custom_call_target="tpu_custom_call" | custom-call | flops 1 | bytes 1 | tf_op jit(solution)/shard_map/fc1_grad_near/pallas_call | solution.py:611
  244.5 6.4 %collective-permute-done.34 = bf16[4,64,2048]{2,1,0:T(8,128)(2,1)S(1)} collective-permute-done((bf16[4,64,2048]{2,1,0:T(8,128)(2,1)S(1)}, bf16[4,64,2048]{2,1,0:T(8,128)(2,1)S(1)}, u32[]{:S(2)}, u32[]{:S(2)}) %collective-permute-start.34) | collective-permute-done | bytes 1048608 | tf_op jit(solution)/shard_map/ppermute | solution.py:626
  252.3 4.8 %collective-permute-start.36 = (bf16[64,2048]{1,0:T(8,128)(2,1)}, bf16[64,2048]{1,0:T(8,128)(2,1)}, u32[]{:S(2)}, u32[]{:S(2)}) collective-permute-start(bf16[64,2048]{1,0:T(8,128)(2,1)} %get-tuple-element.248), channel_id=1, source_target_pairs={{0,8},{1,9},{2,10},{3,11},{4,12},{5,13},{6,14},{7,15},{8,0},{9,1},... | collective-permute-start | bytes 786440 | tf_op jit(solution)/shard_map/ppermute | solution.py:626
  264.8 21.1 %attend_back.1 = (bf16[640,3072]{1,0:T(8,128)(2,1)S(1)}, f32[2,2,1,1536]{3,2,1,0:T(1,128)S(1)}) custom-call(s32[1]{0:T(128)} %bitcast.me_ref, bf16[640,3072]{1,0:T(8,128)(2,1)S(1)} %copy-done.16, bf16[640,1024]{1,0:T(8,128)(2,1)S(1)} %copy-done.23, s32[2,320,1]{2,1,0:T(8,128)S(1)} %copy-done.37), custom_call_target="tpu_custom_call" | custom-call | flops 1 | bytes 1 | tf_op jit(solution)/shard_map/attend_back/pallas_call | solution.py:485
  286.0 4.5 %qkv_grad_far.1 = bf16[2,2,4,64,1536]{4,3,2,1,0:T(8,128)(2,1)S(1)} custom-call(s32[1]{0:T(128)} %bitcast.me_ref, bf16[1024,640]{1,0:T(8,128)(2,1)S(1)} %copy-done.24, bf16[640,3072]{1,0:T(8,128)(2,1)S(1)} %get-tuple-element.189.right_ref.low_ref), custom_call_target="tpu_custom_call" | custom-call | flops 1 | bytes 1 | tf_op jit(solution)/shard_map/qkv_grad_far/pallas_call | solution.py:611
  292.7 2.4 add_convert_fusion
  296.2 4.7 %qkv_grad_near.1 = (bf16[2,4,64,1536]{3,2,1,0:T(8,128)(2,1)S(1)}, bf16[2,4,64,1536]{3,2,1,0:T(8,128)(2,1)}) custom-call(s32[1]{0:T(128)} %bitcast.me_ref, bf16[1024,640]{1,0:T(8,128)(2,1)S(1)} %copy-done.24, bf16[640,3072]{1,0:T(8,128)(2,1)S(1)} %get-tuple-element.189.right_ref.low_ref, bf16[2,2,4,64,1536]{4,3,2,1,0:T(8,128)(2,1)S(1)} %collective-permute-done.40.refs_0_), custom_call_target="tpu_custom_call" | custom-call | flops 1 | bytes 1 | tf_op jit(solution)/shard_map/qkv_grad_near/pallas_call | solution.py:611
  300.9 3.8 collective-permute-start.45
  304.7 8.2 %collective-permute-done.41 = bf16[4,64,2048]{2,1,0:T(8,128)(2,1)S(1)} collective-permute-done((bf16[4,64,2048]{2,1,0:T(8,128)(2,1)S(1)}, bf16[4,64,2048]{2,1,0:T(8,128)(2,1)S(1)}, u32[]{:S(2)}, u32[]{:S(2)}) %collective-permute-start.41) | collective-permute-done | bytes 1048608 | tf_op jit(solution)/shard_map/ppermute | solution.py:626
  319.3 15.1 %norm_one_back.1 = (f32[640,1024]{1,0:T(8,128)}, f32[8,1024]{1,0:T(8,128)}) custom-call(s32[1]{0:T(128)} %bitcast.me_ref, bf16[640,3072]{1,0:T(8,128)(2,1)} %copy-done.5, f32[640,1024]{1,0:T(8,128)} %bitcast.123, f32[640,1024]{1,0:T(8,128)} %copy-done.30, f32[16,1024]{1,0:T(8,128)} %get-tuple-element.126.table_ref, bf16[4,64,1664]{2,1,0:T(8,128)(2,1)} %copy-done.48, ...), custom_call_target="tpu_custom_call" | custom-call | flops 1 | bytes 1 | tf_op jit(solution)/shard_map/norm_one_back/pallas_call | solution.py:394
  342.6 2.9 collective-permute-start.47
  345.5 5.8 %collective-permute-start.57 = (bf16[64,512]{1,0:T(8,128)(2,1)S(1)}, bf16[64,512]{1,0:T(8,128)(2,1)S(1)}, u32[]{:S(2)}, u32[]{:S(2)}) collective-permute-start(bf16[64,512]{1,0:T(8,128)(2,1)S(1)} %get-tuple-element.259), channel_id=1, source_target_pairs={{0,8},{1,9},{2,10},{3,11},{4,12},{5,13},{6,14},{7,15},{8,0},{9,1},... | collective-permute-start | bytes 196616 | tf_op jit(solution)/shard_map/ppermute | solution.py:626
  354.1 2.7 collective-permute-start.51
  357.5 2.4 add_bitcast_fusion
  363.7 6.2 %collective-permute-start.50 = (f32[12,1024]{1,0:T(8,128)S(1)}, f32[12,1024]{1,0:T(8,128)S(1)}, u32[]{:S(2)}, u32[]{:S(2)}) collective-permute-start(f32[12,1024]{1,0:T(8,128)S(1)} %add.105), channel_id=1, source_target_pairs={{0,1},{1,0},{2,3},{3,2},{4,5},{5,4},{6,7},{7,6},{8,9},{9,8},{10,11... | collective-permute-start | bytes 147464 | tf_op jit(solution)/shard_map/ppermute | solution.py:626
  372.2 5.4 %collective-permute-done.52 = bf16[64,1536]{1,0:T(8,128)(2,1)S(1)} collective-permute-done((bf16[64,1536]{1,0:T(8,128)(2,1)S(1)}, bf16[64,1536]{1,0:T(8,128)(2,1)S(1)}, u32[]{:S(2)}, u32[]{:S(2)}) %collective-permute-start.52) | collective-permute-done | bytes 196640 | tf_op jit(solution)/shard_map/ppermute | solution.py:626
  377.6 4.7 %collective-permute-start.54 = (f32[12,1024]{1,0:T(8,128)S(1)}, f32[12,1024]{1,0:T(8,128)S(1)}, u32[]{:S(2)}, u32[]{:S(2)}) collective-permute-start(f32[12,1024]{1,0:T(8,128)S(1)} %add.106), channel_id=1, source_target_pairs={{0,8},{1,9},{2,10},{3,11},{4,12},{5,13},{6,14},{7,15},{8,0},{9,1},... | collective-permute-start | bytes 147464 | tf_op jit(solution)/shard_map/ppermute | solution.py:626
  385.9 4.3 %collective-permute-done.55 = f32[12,1024]{1,0:T(8,128)S(1)} collective-permute-done((f32[12,1024]{1,0:T(8,128)S(1)}, f32[12,1024]{1,0:T(8,128)S(1)}, u32[]{:S(2)}, u32[]{:S(2)}) %collective-permute-start.55) | collective-permute-done | bytes 49184 | tf_op jit(solution)/shard_map/ppermute | solution.py:626
  (294 shorter events, 85.1 us)
Async XLA Ops:
  3.5 12.2 %collective-permute-start = (bf16[64,1664]{1,0:T(8,128)(2,1)S(1)}, bf16[64,1664]{1,0:T(8,128)(2,1)S(1)}, u32[]{:S(2)}, u32[]{:S(2)}) collective-permute-start(bf16[64,1664]{1,0:T(8,128)(2,1)S(1)} %pad_maximum_fusion.4), channel_id=1, source_target_pairs={{0,8},{1,9},{2,10},{3,11},{4,12},{5,13},{6,14},{7,15},{8,0},{9,1},... | collective-permute-start | bytes 638984 | tf_op jit(solution)/shard_map/ppermute | solution.py:626
  6.6 18.2 %collective-permute-start.1 = (bf16[64,1664]{1,0:T(8,128)(2,1)S(1)}, bf16[64,1664]{1,0:T(8,128)(2,1)S(1)}, u32[]{:S(2)}, u32[]{:S(2)}) collective-permute-start(bf16[64,1664]{1,0:T(8,128)(2,1)S(1)} %pad_maximum_fusion.4), channel_id=1, source_target_pairs={{0,16},{1,17},{2,18},{3,19},{4,20},{5,21},{6,22},{7,23},{8,24},{9,... | collective-permute-start | bytes 638984 | tf_op jit(solution)/shard_map/ppermute | solution.py:626
  9.2 15.6 %collective-permute-start.2 = (bf16[64,1664]{1,0:T(8,128)(2,1)S(1)}, bf16[64,1664]{1,0:T(8,128)(2,1)S(1)}, u32[]{:S(2)}, u32[]{:S(2)}) collective-permute-start(bf16[64,1664]{1,0:T(8,128)(2,1)S(1)} %pad_maximum_fusion.4), channel_id=1, source_target_pairs={{0,24},{1,25},{2,26},{3,27},{4,28},{5,29},{6,30},{7,31},{8,16},{9,... | collective-permute-start | bytes 638984 | tf_op jit(solution)/shard_map/ppermute | solution.py:626
  24.8 24.6 %collective-permute-start.3 = (bf16[4,64,1664]{2,1,0:T(8,128)(2,1)S(1)}, bf16[4,64,1664]{2,1,0:T(8,128)(2,1)S(1)}, u32[]{:S(2)}, u32[]{:S(2)}) collective-permute-start(bf16[4,64,1664]{2,1,0:T(8,128)(2,1)S(1)} %pad_maximum_fusion.2.refs_0_), channel_id=1, source_target_pairs={{0,1},{1,0},{2,6},{3,7},{4,5},{5,4},{6,2},{7,3},{8,9},{9,8},{10,14... | collective-permute-start | bytes 2555912 | tf_op jit(solution)/shard_map/ppermute | solution.py:626
  26.4 23.1 %collective-permute-start.4 = (bf16[4,64,1664]{2,1,0:T(8,128)(2,1)S(1)}, bf16[4,64,1664]{2,1,0:T(8,128)(2,1)S(1)}, u32[]{:S(2)}, u32[]{:S(2)}) collective-permute-start(bf16[4,64,1664]{2,1,0:T(8,128)(2,1)S(1)} %pad_maximum_fusion.2.refs_0_), channel_id=1, source_target_pairs={{0,4},{1,5},{2,3},{3,2},{4,0},{5,1},{6,7},{7,6},{8,12},{9,13},{10,... | collective-permute-start | bytes 2555912 | tf_op jit(solution)/shard_map/ppermute | solution.py:626
  27.9 21.6 %collective-permute-start.5 = (bf16[4,64,1664]{2,1,0:T(8,128)(2,1)S(1)}, bf16[4,64,1664]{2,1,0:T(8,128)(2,1)S(1)}, u32[]{:S(2)}, u32[]{:S(2)}) collective-permute-start(bf16[4,64,1664]{2,1,0:T(8,128)(2,1)S(1)} %pad_maximum_fusion.2.refs_0_), channel_id=1, source_target_pairs={{0,2},{1,3},{2,0},{3,1},{4,6},{5,7},{6,4},{7,5},{8,10},{9,11},{10,... | collective-permute-start | bytes 2555912 | tf_op jit(solution)/shard_map/ppermute | solution.py:626
  27.9 19.0 %collective-permute-start.6 = (bf16[64,2560]{1,0:T(8,128)(2,1)S(1)}, bf16[64,2560]{1,0:T(8,128)(2,1)S(1)}, u32[]{:S(2)}, u32[]{:S(2)}) collective-permute-start(bf16[64,2560]{1,0:T(8,128)(2,1)S(1)} %pad_maximum_fusion.3), channel_id=1, source_target_pairs={{0,8},{1,9},{2,10},{3,11},{4,12},{5,13},{6,14},{7,15},{8,0},{9,1},... | collective-permute-start | bytes 983048 | tf_op jit(solution)/shard_map/ppermute | solution.py:626
  31.7 17.8 %collective-permute-start.7 = (bf16[64,2560]{1,0:T(8,128)(2,1)S(1)}, bf16[64,2560]{1,0:T(8,128)(2,1)S(1)}, u32[]{:S(2)}, u32[]{:S(2)}) collective-permute-start(bf16[64,2560]{1,0:T(8,128)(2,1)S(1)} %pad_maximum_fusion.3), channel_id=1, source_target_pairs={{0,16},{1,17},{2,18},{3,19},{4,20},{5,21},{6,22},{7,23},{8,24},{9,... | collective-permute-start | bytes 983048 | tf_op jit(solution)/shard_map/ppermute | solution.py:626
  49.5 12.8 %collective-permute-start.8 = (bf16[4,64,1664]{2,1,0:T(8,128)(2,1)S(1)}, bf16[4,64,1664]{2,1,0:T(8,128)(2,1)S(1)}, u32[]{:S(2)}, u32[]{:S(2)}) collective-permute-start(bf16[4,64,1664]{2,1,0:T(8,128)(2,1)S(1)} %collective-permute-done.3.refs_2_), channel_id=1, source_target_pairs={{0,4},{1,5},{2,3},{3,2},{4,0},{5,1},{6,7},{7,6},{8,12},{9,13},{10,... | collective-permute-start | bytes 2555912 | tf_op jit(solution)/shard_map/ppermute | solution.py:626
  50.1 14.8 %collective-permute-start.11 = (bf16[4,64,1664]{2,1,0:T(8,128)(2,1)S(1)}, bf16[4,64,1664]{2,1,0:T(8,128)(2,1)S(1)}, u32[]{:S(2)}, u32[]{:S(2)}) collective-permute-start(bf16[4,64,1664]{2,1,0:T(8,128)(2,1)S(1)} %collective-permute-done.3.refs_2_), channel_id=1, source_target_pairs={{0,2},{1,3},{2,0},{3,1},{4,6},{5,7},{6,4},{7,5},{8,10},{9,11},{10,... | collective-permute-start | bytes 2555912 | tf_op jit(solution)/shard_map/ppermute | solution.py:626
  50.1 12.0 %collective-permute-start.9 = (bf16[64,2560]{1,0:T(8,128)(2,1)S(1)}, bf16[64,2560]{1,0:T(8,128)(2,1)S(1)}, u32[]{:S(2)}, u32[]{:S(2)}) collective-permute-start(bf16[64,2560]{1,0:T(8,128)(2,1)S(1)} %pad_maximum_fusion.3), channel_id=1, source_target_pairs={{0,24},{1,25},{2,26},{3,27},{4,28},{5,29},{6,30},{7,31},{8,16},{9,... | collective-permute-start | bytes 983048 | tf_op jit(solution)/shard_map/ppermute | solution.py:626
  62.5 31.4 %collective-permute-start.13 = (bf16[4,64,2560]{2,1,0:T(8,128)(2,1)S(1)}, bf16[4,64,2560]{2,1,0:T(8,128)(2,1)S(1)}, u32[]{:S(2)}, u32[]{:S(2)}) collective-permute-start(bf16[4,64,2560]{2,1,0:T(8,128)(2,1)S(1)} %pad_maximum_fusion.refs_0_), channel_id=1, source_target_pairs={{0,1},{1,0},{2,6},{3,7},{4,5},{5,4},{6,2},{7,3},{8,9},{9,8},{10,14... | collective-permute-start | bytes 3932168 | tf_op jit(solution)/shard_map/ppermute | solution.py:626
  63.1 30.9 %collective-permute-start.14 = (bf16[4,64,2560]{2,1,0:T(8,128)(2,1)S(1)}, bf16[4,64,2560]{2,1,0:T(8,128)(2,1)}, u32[]{:S(2)}, u32[]{:S(2)}) collective-permute-start(bf16[4,64,2560]{2,1,0:T(8,128)(2,1)S(1)} %pad_maximum_fusion.refs_0_), channel_id=1, source_target_pairs={{0,4},{1,5},{2,3},{3,2},{4,0},{5,1},{6,7},{7,6},{8,12},{9,13},{10,... | collective-permute-start | bytes 3932168 | tf_op jit(solution)/shard_map/ppermute | solution.py:626
  64.4 29.5 %collective-permute-start.17 = (bf16[4,64,2560]{2,1,0:T(8,128)(2,1)S(1)}, bf16[4,64,2560]{2,1,0:T(8,128)(2,1)}, u32[]{:S(2)}, u32[]{:S(2)}) collective-permute-start(bf16[4,64,2560]{2,1,0:T(8,128)(2,1)S(1)} %pad_maximum_fusion.refs_0_), channel_id=1, source_target_pairs={{0,2},{1,3},{2,0},{3,1},{4,6},{5,7},{6,4},{7,5},{8,10},{9,11},{10,... | collective-permute-start | bytes 3932168 | tf_op jit(solution)/shard_map/ppermute | solution.py:626
  68.7 21.4 %collective-permute-start.15 = (bf16[64,2048]{1,0:T(8,128)(2,1)}, bf16[64,2048]{1,0:T(8,128)(2,1)}, u32[]{:S(2)}, u32[]{:S(2)}) collective-permute-start(bf16[64,2048]{1,0:T(8,128)(2,1)} %convert_bitcast_fusion), channel_id=1, source_target_pairs={{0,8},{1,9},{2,10},{3,11},{4,12},{5,13},{6,14},{7,15},{8,0},{9,1},... | collective-permute-start | bytes 786440 | tf_op jit(solution)/shard_map/ppermute | solution.py:626
  74.8 15.3 %collective-permute-start.16 = (bf16[64,2048]{1,0:T(8,128)(2,1)}, bf16[64,2048]{1,0:T(8,128)(2,1)}, u32[]{:S(2)}, u32[]{:S(2)}) collective-permute-start(bf16[64,2048]{1,0:T(8,128)(2,1)} %convert_bitcast_fusion), channel_id=1, source_target_pairs={{0,16},{1,17},{2,18},{3,19},{4,20},{5,21},{6,22},{7,23},{8,24},{9,... | collective-permute-start | bytes 786440 | tf_op jit(solution)/shard_map/ppermute | solution.py:626
  93.9 19.1 %collective-permute-start.18 = (bf16[4,64,2560]{2,1,0:T(8,128)(2,1)S(1)}, bf16[4,64,2560]{2,1,0:T(8,128)(2,1)}, u32[]{:S(2)}, u32[]{:S(2)}) collective-permute-start(bf16[4,64,2560]{2,1,0:T(8,128)(2,1)S(1)} %collective-permute-done.13.refs_2_), channel_id=1, source_target_pairs={{0,4},{1,5},{2,3},{3,2},{4,0},{5,1},{6,7},{7,6},{8,12},{9,13},{10,... | collective-permute-start | bytes 3932168 | tf_op jit(solution)/shard_map/ppermute | solution.py:626
  94.5 18.5 %collective-permute-start.19 = (bf16[4,64,2560]{2,1,0:T(8,128)(2,1)}, bf16[4,64,2560]{2,1,0:T(8,128)(2,1)}, u32[]{:S(2)}, u32[]{:S(2)}) collective-permute-start(bf16[4,64,2560]{2,1,0:T(8,128)(2,1)} %collective-permute-done.14.refs_1_), channel_id=1, source_target_pairs={{0,2},{1,3},{2,0},{3,1},{4,6},{5,7},{6,4},{7,5},{8,10},{9,11},{10,... | collective-permute-start | bytes 3932168 | tf_op jit(solution)/shard_map/ppermute | solution.py:626
  94.5 18.5 %collective-permute-start.20 = (bf16[4,64,2560]{2,1,0:T(8,128)(2,1)S(1)}, bf16[4,64,2560]{2,1,0:T(8,128)(2,1)}, u32[]{:S(2)}, u32[]{:S(2)}) collective-permute-start(bf16[4,64,2560]{2,1,0:T(8,128)(2,1)S(1)} %collective-permute-done.13.refs_2_), channel_id=1, source_target_pairs={{0,2},{1,3},{2,0},{3,1},{4,6},{5,7},{6,4},{7,5},{8,10},{9,11},{10,... | collective-permute-start | bytes 3932168 | tf_op jit(solution)/shard_map/ppermute | solution.py:626
  95.0 18.1 %collective-permute-start.21 = (bf16[64,2048]{1,0:T(8,128)(2,1)}, bf16[64,2048]{1,0:T(8,128)(2,1)S(1)}, u32[]{:S(2)}, u32[]{:S(2)}) collective-permute-start(bf16[64,2048]{1,0:T(8,128)(2,1)} %convert_bitcast_fusion), channel_id=1, source_target_pairs={{0,24},{1,25},{2,26},{3,27},{4,28},{5,29},{6,30},{7,31},{8,16},{9,... | collective-permute-start | bytes 786440 | tf_op jit(solution)/shard_map/ppermute | solution.py:626
  114.7 25.8 %collective-permute-start.23 = (bf16[4,64,2048]{2,1,0:T(8,128)(2,1)S(1)}, bf16[4,64,2048]{2,1,0:T(8,128)(2,1)}, u32[]{:S(2)}, u32[]{:S(2)}) collective-permute-start(bf16[4,64,2048]{2,1,0:T(8,128)(2,1)S(1)} %pad_maximum_fusion.1.refs_0_), channel_id=1, source_target_pairs={{0,1},{1,0},{2,6},{3,7},{4,5},{5,4},{6,2},{7,3},{8,9},{9,8},{10,14... | collective-permute-start | bytes 3145736 | tf_op jit(solution)/shard_map/ppermute | solution.py:626
  115.3 25.3 %collective-permute-start.24 = (bf16[4,64,2048]{2,1,0:T(8,128)(2,1)S(1)}, bf16[4,64,2048]{2,1,0:T(8,128)(2,1)}, u32[]{:S(2)}, u32[]{:S(2)}) collective-permute-start(bf16[4,64,2048]{2,1,0:T(8,128)(2,1)S(1)} %pad_maximum_fusion.1.refs_0_), channel_id=1, source_target_pairs={{0,4},{1,5},{2,3},{3,2},{4,0},{5,1},{6,7},{7,6},{8,12},{9,13},{10,... | collective-permute-start | bytes 3145736 | tf_op jit(solution)/shard_map/ppermute | solution.py:626
  116.8 23.8 %collective-permute-start.25 = (bf16[4,64,2048]{2,1,0:T(8,128)(2,1)S(1)}, bf16[4,64,2048]{2,1,0:T(8,128)(2,1)S(1)}, u32[]{:S(2)}, u32[]{:S(2)}) collective-permute-start(bf16[4,64,2048]{2,1,0:T(8,128)(2,1)S(1)} %pad_maximum_fusion.1.refs_0_), channel_id=1, source_target_pairs={{0,2},{1,3},{2,0},{3,1},{4,6},{5,7},{6,4},{7,5},{8,10},{9,11},{10,... | collective-permute-start | bytes 3145736 | tf_op jit(solution)/shard_map/ppermute | solution.py:626
  141.6 17.9 %collective-permute-start.26 = (bf16[4,64,2048]{2,1,0:T(8,128)(2,1)}, bf16[4,64,2048]{2,1,0:T(8,128)(2,1)}, u32[]{:S(2)}, u32[]{:S(2)}) collective-permute-start(bf16[4,64,2048]{2,1,0:T(8,128)(2,1)} %collective-permute-done.23.refs_2_), channel_id=1, source_target_pairs={{0,4},{1,5},{2,3},{3,2},{4,0},{5,1},{6,7},{7,6},{8,12},{9,13},{10,... | collective-permute-start | bytes 3145736 | tf_op jit(solution)/shard_map/ppermute | solution.py:626
  142.8 16.6 %collective-permute-start.27 = (bf16[4,64,2048]{2,1,0:T(8,128)(2,1)}, bf16[4,64,2048]{2,1,0:T(8,128)(2,1)S(1)}, u32[]{:S(2)}, u32[]{:S(2)}) collective-permute-start(bf16[4,64,2048]{2,1,0:T(8,128)(2,1)} %collective-permute-done.24.refs_1_), channel_id=1, source_target_pairs={{0,2},{1,3},{2,0},{3,1},{4,6},{5,7},{6,4},{7,5},{8,10},{9,11},{10,... | collective-permute-start | bytes 3145736 | tf_op jit(solution)/shard_map/ppermute | solution.py:626
  142.8 17.6 %collective-permute-start.28 = (bf16[4,64,2048]{2,1,0:T(8,128)(2,1)}, bf16[4,64,2048]{2,1,0:T(8,128)(2,1)S(1)}, u32[]{:S(2)}, u32[]{:S(2)}) collective-permute-start(bf16[4,64,2048]{2,1,0:T(8,128)(2,1)} %collective-permute-done.23.refs_2_), channel_id=1, source_target_pairs={{0,2},{1,3},{2,0},{3,1},{4,6},{5,7},{6,4},{7,5},{8,10},{9,11},{10,... | collective-permute-start | bytes 3145736 | tf_op jit(solution)/shard_map/ppermute | solution.py:626
  172.8 24.8 %collective-permute-start.30 = (bf16[2,2,4,64,2048]{4,3,2,1,0:T(8,128)(2,1)}, bf16[2,2,4,64,2048]{4,3,2,1,0:T(8,128)(2,1)}, u32[]{:S(2)}, u32[]{:S(2)}) collective-permute-start(bf16[2,2,4,64,2048]{4,3,2,1,0:T(8,128)(2,1)} %fc2_grad_far.1), channel_id=1, source_target_pairs={{0,2},{1,3},{2,0},{3,1},{4,6},{5,7},{6,4},{7,5},{8,10},{9,11},{10,... | collective-permute-start | bytes 12582920 | tf_op jit(solution)/shard_map/ppermute | solution.py:626
  205.1 26.1 %collective-permute-start.31 = (bf16[2,4,64,2048]{3,2,1,0:T(8,128)(2,1)S(1)}, bf16[2,4,64,2048]{3,2,1,0:T(8,128)(2,1)}, u32[]{:S(2)}, u32[]{:S(2)}) collective-permute-start(bf16[2,4,64,2048]{3,2,1,0:T(8,128)(2,1)S(1)} %get-tuple-element.171), channel_id=1, source_target_pairs={{0,1},{1,0},{2,6},{3,7},{4,5},{5,4},{6,2},{7,3},{8,9},{9,8},{10,14... | collective-permute-start | bytes 6291464 | tf_op jit(solution)/shard_map/ppermute | solution.py:626
  207.0 29.7 %collective-permute-start.33 = (bf16[2,2,4,64,2048]{4,3,2,1,0:T(8,128)(2,1)}, bf16[2,2,4,64,2048]{4,3,2,1,0:T(8,128)(2,1)}, u32[]{:S(2)}, u32[]{:S(2)}) collective-permute-start(bf16[2,2,4,64,2048]{4,3,2,1,0:T(8,128)(2,1)} %fc1_grad_far.1), channel_id=1, source_target_pairs={{0,2},{1,3},{2,0},{3,1},{4,6},{5,7},{6,4},{7,5},{8,10},{9,11},{10,... | collective-permute-start | bytes 12582920 | tf_op jit(solution)/shard_map/ppermute | solution.py:626
  234.1 16.8 %collective-permute-start.34 = (bf16[4,64,2048]{2,1,0:T(8,128)(2,1)S(1)}, bf16[4,64,2048]{2,1,0:T(8,128)(2,1)S(1)}, u32[]{:S(2)}, u32[]{:S(2)}) collective-permute-start(bf16[4,64,2048]{2,1,0:T(8,128)(2,1)S(1)} %get-tuple-element.239), channel_id=1, source_target_pairs={{0,4},{1,5},{2,3},{3,2},{4,0},{5,1},{6,7},{7,6},{8,12},{9,13},{10,... | collective-permute-start | bytes 3145736 | tf_op jit(solution)/shard_map/ppermute | solution.py:626
  242.4 43.6 %collective-permute-start.35 = (bf16[2,4,64,512]{3,2,1,0:T(8,128)(2,1)}, bf16[2,4,64,512]{3,2,1,0:T(8,128)(2,1)}, u32[]{:S(2)}, u32[]{:S(2)}) collective-permute-start(bf16[2,4,64,512]{3,2,1,0:T(8,128)(2,1)} %get-tuple-element.181), channel_id=1, source_target_pairs={{0,1},{1,0},{2,6},{3,7},{4,5},{5,4},{6,2},{7,3},{8,9},{9,8},{10,14... | collective-permute-start | bytes 1572872 | tf_op jit(solution)/shard_map/ppermute | solution.py:626
  244.1 48.7 %collective-permute-start.39 = (bf16[2,4,64,2048]{3,2,1,0:T(8,128)(2,1)}, bf16[2,4,64,2048]{3,2,1,0:T(8,128)(2,1)}, u32[]{:S(2)}, u32[]{:S(2)}) collective-permute-start(bf16[2,4,64,2048]{3,2,1,0:T(8,128)(2,1)} %get-tuple-element.185), channel_id=1, source_target_pairs={{0,1},{1,0},{2,6},{3,7},{4,5},{5,4},{6,2},{7,3},{8,9},{9,8},{10,14... | collective-permute-start | bytes 6291464 | tf_op jit(solution)/shard_map/ppermute | solution.py:626
  252.3 33.7 %collective-permute-start.36 = (bf16[64,2048]{1,0:T(8,128)(2,1)}, bf16[64,2048]{1,0:T(8,128)(2,1)}, u32[]{:S(2)}, u32[]{:S(2)}) collective-permute-start(bf16[64,2048]{1,0:T(8,128)(2,1)} %get-tuple-element.248), channel_id=1, source_target_pairs={{0,8},{1,9},{2,10},{3,11},{4,12},{5,13},{6,14},{7,15},{8,0},{9,1},... | collective-permute-start | bytes 786440 | tf_op jit(solution)/shard_map/ppermute | solution.py:626
  257.1 28.8 %collective-permute-start.37 = (bf16[64,2048]{1,0:T(8,128)(2,1)}, bf16[64,2048]{1,0:T(8,128)(2,1)}, u32[]{:S(2)}, u32[]{:S(2)}) collective-permute-start(bf16[64,2048]{1,0:T(8,128)(2,1)} %get-tuple-element.247), channel_id=1, source_target_pairs={{0,16},{1,17},{2,18},{3,19},{4,20},{5,21},{6,22},{7,23},{8,24},{9,... | collective-permute-start | bytes 786440 | tf_op jit(solution)/shard_map/ppermute | solution.py:626
  257.6 28.4 %collective-permute-start.38 = (bf16[64,2048]{1,0:T(8,128)(2,1)}, bf16[64,2048]{1,0:T(8,128)(2,1)}, u32[]{:S(2)}, u32[]{:S(2)}) collective-permute-start(bf16[64,2048]{1,0:T(8,128)(2,1)} %get-tuple-element.246), channel_id=1, source_target_pairs={{0,24},{1,25},{2,26},{3,27},{4,28},{5,29},{6,30},{7,31},{8,16},{9,... | collective-permute-start | bytes 786440 | tf_op jit(solution)/shard_map/ppermute | solution.py:626
  295.4 17.6 %collective-permute-start.41 = (bf16[4,64,2048]{2,1,0:T(8,128)(2,1)S(1)}, bf16[4,64,2048]{2,1,0:T(8,128)(2,1)S(1)}, u32[]{:S(2)}, u32[]{:S(2)}) collective-permute-start(bf16[4,64,2048]{2,1,0:T(8,128)(2,1)S(1)} %get-tuple-element.237), channel_id=1, source_target_pairs={{0,4},{1,5},{2,3},{3,2},{4,0},{5,1},{6,7},{7,6},{8,12},{9,13},{10,... | collective-permute-start | bytes 3145736 | tf_op jit(solution)/shard_map/ppermute | solution.py:626
  300.9 34.4 %collective-permute-start.45 = (bf16[2,4,64,1536]{3,2,1,0:T(8,128)(2,1)}, bf16[2,4,64,1536]{3,2,1,0:T(8,128)(2,1)}, u32[]{:S(2)}, u32[]{:S(2)}) collective-permute-start(bf16[2,4,64,1536]{3,2,1,0:T(8,128)(2,1)} %get-tuple-element.197), channel_id=1, source_target_pairs={{0,1},{1,0},{2,6},{3,7},{4,5},{5,4},{6,2},{7,3},{8,9},{9,8},{10,14... | collective-permute-start | bytes 4718600 | tf_op jit(solution)/shard_map/ppermute | solution.py:626
  314.1 20.3 %collective-permute-start.42 = (bf16[64,2048]{1,0:T(8,128)(2,1)S(1)}, bf16[64,2048]{1,0:T(8,128)(2,1)S(1)}, u32[]{:S(2)}, u32[]{:S(2)}) collective-permute-start(bf16[64,2048]{1,0:T(8,128)(2,1)S(1)} %get-tuple-element.244), channel_id=1, source_target_pairs={{0,8},{1,9},{2,10},{3,11},{4,12},{5,13},{6,14},{7,15},{8,0},{9,1},... | collective-permute-start | bytes 786440 | tf_op jit(solution)/shard_map/ppermute | solution.py:626
  315.3 19.2 %collective-permute-start.43 = (bf16[64,2048]{1,0:T(8,128)(2,1)S(1)}, bf16[64,2048]{1,0:T(8,128)(2,1)S(1)}, u32[]{:S(2)}, u32[]{:S(2)}) collective-permute-start(bf16[64,2048]{1,0:T(8,128)(2,1)S(1)} %get-tuple-element.243), channel_id=1, source_target_pairs={{0,16},{1,17},{2,18},{3,19},{4,20},{5,21},{6,22},{7,23},{8,24},{9,... | collective-permute-start | bytes 786440 | tf_op jit(solution)/shard_map/ppermute | solution.py:626
  316.6 17.9 %collective-permute-start.44 = (bf16[64,2048]{1,0:T(8,128)(2,1)S(1)}, bf16[64,2048]{1,0:T(8,128)(2,1)S(1)}, u32[]{:S(2)}, u32[]{:S(2)}) collective-permute-start(bf16[64,2048]{1,0:T(8,128)(2,1)S(1)} %get-tuple-element.242), channel_id=1, source_target_pairs={{0,24},{1,25},{2,26},{3,27},{4,28},{5,29},{6,30},{7,31},{8,16},{9,... | collective-permute-start | bytes 786440 | tf_op jit(solution)/shard_map/ppermute | solution.py:626
  318.5 23.1 %collective-permute-start.46 = (bf16[4,64,512]{2,1,0:T(8,128)(2,1)}, bf16[4,64,512]{2,1,0:T(8,128)(2,1)}, u32[]{:S(2)}, u32[]{:S(2)}) collective-permute-start(bf16[4,64,512]{2,1,0:T(8,128)(2,1)} %get-tuple-element.254), channel_id=1, source_target_pairs={{0,4},{1,5},{2,3},{3,2},{4,0},{5,1},{6,7},{7,6},{8,12},{9,13},{10,... | collective-permute-start | bytes 786440 | tf_op jit(solution)/shard_map/ppermute | solution.py:626
  338.1 15.6 %collective-permute-start.48 = (bf16[4,64,1536]{2,1,0:T(8,128)(2,1)}, bf16[4,64,1536]{2,1,0:T(8,128)(2,1)S(1)}, u32[]{:S(2)}, u32[]{:S(2)}) collective-permute-start(bf16[4,64,1536]{2,1,0:T(8,128)(2,1)} %get-tuple-element.240), channel_id=1, source_target_pairs={{0,4},{1,5},{2,3},{3,2},{4,0},{5,1},{6,7},{7,6},{8,12},{9,13},{10,... | collective-permute-start | bytes 2359304 | tf_op jit(solution)/shard_map/ppermute | solution.py:626
  345.5 16.0 %collective-permute-start.57 = (bf16[64,512]{1,0:T(8,128)(2,1)S(1)}, bf16[64,512]{1,0:T(8,128)(2,1)S(1)}, u32[]{:S(2)}, u32[]{:S(2)}) collective-permute-start(bf16[64,512]{1,0:T(8,128)(2,1)S(1)} %get-tuple-element.259), channel_id=1, source_target_pairs={{0,8},{1,9},{2,10},{3,11},{4,12},{5,13},{6,14},{7,15},{8,0},{9,1},... | collective-permute-start | bytes 196616 | tf_op jit(solution)/shard_map/ppermute | solution.py:626
  351.4 12.4 %collective-permute-start.58 = (bf16[64,512]{1,0:T(8,128)(2,1)S(1)}, bf16[64,512]{1,0:T(8,128)(2,1)S(1)}, u32[]{:S(2)}, u32[]{:S(2)}) collective-permute-start(bf16[64,512]{1,0:T(8,128)(2,1)S(1)} %get-tuple-element.261), channel_id=1, source_target_pairs={{0,16},{1,17},{2,18},{3,19},{4,20},{5,21},{6,22},{7,23},{8,24},{9,... | collective-permute-start | bytes 196616 | tf_op jit(solution)/shard_map/ppermute | solution.py:626
  351.8 18.1 %collective-permute-start.59 = (bf16[64,512]{1,0:T(8,128)(2,1)S(1)}, bf16[64,512]{1,0:T(8,128)(2,1)S(1)}, u32[]{:S(2)}, u32[]{:S(2)}) collective-permute-start(bf16[64,512]{1,0:T(8,128)(2,1)S(1)} %get-tuple-element.260), channel_id=1, source_target_pairs={{0,24},{1,25},{2,26},{3,27},{4,28},{5,29},{6,30},{7,31},{8,16},{9,... | collective-permute-start | bytes 196616 | tf_op jit(solution)/shard_map/ppermute | solution.py:626
  354.1 18.1 %collective-permute-start.51 = (bf16[64,1536]{1,0:T(8,128)(2,1)S(1)}, bf16[64,1536]{1,0:T(8,128)(2,1)S(1)}, u32[]{:S(2)}, u32[]{:S(2)}) collective-permute-start(bf16[64,1536]{1,0:T(8,128)(2,1)S(1)} %get-tuple-element.252), channel_id=1, source_target_pairs={{0,8},{1,9},{2,10},{3,11},{4,12},{5,13},{6,14},{7,15},{8,0},{9,1},... | collective-permute-start | bytes 589832 | tf_op jit(solution)/shard_map/ppermute | solution.py:626
  361.5 16.1 %collective-permute-start.52 = (bf16[64,1536]{1,0:T(8,128)(2,1)S(1)}, bf16[64,1536]{1,0:T(8,128)(2,1)S(1)}, u32[]{:S(2)}, u32[]{:S(2)}) collective-permute-start(bf16[64,1536]{1,0:T(8,128)(2,1)S(1)} %get-tuple-element.251), channel_id=1, source_target_pairs={{0,16},{1,17},{2,18},{3,19},{4,20},{5,21},{6,22},{7,23},{8,24},{9,... | collective-permute-start | bytes 589832 | tf_op jit(solution)/shard_map/ppermute | solution.py:626
  361.5 16.0 %collective-permute-start.53 = (bf16[64,1536]{1,0:T(8,128)(2,1)S(1)}, bf16[64,1536]{1,0:T(8,128)(2,1)S(1)}, u32[]{:S(2)}, u32[]{:S(2)}) collective-permute-start(bf16[64,1536]{1,0:T(8,128)(2,1)S(1)} %get-tuple-element.250), channel_id=1, source_target_pairs={{0,24},{1,25},{2,26},{3,27},{4,28},{5,29},{6,30},{7,31},{8,16},{9,... | collective-permute-start | bytes 589832 | tf_op jit(solution)/shard_map/ppermute | solution.py:626
  (81 other events, 741.1 us)

commit v2 on v1

--- a/solution.py
+++ b/solution.py
@@ -32,7 +32,7 @@
     return pl.BlockSpec(shape, lambda t, me: (0,) * len(shape))
 
 
-def call(body, grid, ins, outs, shapes, scratch, flops, moved, name, room=32):
+def call(body, grid, ins, outs, shapes, scratch, flops, moved, name, room=32, heavy=False):
     return pl.pallas_call(
         body,
         grid_spec=pltpu.PrefetchScalarGridSpec(
@@ -46,7 +46,9 @@
         compiler_params=pltpu.CompilerParams(
             dimension_semantics=("arbitrary",) * len(grid), vmem_limit_bytes=room << 20
         ),
-        cost_estimate=pl.CostEstimate(flops=1, bytes_accessed=1, transcendentals=0),
+        cost_estimate=pl.CostEstimate(
+            flops=flops if heavy else 1, bytes_accessed=moved if heavy else 1, transcendentals=0
+        ),
         name=name,
     )
 
@@ -321,6 +323,7 @@
         4 * count * width * 2 * span,
         count * span * 12 + width * span * 4,
         "contract",
+        heavy=True,
     )(me, hidden, slope, out_low, middle, table, *pieces)
 
 
@@ -669,9 +672,13 @@
         self.received = swap(self.sent, self.size, Y_BIT, X_BIT)
         return self.kept
 
-    def second(self, *others):
+    def second(self, *others, joined=()):
         kept = after(self.kept, *others)
         total = (kept.astype(F32) + self.received.astype(F32)).astype(LOW)
+        for other in joined:
+            kept = after(other.kept, *others)
+            more = (kept.astype(F32) + other.received.astype(F32)).astype(LOW)
+            total = jnp.concatenate([total, more], axis=-1)
         self.kept = total[0]
         self.received = swap(total[1], self.size, X_BIT, Y_BIT)
         return self.kept
@@ -788,18 +795,18 @@
     second_three = along_second(held_three, size)
     far_three = [along_core(held_three, size)]
     middle, normed_two, turned_two = project_call(me, mixed, rows_in, table, pieces_two)
-    normed_two, first_three, second_three, far_own = lax.optimization_barrier(
-        (normed_two, first_three, second_three, *far_three)
+    hidden, slope = expand_call(me, normed_two, fc1_full, pieces_two)
+    hidden, first_three, second_three, far_own = lax.optimization_barrier(
+        (hidden, first_three, second_three, *far_three)
     )
     both_three = along_second(first_three, size)
     far_three = [far_own, along_core(second_three, size), along_core(first_three, size)]
     plane_three = [held_three, second_three, first_three]
-    hidden, slope = expand_call(me, normed_two, fc1_full, pieces_two)
-    hidden, both_three, *far_three = lax.optimization_barrier((hidden, both_three, *far_three))
+    fc2 = Scatter(out_turned, hidden, size, depth, "fc2_grad")
+    done = fc2.far(me)
+    both_three = after(both_three, done)
     far_three += [along_core(both_three, size)]
     pieces_three = plane_three + [both_three] + far_three
-    fc2 = Scatter(out_turned, after(hidden, far_three[3]), size, depth, "fc2_grad")
-    done = fc2.far(me)
     outputs, pre_low, fc1_sum = contract_call(
         me, after(hidden, done), slope, out_low, middle, table, pieces_three
     )
@@ -817,11 +824,9 @@
     done = fc1.near(done)
     done = fc2.third(done)
     qkv_low, qkv_sum = attend_back_call(me, qkv, after(mixed_grad, done), visible_rows)
-    landed = after(qkv_low, proj.received, *fc2.received)
-    qkv_out = Scatter(turned_one, landed, size, depth, "qkv_grad")
+    done = fc1.second(qkv_low, proj.received, *fc2.received, joined=[proj])
+    qkv_out = Scatter(turned_one, after(qkv_low, done), size, depth, "qkv_grad")
     done = qkv_out.far(me)
-    done = proj.second(done)
-    done = fc1.second(done)
     done = qkv_out.near(done)
     done = fc1.third(done)
     input_grad, vec_one = norm_back_call(
@@ -850,17 +855,16 @@
         ]
     )
     done = qkv_out.second(input_grad, *fc1.received)
-    done = proj.third(done)
     sums = after(sums, done)
     sums = sums + along_core(sums, size)
     done = qkv_out.third(sums)
-    fc1_grad = fc1.last(done)
-    fc2_grad = fc2.last(done)
-    proj_grad = proj.last(done)
     sums = after(sums, done)
     for bits in (X_BIT, Y_BIT):
         sums = sums + swap(sums, size, bits)
-    sums = after(sums, *qkv_out.received)
+    sums = after(sums, qkv_out.received[0])
+    fc2_grad = fc2.last(sums)
+    fc1_grad = fc1.last(sums)
+    fc1_grad, proj_grad = fc1_grad[:, : 4 * half], fc1_grad[:, 4 * half :]
     sums = sum(along_depth(sums, size, range(1, depth)))
     qkv_grad = qkv_out.last()
     mine = lax.dynamic_slice_in_dim(sums[:8], dp_rank * rows, rows, 1)

time: 393 us -> 394 us (level)
  starting transfers between devices: 88.4 us -> 67 us
  waiting for transfers between devices: 92.9 us -> 114 us
    ppermute x60 -> x56, starting transfers between devices: 88.4 us -> 67 us  [swap(): lax.ppermute(value, AXES, [(i, i ^ (other if i & CORE_BIT else bits)) for...]
    ppermute x60 -> x56, waiting for transfers between devices: 92.9 us -> 114 us  [swap(): lax.ppermute(value, AXES, [(i, i ^ (other if i & CORE_BIT else bits)) for...]
    unnamed x144 -> x98, local copies, waits for them, and re-layouts: 22.1 us -> 20 us
    convert_element_type x4 -> x3, other arithmetic: 8.04 us -> 6.88 us  [second(): total = (kept.astype(F32) + self.received.astype(F32)).astype(LOW)]
  transfers between devices with their start and end apart: 60 -> 56, of which waited for: 17 -> 21; matrix products, arithmetic and copies ran while one was open for 8% -> 7% of each run, Pallas kernels for 36% -> 37%
where the time goes in v2:
time: 394 us; the launch traced here: 393 us
  Pallas kernels  154 us (39%)
  waiting for transfers between devices  114 us (29%)
  starting transfers between devices  67 us (17%)
  local copies, waits for them, and re-layouts  35.8 us (9%)
  other arithmetic  21.3 us (5%)
    ppermute x56, waiting for transfers between devices, swap(): lax.ppermute(value, AXES, [(i, i ^ (other if i & CORE_BIT else bits)) for...  114 us
    ppermute x56, starting transfers between devices, swap(): lax.ppermute(value, AXES, [(i, i ^ (other if i & CORE_BIT else bits)) for...  67 us
    pallas_call x8, Pallas kernels, weight_grad_call(): call(body, (steps,), ins, outs, shapes, scratch, 2 * count * width * span...  36.2 us
    pallas_call x2, Pallas kernels, norm_back_call(): call(body, (4,), [pl.BlockSpec((count, chunk), lambda t, me: (0, t)), who...  29.3 us
    pallas_call x1, Pallas kernels, attend_back_call(): call(body, (images, 2), [pl.BlockSpec((seq, 3 * half), lambda i, y, me: (...  21.1 us
    unnamed x98, local copies, waits for them, and re-layouts  20 us
    pallas_call x1, Pallas kernels, contract_call(): call(body, (8,), [part, part, whole(count, width), whole(count, width), w...  17.9 us
    pallas_call x1, Pallas kernels, expand_call(): call(body, (8,), [whole(count, width), pl.BlockSpec((1, chunk), lambda t,...  16.3 us
  transfers between devices with their start and end apart: 56, of which 21 were waited for; matrix products, arithmetic and copies ran while one was open for 7% of the time, Pallas kernels for 37%

profile of v2, /device:TPU:0, one launch (start us, length us, event | category | flops | bytes accessed | tf_op | source)
XLA Modules:
  0.0 393.4 jit_solution(6665910170258394108)
XLA Ops:
  3.5 3.1 collective-permute-start
  6.6 2.6 collective-permute-start.1
  10.3 3.1 fusion.5
  13.4 2.2 collective-permute-done
  15.7 9.1 %collective-permute-done.1 = bf16[64,1664]{1,0:T(8,128)(2,1)S(1)} collective-permute-done((bf16[64,1664]{1,0:T(8,128)(2,1)S(1)}, bf16[64,1664]{1,0:T(8,128)(2,1)S(1)}, u32[]{:S(2)}, u32[]{:S(2)}) %collective-permute-start.1) | collective-permute-done | bytes 213024 | tf_op jit(solution)/shard_map/ppermute | solution.py:629
  27.9 3.8 collective-permute-start.6
  32.7 14.3 %collective-permute-done.6 = bf16[64,2560]{1,0:T(8,128)(2,1)S(1)} collective-permute-done((bf16[64,2560]{1,0:T(8,128)(2,1)S(1)}, bf16[64,2560]{1,0:T(8,128)(2,1)S(1)}, u32[]{:S(2)}, u32[]{:S(2)}) %collective-permute-start.6) | collective-permute-done | bytes 327712 | tf_op jit(solution)/shard_map/ppermute | solution.py:629
  47.0 2.5 collective-permute-done.7
  51.0 2.5 collective-permute-start.9
  54.2 8.8 %collective-permute-done.9 = bf16[64,2560]{1,0:T(8,128)(2,1)S(1)} collective-permute-done((bf16[64,2560]{1,0:T(8,128)(2,1)S(1)}, bf16[64,2560]{1,0:T(8,128)(2,1)S(1)}, u32[]{:S(2)}, u32[]{:S(2)}) %collective-permute-start.9) | collective-permute-done | bytes 327712 | tf_op jit(solution)/shard_map/ppermute | solution.py:629
  65.9 3.7 collective-permute-done.10.refs_5_
  69.6 6.1 %collective-permute-start.15 = (bf16[64,2048]{1,0:T(8,128)(2,1)}, bf16[64,2048]{1,0:T(8,128)(2,1)}, u32[]{:S(2)}, u32[]{:S(2)}) collective-permute-start(bf16[64,2048]{1,0:T(8,128)(2,1)} %convert_bitcast_fusion), channel_id=1, source_target_pairs={{0,8},{1,9},{2,10},{3,11},{4,12},{5,13},{6,14},{7,15},{8,0},{9,1},... | collective-permute-start | bytes 786440 | tf_op jit(solution)/shard_map/ppermute | solution.py:629
  77.9 13.1 %qkv.1 = (bf16[640,1024]{1,0:T(8,128)(2,1)}, bf16[1024,640]{1,0:T(8,128)(2,1)}, bf16[640,3072]{1,0:T(8,128)(2,1)}, f32[16,1024]{1,0:T(8,128)}) custom-call(s32[1]{0:T(128)} %bitcast.me_ref, f32[640,1024]{1,0:T(8,128)} %bitcast.110, bf16[4,64,1664]{2,1,0:T(8,128)(2,1)} %copy-done.30, bf16[4,64,1664]{2,1,0:T(8,128)(2,1)} %copy-done.32, ...), custom_call_target="tpu_custom_call" | custom-call | flops 1 | bytes 1 | tf_op jit(solution)/shard_map/qkv/pallas_call | solution.py:132
  91.0 3.8 collective-permute-done.13.refs_2_
  95.9 2.5 collective-permute-start.21
  102.2 11.7 %attend.1.mixed_ref.right_ref = bf16[640,1024]{1,0:T(8,128)(2,1)S(1)} custom-call(s32[1]{0:T(128)} %bitcast.me_ref, bf16[640,3072]{1,0:T(8,128)(2,1)S(1)} %copy-done.14, s32[2,1,320]{2,1,0:T(1,128)S(1)} %broadcast_in_dim.10.seen_ref), custom_call_target="tpu_custom_call" | custom-call | flops 1 | bytes 1 | tf_op jit(solution)/shard_map/attend/pallas_call | solution.py:190
  119.2 2.4 copy.56.turn_ref
  124.7 4.9 %project.1 = (f32[640,1024]{1,0:T(8,128)S(1)}, bf16[640,1024]{1,0:T(8,128)(2,1)S(1)}, bf16[1024,640]{1,0:T(8,128)(2,1)S(1)}) custom-call(s32[1]{0:T(128)} %bitcast.me_ref, bf16[640,1024]{1,0:T(8,128)(2,1)S(1)} %copy-done.12, f32[640,1024]{1,0:T(8,128)S(1)} %bitcast.112, f32[16,1024]{1,0:T(8,128)S(1)} %copy-done.27, ...), custom_call_target="tpu_custom_call" | custom-call | flops 1 | bytes 1 | tf_op jit(solution)/shard_map/project/pallas_call | solution.py:227
  133.2 16.3 %expand.1 = (bf16[640,4096]{1,0:T(8,128)(2,1)}, bf16[640,4096]{1,0:T(8,128)(2,1)}) custom-call(s32[1]{0:T(128)} %bitcast.me_ref, bf16[640,1024]{1,0:T(8,128)(2,1)} %copy-done.26, f32[1,4096]{1,0:T(1,128)} %reshape.119.bias_ref, bf16[4,64,2560]{2,1,0:T(8,128)(2,1)} %copy-done.4, bf16[4,64,2560]{2,1,0:T(8,128)(2,1)} %collective-permute-done.14.refs_1_, ...), custom_call_target="tpu_custom_call" | custom-call | flops 1 | bytes 1 | tf_op jit(solution)/shard_map/expand/pallas_call | solution.py:270
  149.6 2.5 copy-done.9
  152.1 5.9 %fc2_grad_far.1 = bf16[2,2,4,64,2048]{4,3,2,1,0:T(8,128)(2,1)} custom-call(s32[1]{0:T(128)} %bitcast.me_ref, bf16[1024,640]{1,0:T(8,128)(2,1)S(1)} %copy-done.16, bf16[640,4096]{1,0:T(8,128)(2,1)S(1)} %copy-done.9), custom_call_target="tpu_custom_call" | custom-call | flops 1 | bytes 1 | tf_op jit(solution)/shard_map/fc2_grad_far/pallas_call | solution.py:614
  160.3 12.9 %collective-permute-done.26.refs_3_ = bf16[4,64,2048]{2,1,0:T(8,128)(2,1)S(1)} collective-permute-done((bf16[4,64,2048]{2,1,0:T(8,128)(2,1)}, bf16[4,64,2048]{2,1,0:T(8,128)(2,1)S(1)}, u32[]{:S(2)}, u32[]{:S(2)}) %collective-permute-start.26) | collective-permute-done | bytes 1048608 | tf_op jit(solution)/shard_map/ppermute | solution.py:629
  173.2 2.6 collective-permute-done.29.refs_7_
  175.9 17.9 %contract.1 = (f32[640,1024]{1,0:T(8,128)}, bf16[640,4096]{1,0:T(8,128)(2,1)S(1)}, f32[1,4096]{1,0:T(1,128)S(1)}) custom-call(s32[1]{0:T(128)} %bitcast.me_ref, bf16[640,4096]{1,0:T(8,128)(2,1)S(1)} %copy-done.10, bf16[640,4096]{1,0:T(8,128)(2,1)} %get-tuple-element.142.slope_ref, bf16[640,1024]{1,0:T(8,128)(2,1)S(1)} %copy-done.18, ...), custom_call_target="tpu_custom_call" | custom-call | flops 10737418240 | bytes 24117248 | tf_op jit(solution)/shard_map/contract/pallas_call | solution.py:312
  193.9 5.9 %fc1_grad_far.1 = bf16[2,2,4,64,2048]{4,3,2,1,0:T(8,128)(2,1)} custom-call(s32[1]{0:T(128)} %bitcast.me_ref, bf16[1024,640]{1,0:T(8,128)(2,1)S(1)} %copy-done.21, bf16[640,4096]{1,0:T(8,128)(2,1)S(1)} %get-tuple-element.162.right_ref.low_ref), custom_call_target="tpu_custom_call" | custom-call | flops 1 | bytes 1 | tf_op jit(solution)/shard_map/fc1_grad_far/pallas_call | solution.py:614
  200.1 6.2 %fc2_grad_near.1 = (bf16[2,4,64,2048]{3,2,1,0:T(8,128)(2,1)S(1)}, bf16[2,4,64,2048]{3,2,1,0:T(8,128)(2,1)S(1)}) custom-call(s32[1]{0:T(128)} %bitcast.me_ref, bf16[1024,640]{1,0:T(8,128)(2,1)S(1)} %copy-done.16, bf16[640,4096]{1,0:T(8,128)(2,1)S(1)} %bitcast.114, bf16[2,2,4,64,2048]{4,3,2,1,0:T(8,128)(2,1)} %collective-permute-done.30.refs_0_), custom_call_target="tpu_custom_call" | custom-call | flops 1 | bytes 1 | tf_op jit(solution)/shard_map/fc2_grad_near/pallas_call | solution.py:614
  208.1 14.2 %norm_two_back.1 = (f32[640,1024]{1,0:T(8,128)S(1)}, f32[8,1024]{1,0:T(8,128)S(1)}, bf16[640,1024]{1,0:T(8,128)(2,1)S(1)}, bf16[1024,640]{1,0:T(8,128)(2,1)S(1)}) custom-call(s32[1]{0:T(128)} %bitcast.me_ref, bf16[640,4096]{1,0:T(8,128)(2,1)} %copy-done.2, f32[640,1024]{1,0:T(8,128)S(1)} %copy-done.24, f32[640,1024]{1,0:T(8,128)S(1)} %bitcast.115, ...), custom_call_target="tpu_custom_call" | custom-call | flops 1 | bytes 1 | tf_op jit(solution)/shard_map/norm_two_back/pallas_call | solution.py:397
  223.9 3.3 mixed_back.1.grad_ref
  228.9 3.6 collective-permute-done.31
  232.5 2.5 add_convert_fusion.1
  237.8 5.8 %fc1_grad_near.1 = (bf16[2,4,64,2048]{3,2,1,0:T(8,128)(2,1)S(1)}, bf16[2,4,64,2048]{3,2,1,0:T(8,128)(2,1)}) custom-call(s32[1]{0:T(128)} %bitcast.me_ref, bf16[1024,640]{1,0:T(8,128)(2,1)S(1)} %copy-done.21, bf16[640,4096]{1,0:T(8,128)(2,1)S(1)} %bitcast.109, bf16[2,2,4,64,2048]{4,3,2,1,0:T(8,128)(2,1)} %collective-permute-done.33.refs_0_), custom_call_target="tpu_custom_call" | custom-call | flops 1 | bytes 1 | tf_op jit(solution)/shard_map/fc1_grad_near/pallas_call | solution.py:614
  245.7 6.1 %collective-permute-done.34 = bf16[4,64,2048]{2,1,0:T(8,128)(2,1)S(1)} collective-permute-done((bf16[4,64,2048]{2,1,0:T(8,128)(2,1)S(1)}, bf16[4,64,2048]{2,1,0:T(8,128)(2,1)S(1)}, u32[]{:S(2)}, u32[]{:S(2)}) %collective-permute-start.34) | collective-permute-done | bytes 1048608 | tf_op jit(solution)/shard_map/ppermute | solution.py:629
  253.2 6.3 %collective-permute-start.36 = (bf16[64,2048]{1,0:T(8,128)(2,1)}, bf16[64,2048]{1,0:T(8,128)(2,1)}, u32[]{:S(2)}, u32[]{:S(2)}) collective-permute-start(bf16[64,2048]{1,0:T(8,128)(2,1)} %get-tuple-element.234), channel_id=1, source_target_pairs={{0,8},{1,9},{2,10},{3,11},{4,12},{5,13},{6,14},{7,15},{8,0},{9,1},... | collective-permute-start | bytes 786440 | tf_op jit(solution)/shard_map/ppermute | solution.py:629
  259.5 2.4 collective-permute-start.38
  265.8 21.1 %attend_back.1 = (bf16[640,3072]{1,0:T(8,128)(2,1)S(1)}, f32[2,2,1,1536]{3,2,1,0:T(1,128)S(1)}) custom-call(s32[1]{0:T(128)} %bitcast.me_ref, bf16[640,3072]{1,0:T(8,128)(2,1)S(1)} %copy-done.15, bf16[640,1024]{1,0:T(8,128)(2,1)S(1)} %mixed_back.1.grad_ref, s32[2,320,1]{2,1,0:T(8,128)S(1)} %copy-done.25), custom_call_target="tpu_custom_call" | custom-call | flops 1 | bytes 1 | tf_op jit(solution)/shard_map/attend_back/pallas_call | solution.py:488
  288.6 2.4 add_convert_fusion
  292.3 4.2 %qkv_grad_far.1 = bf16[2,2,4,64,1536]{4,3,2,1,0:T(8,128)(2,1)S(1)} custom-call(s32[1]{0:T(128)} %bitcast.me_ref, bf16[1024,640]{1,0:T(8,128)(2,1)S(1)} %copy-done.19, bf16[640,3072]{1,0:T(8,128)(2,1)S(1)} %get-tuple-element.177.right_ref.low_ref), custom_call_target="tpu_custom_call" | custom-call | flops 1 | bytes 1 | tf_op jit(solution)/shard_map/qkv_grad_far/pallas_call | solution.py:614
  296.9 5.4 %collective-permute-done.40.refs_0_ = bf16[2,2,4,64,1536]{4,3,2,1,0:T(8,128)(2,1)S(1)} collective-permute-done((bf16[2,2,4,64,1536]{4,3,2,1,0:T(8,128)(2,1)S(1)}, bf16[2,2,4,64,1536]{4,3,2,1,0:T(8,128)(2,1)S(1)}, u32[]{:S(2)}, u32[]{:S(2)}) %collective-permute-start.40) | collective-permute-done | bytes 3145760 | tf_op jit(solution)/shard_map/ppermute | solution.py:629
  302.3 4.9 %qkv_grad_near.1 = (bf16[2,4,64,1536]{3,2,1,0:T(8,128)(2,1)S(1)}, bf16[2,4,64,1536]{3,2,1,0:T(8,128)(2,1)S(1)}) custom-call(s32[1]{0:T(128)} %bitcast.me_ref, bf16[1024,640]{1,0:T(8,128)(2,1)S(1)} %copy-done.19, bf16[640,3072]{1,0:T(8,128)(2,1)S(1)} %get-tuple-element.177.right_ref.low_ref, bf16[2,2,4,64,1536]{4,3,2,1,0:T(8,128)(2,1)S(1)} %collective-permute-done.40.refs_0_), custom_call_target="tpu_custom_call" | custom-call | flops 1 | bytes 1 | tf_op jit(solution)/shard_map/qkv_grad_near/pallas_call | solution.py:614
  307.5 11.1 %collective-permute-done.41 = bf16[4,64,2560]{2,1,0:T(8,128)(2,1)S(1)} collective-permute-done((bf16[4,64,2560]{2,1,0:T(8,128)(2,1)S(1)}, bf16[4,64,2560]{2,1,0:T(8,128)(2,1)S(1)}, u32[]{:S(2)}, u32[]{:S(2)}) %collective-permute-start.41) | collective-permute-done | bytes 1310752 | tf_op jit(solution)/shard_map/ppermute | solution.py:629
  321.9 2.4 collective-permute-start.44
  324.3 15.2 %norm_one_back.1 = (f32[640,1024]{1,0:T(8,128)}, f32[8,1024]{1,0:T(8,128)}) custom-call(s32[1]{0:T(128)} %bitcast.me_ref, bf16[640,3072]{1,0:T(8,128)(2,1)} %copy-done.3, f32[640,1024]{1,0:T(8,128)} %bitcast.111, f32[640,1024]{1,0:T(8,128)} %copy-done.22, f32[16,1024]{1,0:T(8,128)} %get-tuple-element.119.table_ref, bf16[4,64,1664]{2,1,0:T(8,128)(2,1)} %copy-done.30, ...), custom_call_target="tpu_custom_call" | custom-call | flops 1 | bytes 1 | tf_op jit(solution)/shard_map/norm_one_back/pallas_call | solution.py:397
  339.4 7.1 %collective-permute-done.43 = bf16[64,2560]{1,0:T(8,128)(2,1)} collective-permute-done((bf16[64,2560]{1,0:T(8,128)(2,1)S(1)}, bf16[64,2560]{1,0:T(8,128)(2,1)}, u32[]{:S(2)}, u32[]{:S(2)}) %collective-permute-start.43) | collective-permute-done | bytes 327712 | tf_op jit(solution)/shard_map/ppermute | solution.py:629
  353.2 8.6 %collective-permute-done.47 = bf16[4,64,1536]{2,1,0:T(8,128)(2,1)S(1)} collective-permute-done((bf16[4,64,1536]{2,1,0:T(8,128)(2,1)}, bf16[4,64,1536]{2,1,0:T(8,128)(2,1)S(1)}, u32[]{:S(2)}, u32[]{:S(2)}) %collective-permute-start.47) | collective-permute-done | bytes 786464 | tf_op jit(solution)/shard_map/ppermute | solution.py:629
  362.0 5.4 %collective-permute-start.50 = (bf16[64,1536]{1,0:T(8,128)(2,1)S(1)}, bf16[64,1536]{1,0:T(8,128)(2,1)S(1)}, u32[]{:S(2)}, u32[]{:S(2)}) collective-permute-start(bf16[64,1536]{1,0:T(8,128)(2,1)S(1)} %get-tuple-element.238), channel_id=1, source_target_pairs={{0,8},{1,9},{2,10},{3,11},{4,12},{5,13},{6,14},{7,15},{8,0},{9,1},... | collective-permute-start | bytes 589832 | tf_op jit(solution)/shard_map/ppermute | solution.py:629
  367.5 4.2 %collective-permute-done.48 = f32[12,1024]{1,0:T(8,128)S(1)} collective-permute-done((f32[12,1024]{1,0:T(8,128)S(1)}, f32[12,1024]{1,0:T(8,128)S(1)}, u32[]{:S(2)}, u32[]{:S(2)}) %collective-permute-start.48) | collective-permute-done | bytes 49184 | tf_op jit(solution)/shard_map/ppermute | solution.py:629
  377.6 2.9 collective-permute-start.53
  383.9 3.7 collective-permute-done.54
  (240 shorter events, 78.9 us)
Async XLA Ops:
  3.5 12.2 %collective-permute-start = (bf16[64,1664]{1,0:T(8,128)(2,1)S(1)}, bf16[64,1664]{1,0:T(8,128)(2,1)S(1)}, u32[]{:S(2)}, u32[]{:S(2)}) collective-permute-start(bf16[64,1664]{1,0:T(8,128)(2,1)S(1)} %pad_maximum_fusion.5), channel_id=1, source_target_pairs={{0,8},{1,9},{2,10},{3,11},{4,12},{5,13},{6,14},{7,15},{8,0},{9,1},... | collective-permute-start | bytes 638984 | tf_op jit(solution)/shard_map/ppermute | solution.py:629
  6.6 18.2 %collective-permute-start.1 = (bf16[64,1664]{1,0:T(8,128)(2,1)S(1)}, bf16[64,1664]{1,0:T(8,128)(2,1)S(1)}, u32[]{:S(2)}, u32[]{:S(2)}) collective-permute-start(bf16[64,1664]{1,0:T(8,128)(2,1)S(1)} %pad_maximum_fusion.5), channel_id=1, source_target_pairs={{0,16},{1,17},{2,18},{3,19},{4,20},{5,21},{6,22},{7,23},{8,24},{9,... | collective-permute-start | bytes 638984 | tf_op jit(solution)/shard_map/ppermute | solution.py:629
  9.2 15.6 %collective-permute-start.2 = (bf16[64,1664]{1,0:T(8,128)(2,1)S(1)}, bf16[64,1664]{1,0:T(8,128)(2,1)S(1)}, u32[]{:S(2)}, u32[]{:S(2)}) collective-permute-start(bf16[64,1664]{1,0:T(8,128)(2,1)S(1)} %pad_maximum_fusion.5), channel_id=1, source_target_pairs={{0,24},{1,25},{2,26},{3,27},{4,28},{5,29},{6,30},{7,31},{8,16},{9,... | collective-permute-start | bytes 638984 | tf_op jit(solution)/shard_map/ppermute | solution.py:629
  24.8 24.6 %collective-permute-start.3 = (bf16[4,64,1664]{2,1,0:T(8,128)(2,1)S(1)}, bf16[4,64,1664]{2,1,0:T(8,128)(2,1)S(1)}, u32[]{:S(2)}, u32[]{:S(2)}) collective-permute-start(bf16[4,64,1664]{2,1,0:T(8,128)(2,1)S(1)} %pad_maximum_fusion.3.refs_0_), channel_id=1, source_target_pairs={{0,1},{1,0},{2,6},{3,7},{4,5},{5,4},{6,2},{7,3},{8,9},{9,8},{10,14... | collective-permute-start | bytes 2555912 | tf_op jit(solution)/shard_map/ppermute | solution.py:629
  26.4 23.1 %collective-permute-start.4 = (bf16[4,64,1664]{2,1,0:T(8,128)(2,1)S(1)}, bf16[4,64,1664]{2,1,0:T(8,128)(2,1)S(1)}, u32[]{:S(2)}, u32[]{:S(2)}) collective-permute-start(bf16[4,64,1664]{2,1,0:T(8,128)(2,1)S(1)} %pad_maximum_fusion.3.refs_0_), channel_id=1, source_target_pairs={{0,4},{1,5},{2,3},{3,2},{4,0},{5,1},{6,7},{7,6},{8,12},{9,13},{10,... | collective-permute-start | bytes 2555912 | tf_op jit(solution)/shard_map/ppermute | solution.py:629
  27.9 21.6 %collective-permute-start.5 = (bf16[4,64,1664]{2,1,0:T(8,128)(2,1)S(1)}, bf16[4,64,1664]{2,1,0:T(8,128)(2,1)S(1)}, u32[]{:S(2)}, u32[]{:S(2)}) collective-permute-start(bf16[4,64,1664]{2,1,0:T(8,128)(2,1)S(1)} %pad_maximum_fusion.3.refs_0_), channel_id=1, source_target_pairs={{0,2},{1,3},{2,0},{3,1},{4,6},{5,7},{6,4},{7,5},{8,10},{9,11},{10,... | collective-permute-start | bytes 2555912 | tf_op jit(solution)/shard_map/ppermute | solution.py:629
  27.9 19.0 %collective-permute-start.6 = (bf16[64,2560]{1,0:T(8,128)(2,1)S(1)}, bf16[64,2560]{1,0:T(8,128)(2,1)S(1)}, u32[]{:S(2)}, u32[]{:S(2)}) collective-permute-start(bf16[64,2560]{1,0:T(8,128)(2,1)S(1)} %pad_maximum_fusion.4), channel_id=1, source_target_pairs={{0,8},{1,9},{2,10},{3,11},{4,12},{5,13},{6,14},{7,15},{8,0},{9,1},... | collective-permute-start | bytes 983048 | tf_op jit(solution)/shard_map/ppermute | solution.py:629
  31.7 17.8 %collective-permute-start.7 = (bf16[64,2560]{1,0:T(8,128)(2,1)S(1)}, bf16[64,2560]{1,0:T(8,128)(2,1)S(1)}, u32[]{:S(2)}, u32[]{:S(2)}) collective-permute-start(bf16[64,2560]{1,0:T(8,128)(2,1)S(1)} %pad_maximum_fusion.4), channel_id=1, source_target_pairs={{0,16},{1,17},{2,18},{3,19},{4,20},{5,21},{6,22},{7,23},{8,24},{9,... | collective-permute-start | bytes 983048 | tf_op jit(solution)/shard_map/ppermute | solution.py:629
  50.5 12.7 %collective-permute-start.8 = (bf16[4,64,1664]{2,1,0:T(8,128)(2,1)S(1)}, bf16[4,64,1664]{2,1,0:T(8,128)(2,1)S(1)}, u32[]{:S(2)}, u32[]{:S(2)}) collective-permute-start(bf16[4,64,1664]{2,1,0:T(8,128)(2,1)S(1)} %collective-permute-done.3.refs_2_), channel_id=1, source_target_pairs={{0,4},{1,5},{2,3},{3,2},{4,0},{5,1},{6,7},{7,6},{8,12},{9,13},{10,... | collective-permute-start | bytes 2555912 | tf_op jit(solution)/shard_map/ppermute | solution.py:629
  51.0 14.8 %collective-permute-start.11 = (bf16[4,64,1664]{2,1,0:T(8,128)(2,1)S(1)}, bf16[4,64,1664]{2,1,0:T(8,128)(2,1)S(1)}, u32[]{:S(2)}, u32[]{:S(2)}) collective-permute-start(bf16[4,64,1664]{2,1,0:T(8,128)(2,1)S(1)} %collective-permute-done.3.refs_2_), channel_id=1, source_target_pairs={{0,2},{1,3},{2,0},{3,1},{4,6},{5,7},{6,4},{7,5},{8,10},{9,11},{10,... | collective-permute-start | bytes 2555912 | tf_op jit(solution)/shard_map/ppermute | solution.py:629
  51.0 12.0 %collective-permute-start.9 = (bf16[64,2560]{1,0:T(8,128)(2,1)S(1)}, bf16[64,2560]{1,0:T(8,128)(2,1)S(1)}, u32[]{:S(2)}, u32[]{:S(2)}) collective-permute-start(bf16[64,2560]{1,0:T(8,128)(2,1)S(1)} %pad_maximum_fusion.4), channel_id=1, source_target_pairs={{0,24},{1,25},{2,26},{3,27},{4,28},{5,29},{6,30},{7,31},{8,16},{9,... | collective-permute-start | bytes 983048 | tf_op jit(solution)/shard_map/ppermute | solution.py:629
  63.4 31.4 %collective-permute-start.13 = (bf16[4,64,2560]{2,1,0:T(8,128)(2,1)S(1)}, bf16[4,64,2560]{2,1,0:T(8,128)(2,1)S(1)}, u32[]{:S(2)}, u32[]{:S(2)}) collective-permute-start(bf16[4,64,2560]{2,1,0:T(8,128)(2,1)S(1)} %pad_maximum_fusion.1.refs_0_), channel_id=1, source_target_pairs={{0,1},{1,0},{2,6},{3,7},{4,5},{5,4},{6,2},{7,3},{8,9},{9,8},{10,14... | collective-permute-start | bytes 3932168 | tf_op jit(solution)/shard_map/ppermute | solution.py:629
  63.9 30.9 %collective-permute-start.14 = (bf16[4,64,2560]{2,1,0:T(8,128)(2,1)S(1)}, bf16[4,64,2560]{2,1,0:T(8,128)(2,1)}, u32[]{:S(2)}, u32[]{:S(2)}) collective-permute-start(bf16[4,64,2560]{2,1,0:T(8,128)(2,1)S(1)} %pad_maximum_fusion.1.refs_0_), channel_id=1, source_target_pairs={{0,4},{1,5},{2,3},{3,2},{4,0},{5,1},{6,7},{7,6},{8,12},{9,13},{10,... | collective-permute-start | bytes 3932168 | tf_op jit(solution)/shard_map/ppermute | solution.py:629
  65.3 29.5 %collective-permute-start.17 = (bf16[4,64,2560]{2,1,0:T(8,128)(2,1)S(1)}, bf16[4,64,2560]{2,1,0:T(8,128)(2,1)}, u32[]{:S(2)}, u32[]{:S(2)}) collective-permute-start(bf16[4,64,2560]{2,1,0:T(8,128)(2,1)S(1)} %pad_maximum_fusion.1.refs_0_), channel_id=1, source_target_pairs={{0,2},{1,3},{2,0},{3,1},{4,6},{5,7},{6,4},{7,5},{8,10},{9,11},{10,... | collective-permute-start | bytes 3932168 | tf_op jit(solution)/shard_map/ppermute | solution.py:629
  65.8 9.8 %collective-permute-start.12 = (bf16[4,64,1664]{2,1,0:T(8,128)(2,1)S(1)}, bf16[4,64,1664]{2,1,0:T(8,128)(2,1)S(1)}, u32[]{:S(2)}, u32[]{:S(2)}) collective-permute-start(bf16[4,64,1664]{2,1,0:T(8,128)(2,1)S(1)} %collective-permute-done.8.refs_3_), channel_id=1, source_target_pairs={{0,2},{1,3},{2,0},{3,1},{4,6},{5,7},{6,4},{7,5},{8,10},{9,11},{10,... | collective-permute-start | bytes 2555912 | tf_op jit(solution)/shard_map/ppermute | solution.py:629
  69.6 21.4 %collective-permute-start.15 = (bf16[64,2048]{1,0:T(8,128)(2,1)}, bf16[64,2048]{1,0:T(8,128)(2,1)}, u32[]{:S(2)}, u32[]{:S(2)}) collective-permute-start(bf16[64,2048]{1,0:T(8,128)(2,1)} %convert_bitcast_fusion), channel_id=1, source_target_pairs={{0,8},{1,9},{2,10},{3,11},{4,12},{5,13},{6,14},{7,15},{8,0},{9,1},... | collective-permute-start | bytes 786440 | tf_op jit(solution)/shard_map/ppermute | solution.py:629
  75.7 15.3 %collective-permute-start.16 = (bf16[64,2048]{1,0:T(8,128)(2,1)}, bf16[64,2048]{1,0:T(8,128)(2,1)}, u32[]{:S(2)}, u32[]{:S(2)}) collective-permute-start(bf16[64,2048]{1,0:T(8,128)(2,1)} %convert_bitcast_fusion), channel_id=1, source_target_pairs={{0,16},{1,17},{2,18},{3,19},{4,20},{5,21},{6,22},{7,23},{8,24},{9,... | collective-permute-start | bytes 786440 | tf_op jit(solution)/shard_map/ppermute | solution.py:629
  94.8 20.1 %collective-permute-start.18 = (bf16[4,64,2560]{2,1,0:T(8,128)(2,1)S(1)}, bf16[4,64,2560]{2,1,0:T(8,128)(2,1)}, u32[]{:S(2)}, u32[]{:S(2)}) collective-permute-start(bf16[4,64,2560]{2,1,0:T(8,128)(2,1)S(1)} %collective-permute-done.13.refs_2_), channel_id=1, source_target_pairs={{0,4},{1,5},{2,3},{3,2},{4,0},{5,1},{6,7},{7,6},{8,12},{9,13},{10,... | collective-permute-start | bytes 3932168 | tf_op jit(solution)/shard_map/ppermute | solution.py:629
  95.4 19.5 %collective-permute-start.19 = (bf16[4,64,2560]{2,1,0:T(8,128)(2,1)}, bf16[4,64,2560]{2,1,0:T(8,128)(2,1)}, u32[]{:S(2)}, u32[]{:S(2)}) collective-permute-start(bf16[4,64,2560]{2,1,0:T(8,128)(2,1)} %collective-permute-done.14.refs_1_), channel_id=1, source_target_pairs={{0,2},{1,3},{2,0},{3,1},{4,6},{5,7},{6,4},{7,5},{8,10},{9,11},{10,... | collective-permute-start | bytes 3932168 | tf_op jit(solution)/shard_map/ppermute | solution.py:629
  95.4 19.5 %collective-permute-start.20 = (bf16[4,64,2560]{2,1,0:T(8,128)(2,1)S(1)}, bf16[4,64,2560]{2,1,0:T(8,128)(2,1)}, u32[]{:S(2)}, u32[]{:S(2)}) collective-permute-start(bf16[4,64,2560]{2,1,0:T(8,128)(2,1)S(1)} %collective-permute-done.13.refs_2_), channel_id=1, source_target_pairs={{0,2},{1,3},{2,0},{3,1},{4,6},{5,7},{6,4},{7,5},{8,10},{9,11},{10,... | collective-permute-start | bytes 3932168 | tf_op jit(solution)/shard_map/ppermute | solution.py:629
  95.9 19.1 %collective-permute-start.21 = (bf16[64,2048]{1,0:T(8,128)(2,1)}, bf16[64,2048]{1,0:T(8,128)(2,1)S(1)}, u32[]{:S(2)}, u32[]{:S(2)}) collective-permute-start(bf16[64,2048]{1,0:T(8,128)(2,1)} %convert_bitcast_fusion), channel_id=1, source_target_pairs={{0,24},{1,25},{2,26},{3,27},{4,28},{5,29},{6,30},{7,31},{8,16},{9,... | collective-permute-start | bytes 786440 | tf_op jit(solution)/shard_map/ppermute | solution.py:629
  117.2 32.3 %collective-permute-start.23 = (bf16[4,64,2048]{2,1,0:T(8,128)(2,1)}, bf16[4,64,2048]{2,1,0:T(8,128)(2,1)}, u32[]{:S(2)}, u32[]{:S(2)}) collective-permute-start(bf16[4,64,2048]{2,1,0:T(8,128)(2,1)} %pad_maximum_fusion.2.refs_0_), channel_id=1, source_target_pairs={{0,1},{1,0},{2,6},{3,7},{4,5},{5,4},{6,2},{7,3},{8,9},{9,8},{10,14... | collective-permute-start | bytes 3145736 | tf_op jit(solution)/shard_map/ppermute | solution.py:629
  117.9 31.7 %collective-permute-start.24 = (bf16[4,64,2048]{2,1,0:T(8,128)(2,1)}, bf16[4,64,2048]{2,1,0:T(8,128)(2,1)}, u32[]{:S(2)}, u32[]{:S(2)}) collective-permute-start(bf16[4,64,2048]{2,1,0:T(8,128)(2,1)} %pad_maximum_fusion.2.refs_0_), channel_id=1, source_target_pairs={{0,4},{1,5},{2,3},{3,2},{4,0},{5,1},{6,7},{7,6},{8,12},{9,13},{10,... | collective-permute-start | bytes 3145736 | tf_op jit(solution)/shard_map/ppermute | solution.py:629
  119.2 30.3 %collective-permute-start.25 = (bf16[4,64,2048]{2,1,0:T(8,128)(2,1)}, bf16[4,64,2048]{2,1,0:T(8,128)(2,1)}, u32[]{:S(2)}, u32[]{:S(2)}) collective-permute-start(bf16[4,64,2048]{2,1,0:T(8,128)(2,1)} %pad_maximum_fusion.2.refs_0_), channel_id=1, source_target_pairs={{0,2},{1,3},{2,0},{3,1},{4,6},{5,7},{6,4},{7,5},{8,10},{9,11},{10,... | collective-permute-start | bytes 3145736 | tf_op jit(solution)/shard_map/ppermute | solution.py:629
  158.0 42.1 %collective-permute-start.30 = (bf16[2,2,4,64,2048]{4,3,2,1,0:T(8,128)(2,1)}, bf16[2,2,4,64,2048]{4,3,2,1,0:T(8,128)(2,1)}, u32[]{:S(2)}, u32[]{:S(2)}) collective-permute-start(bf16[2,2,4,64,2048]{4,3,2,1,0:T(8,128)(2,1)} %fc2_grad_far.1), channel_id=1, source_target_pairs={{0,2},{1,3},{2,0},{3,1},{4,6},{5,7},{6,4},{7,5},{8,10},{9,11},{10,... | collective-permute-start | bytes 12582920 | tf_op jit(solution)/shard_map/ppermute | solution.py:629
  158.2 15.0 %collective-permute-start.26 = (bf16[4,64,2048]{2,1,0:T(8,128)(2,1)}, bf16[4,64,2048]{2,1,0:T(8,128)(2,1)S(1)}, u32[]{:S(2)}, u32[]{:S(2)}) collective-permute-start(bf16[4,64,2048]{2,1,0:T(8,128)(2,1)} %collective-permute-done.23.refs_2_), channel_id=1, source_target_pairs={{0,4},{1,5},{2,3},{3,2},{4,0},{5,1},{6,7},{7,6},{8,12},{9,13},{10,... | collective-permute-start | bytes 3145736 | tf_op jit(solution)/shard_map/ppermute | solution.py:629
  158.9 14.3 %collective-permute-start.28 = (bf16[4,64,2048]{2,1,0:T(8,128)(2,1)}, bf16[4,64,2048]{2,1,0:T(8,128)(2,1)S(1)}, u32[]{:S(2)}, u32[]{:S(2)}) collective-permute-start(bf16[4,64,2048]{2,1,0:T(8,128)(2,1)} %collective-permute-done.23.refs_2_), channel_id=1, source_target_pairs={{0,2},{1,3},{2,0},{3,1},{4,6},{5,7},{6,4},{7,5},{8,10},{9,11},{10,... | collective-permute-start | bytes 3145736 | tf_op jit(solution)/shard_map/ppermute | solution.py:629
  160.3 12.9 %collective-permute-start.27 = (bf16[4,64,2048]{2,1,0:T(8,128)(2,1)}, bf16[4,64,2048]{2,1,0:T(8,128)(2,1)S(1)}, u32[]{:S(2)}, u32[]{:S(2)}) collective-permute-start(bf16[4,64,2048]{2,1,0:T(8,128)(2,1)} %collective-permute-done.24.refs_1_), channel_id=1, source_target_pairs={{0,2},{1,3},{2,0},{3,1},{4,6},{5,7},{6,4},{7,5},{8,10},{9,11},{10,... | collective-permute-start | bytes 3145736 | tf_op jit(solution)/shard_map/ppermute | solution.py:629
  199.8 37.9 %collective-permute-start.33 = (bf16[2,2,4,64,2048]{4,3,2,1,0:T(8,128)(2,1)}, bf16[2,2,4,64,2048]{4,3,2,1,0:T(8,128)(2,1)}, u32[]{:S(2)}, u32[]{:S(2)}) collective-permute-start(bf16[2,2,4,64,2048]{4,3,2,1,0:T(8,128)(2,1)} %fc1_grad_far.1), channel_id=1, source_target_pairs={{0,2},{1,3},{2,0},{3,1},{4,6},{5,7},{6,4},{7,5},{8,10},{9,11},{10,... | collective-permute-start | bytes 12582920 | tf_op jit(solution)/shard_map/ppermute | solution.py:629
  206.3 26.2 %collective-permute-start.31 = (bf16[2,4,64,2048]{3,2,1,0:T(8,128)(2,1)S(1)}, bf16[2,4,64,2048]{3,2,1,0:T(8,128)(2,1)}, u32[]{:S(2)}, u32[]{:S(2)}) collective-permute-start(bf16[2,4,64,2048]{3,2,1,0:T(8,128)(2,1)S(1)} %get-tuple-element.159), channel_id=1, source_target_pairs={{0,1},{1,0},{2,6},{3,7},{4,5},{5,4},{6,2},{7,3},{8,9},{9,8},{10,14... | collective-permute-start | bytes 6291464 | tf_op jit(solution)/shard_map/ppermute | solution.py:629
  235.2 16.6 %collective-permute-start.34 = (bf16[4,64,2048]{2,1,0:T(8,128)(2,1)S(1)}, bf16[4,64,2048]{2,1,0:T(8,128)(2,1)S(1)}, u32[]{:S(2)}, u32[]{:S(2)}) collective-permute-start(bf16[4,64,2048]{2,1,0:T(8,128)(2,1)S(1)} %get-tuple-element.225), channel_id=1, source_target_pairs={{0,4},{1,5},{2,3},{3,2},{4,0},{5,1},{6,7},{7,6},{8,12},{9,13},{10,... | collective-permute-start | bytes 3145736 | tf_op jit(solution)/shard_map/ppermute | solution.py:629
  243.6 45.0 %collective-permute-start.39 = (bf16[2,4,64,2048]{3,2,1,0:T(8,128)(2,1)}, bf16[2,4,64,2048]{3,2,1,0:T(8,128)(2,1)}, u32[]{:S(2)}, u32[]{:S(2)}) collective-permute-start(bf16[2,4,64,2048]{3,2,1,0:T(8,128)(2,1)} %get-tuple-element.170), channel_id=1, source_target_pairs={{0,1},{1,0},{2,6},{3,7},{4,5},{5,4},{6,2},{7,3},{8,9},{9,8},{10,14... | collective-permute-start | bytes 6291464 | tf_op jit(solution)/shard_map/ppermute | solution.py:629
  245.3 41.6 %collective-permute-start.35 = (bf16[2,4,64,512]{3,2,1,0:T(8,128)(2,1)}, bf16[2,4,64,512]{3,2,1,0:T(8,128)(2,1)}, u32[]{:S(2)}, u32[]{:S(2)}) collective-permute-start(bf16[2,4,64,512]{3,2,1,0:T(8,128)(2,1)} %get-tuple-element.168), channel_id=1, source_target_pairs={{0,1},{1,0},{2,6},{3,7},{4,5},{5,4},{6,2},{7,3},{8,9},{9,8},{10,14... | collective-permute-start | bytes 1572872 | tf_op jit(solution)/shard_map/ppermute | solution.py:629
  253.2 33.8 %collective-permute-start.36 = (bf16[64,2048]{1,0:T(8,128)(2,1)}, bf16[64,2048]{1,0:T(8,128)(2,1)}, u32[]{:S(2)}, u32[]{:S(2)}) collective-permute-start(bf16[64,2048]{1,0:T(8,128)(2,1)} %get-tuple-element.234), channel_id=1, source_target_pairs={{0,8},{1,9},{2,10},{3,11},{4,12},{5,13},{6,14},{7,15},{8,0},{9,1},... | collective-permute-start | bytes 786440 | tf_op jit(solution)/shard_map/ppermute | solution.py:629
  259.5 27.5 %collective-permute-start.37 = (bf16[64,2048]{1,0:T(8,128)(2,1)}, bf16[64,2048]{1,0:T(8,128)(2,1)}, u32[]{:S(2)}, u32[]{:S(2)}) collective-permute-start(bf16[64,2048]{1,0:T(8,128)(2,1)} %get-tuple-element.233), channel_id=1, source_target_pairs={{0,16},{1,17},{2,18},{3,19},{4,20},{5,21},{6,22},{7,23},{8,24},{9,... | collective-permute-start | bytes 786440 | tf_op jit(solution)/shard_map/ppermute | solution.py:629
  259.5 27.5 %collective-permute-start.38 = (bf16[64,2048]{1,0:T(8,128)(2,1)}, bf16[64,2048]{1,0:T(8,128)(2,1)}, u32[]{:S(2)}, u32[]{:S(2)}) collective-permute-start(bf16[64,2048]{1,0:T(8,128)(2,1)} %get-tuple-element.232), channel_id=1, source_target_pairs={{0,24},{1,25},{2,26},{3,27},{4,28},{5,29},{6,30},{7,31},{8,16},{9,... | collective-permute-start | bytes 786440 | tf_op jit(solution)/shard_map/ppermute | solution.py:629
  296.6 22.0 %collective-permute-start.41 = (bf16[4,64,2560]{2,1,0:T(8,128)(2,1)S(1)}, bf16[4,64,2560]{2,1,0:T(8,128)(2,1)S(1)}, u32[]{:S(2)}, u32[]{:S(2)}) collective-permute-start(bf16[4,64,2560]{2,1,0:T(8,128)(2,1)S(1)} %get-tuple-element.223), channel_id=1, source_target_pairs={{0,4},{1,5},{2,3},{3,2},{4,0},{5,1},{6,7},{7,6},{8,12},{9,13},{10,... | collective-permute-start | bytes 3932168 | tf_op jit(solution)/shard_map/ppermute | solution.py:629
  307.1 39.5 %collective-permute-start.45 = (bf16[2,4,64,1536]{3,2,1,0:T(8,128)(2,1)S(1)}, bf16[2,4,64,1536]{3,2,1,0:T(8,128)(2,1)}, u32[]{:S(2)}, u32[]{:S(2)}) collective-permute-start(bf16[2,4,64,1536]{3,2,1,0:T(8,128)(2,1)S(1)} %get-tuple-element.185), channel_id=1, source_target_pairs={{0,1},{1,0},{2,6},{3,7},{4,5},{5,4},{6,2},{7,3},{8,9},{9,8},{10,14... | collective-permute-start | bytes 4718600 | tf_op jit(solution)/shard_map/ppermute | solution.py:629
  319.9 19.6 %collective-permute-start.42 = (bf16[64,2560]{1,0:T(8,128)(2,1)}, bf16[64,2560]{1,0:T(8,128)(2,1)}, u32[]{:S(2)}, u32[]{:S(2)}) collective-permute-start(bf16[64,2560]{1,0:T(8,128)(2,1)} %get-tuple-element.230), channel_id=1, source_target_pairs={{0,8},{1,9},{2,10},{3,11},{4,12},{5,13},{6,14},{7,15},{8,0},{9,1},... | collective-permute-start | bytes 983048 | tf_op jit(solution)/shard_map/ppermute | solution.py:629
  321.0 25.6 %collective-permute-start.43 = (bf16[64,2560]{1,0:T(8,128)(2,1)S(1)}, bf16[64,2560]{1,0:T(8,128)(2,1)}, u32[]{:S(2)}, u32[]{:S(2)}) collective-permute-start(bf16[64,2560]{1,0:T(8,128)(2,1)S(1)} %get-tuple-element.229), channel_id=1, source_target_pairs={{0,16},{1,17},{2,18},{3,19},{4,20},{5,21},{6,22},{7,23},{8,24},{9,... | collective-permute-start | bytes 983048 | tf_op jit(solution)/shard_map/ppermute | solution.py:629
  321.9 24.7 %collective-permute-start.44 = (bf16[64,2560]{1,0:T(8,128)(2,1)S(1)}, bf16[64,2560]{1,0:T(8,128)(2,1)}, u32[]{:S(2)}, u32[]{:S(2)}) collective-permute-start(bf16[64,2560]{1,0:T(8,128)(2,1)S(1)} %get-tuple-element.228), channel_id=1, source_target_pairs={{0,24},{1,25},{2,26},{3,27},{4,28},{5,29},{6,30},{7,31},{8,16},{9,... | collective-permute-start | bytes 983048 | tf_op jit(solution)/shard_map/ppermute | solution.py:629
  349.5 12.2 %collective-permute-start.47 = (bf16[4,64,1536]{2,1,0:T(8,128)(2,1)}, bf16[4,64,1536]{2,1,0:T(8,128)(2,1)S(1)}, u32[]{:S(2)}, u32[]{:S(2)}) collective-permute-start(bf16[4,64,1536]{2,1,0:T(8,128)(2,1)} %get-tuple-element.226), channel_id=1, source_target_pairs={{0,4},{1,5},{2,3},{3,2},{4,0},{5,1},{6,7},{7,6},{8,12},{9,13},{10,... | collective-permute-start | bytes 2359304 | tf_op jit(solution)/shard_map/ppermute | solution.py:629
  362.0 14.0 %collective-permute-start.50 = (bf16[64,1536]{1,0:T(8,128)(2,1)S(1)}, bf16[64,1536]{1,0:T(8,128)(2,1)S(1)}, u32[]{:S(2)}, u32[]{:S(2)}) collective-permute-start(bf16[64,1536]{1,0:T(8,128)(2,1)S(1)} %get-tuple-element.238), channel_id=1, source_target_pairs={{0,8},{1,9},{2,10},{3,11},{4,12},{5,13},{6,14},{7,15},{8,0},{9,1},... | collective-permute-start | bytes 589832 | tf_op jit(solution)/shard_map/ppermute | solution.py:629
  372.0 15.5 %collective-permute-start.54 = (bf16[64,1536]{1,0:T(8,128)(2,1)S(1)}, bf16[64,1536]{1,0:T(8,128)(2,1)S(1)}, u32[]{:S(2)}, u32[]{:S(2)}) collective-permute-start(bf16[64,1536]{1,0:T(8,128)(2,1)S(1)} %get-tuple-element.236), channel_id=1, source_target_pairs={{0,16},{1,17},{2,18},{3,19},{4,20},{5,21},{6,22},{7,23},{8,24},{9,... | collective-permute-start | bytes 589832 | tf_op jit(solution)/shard_map/ppermute | solution.py:629
  373.0 14.5 %collective-permute-start.55 = (bf16[64,1536]{1,0:T(8,128)(2,1)S(1)}, bf16[64,1536]{1,0:T(8,128)(2,1)S(1)}, u32[]{:S(2)}, u32[]{:S(2)}) collective-permute-start(bf16[64,1536]{1,0:T(8,128)(2,1)S(1)} %get-tuple-element.237), channel_id=1, source_target_pairs={{0,24},{1,25},{2,26},{3,27},{4,28},{5,29},{6,30},{7,31},{8,16},{9,... | collective-permute-start | bytes 589832 | tf_op jit(solution)/shard_map/ppermute | solution.py:629
  376.0 14.3 %collective-permute-start.51 = (f32[12,1024]{1,0:T(8,128)S(1)}, f32[12,1024]{1,0:T(8,128)S(1)}, u32[]{:S(2)}, u32[]{:S(2)}) collective-permute-start(f32[12,1024]{1,0:T(8,128)S(1)} %add.93), channel_id=1, source_target_pairs={{0,8},{1,9},{2,10},{3,11},{4,12},{5,13},{6,14},{7,15},{8,0},{9,1},... | collective-permute-start | bytes 147464 | tf_op jit(solution)/shard_map/ppermute | solution.py:629
  376.2 15.4 %collective-permute-start.52 = (f32[12,1024]{1,0:T(8,128)S(1)}, f32[12,1024]{1,0:T(8,128)S(1)}, u32[]{:S(2)}, u32[]{:S(2)}) collective-permute-start(f32[12,1024]{1,0:T(8,128)S(1)} %add.93), channel_id=1, source_target_pairs={{0,16},{1,17},{2,18},{3,19},{4,20},{5,21},{6,22},{7,23},{8,24},{9,... | collective-permute-start | bytes 147464 | tf_op jit(solution)/shard_map/ppermute | solution.py:629
  377.6 13.9 %collective-permute-start.53 = (f32[12,1024]{1,0:T(8,128)S(1)}, f32[12,1024]{1,0:T(8,128)S(1)}, u32[]{:S(2)}, u32[]{:S(2)}) collective-permute-start(f32[12,1024]{1,0:T(8,128)S(1)} %add.93), channel_id=1, source_target_pairs={{0,24},{1,25},{2,26},{3,27},{4,28},{5,29},{6,30},{7,31},{8,16},{9,... | collective-permute-start | bytes 147464 | tf_op jit(solution)/shard_map/ppermute | solution.py:629
  (54 other events, 642.9 us)

commit v3 on v2

--- a/solution.py
+++ b/solution.py
@@ -47,7 +47,7 @@
             dimension_semantics=("arbitrary",) * len(grid), vmem_limit_bytes=room << 20
         ),
         cost_estimate=pl.CostEstimate(
-            flops=flops if heavy else 1, bytes_accessed=moved if heavy else 1, transcendentals=0
+            flops=flops * 100 if heavy else 1, bytes_accessed=moved if heavy else 1, transcendentals=0
         ),
         name=name,
     )
@@ -828,7 +828,6 @@
     qkv_out = Scatter(turned_one, after(qkv_low, done), size, depth, "qkv_grad")
     done = qkv_out.far(me)
     done = qkv_out.near(done)
-    done = fc1.third(done)
     input_grad, vec_one = norm_back_call(
         me,
         after(qkv_low, done),
@@ -854,13 +853,12 @@
             fc1_sum.reshape(4, width),
         ]
     )
-    done = qkv_out.second(input_grad, *fc1.received)
+    done = fc1.third(input_grad)
+    done = qkv_out.second(done)
     sums = after(sums, done)
-    sums = sums + along_core(sums, size)
-    done = qkv_out.third(sums)
-    sums = after(sums, done)
-    for bits in (X_BIT, Y_BIT):
+    for bits in (CORE_BIT, X_BIT, Y_BIT):
         sums = sums + swap(sums, size, bits)
+    done = qkv_out.third(sums, *fc1.received)
     sums = after(sums, qkv_out.received[0])
     fc2_grad = fc2.last(sums)
     fc1_grad = fc1.last(sums)

time: 394 us -> 386 us (0.980)
  waiting for transfers between devices: 114 us -> 102 us
    ppermute x56, waiting for transfers between devices: 114 us -> 102 us  [swap(): lax.ppermute(value, AXES, [(i, i ^ (other if i & CORE_BIT else bits)) for...]
    unnamed x98 -> x132, local copies, waits for them, and re-layouts: 20 us -> 17.3 us
  transfers between devices with their start and end apart: 56 -> 56, of which waited for: 21 -> 21; matrix products, arithmetic and copies ran while one was open for 7% -> 8% of each run, Pallas kernels for 37% -> 39%
where the time goes in v3:
time: 386 us; the launch traced here: 384 us
  Pallas kernels  154 us (40%)
  waiting for transfers between devices  102 us (26%)
  starting transfers between devices  69.9 us (18%)
  local copies, waits for them, and re-layouts  32.1 us (8%)
  other arithmetic  24.4 us (6%)
    ppermute x56, waiting for transfers between devices, swap(): lax.ppermute(value, AXES, [(i, i ^ (other if i & CORE_BIT else bits)) for...  102 us
    ppermute x56, starting transfers between devices, swap(): lax.ppermute(value, AXES, [(i, i ^ (other if i & CORE_BIT else bits)) for...  69.9 us
    pallas_call x8, Pallas kernels, weight_grad_call(): call(body, (steps,), ins, outs, shapes, scratch, 2 * count * width * span...  35.4 us
    pallas_call x2, Pallas kernels, norm_back_call(): call(body, (4,), [pl.BlockSpec((count, chunk), lambda t, me: (0, t)), who...  29.3 us
    pallas_call x1, Pallas kernels, attend_back_call(): call(body, (images, 2), [pl.BlockSpec((seq, 3 * half), lambda i, y, me: (...  21.1 us
    pallas_call x1, Pallas kernels, contract_call(): call(body, (8,), [part, part, whole(count, width), whole(count, width), w...  18 us
    unnamed x132, local copies, waits for them, and re-layouts  17.3 us
    pallas_call x1, Pallas kernels, expand_call(): call(body, (8,), [whole(count, width), pl.BlockSpec((1, chunk), lambda t,...  16.2 us
  transfers between devices with their start and end apart: 56, of which 21 were waited for; matrix products, arithmetic and copies ran while one was open for 8% of the time, Pallas kernels for 39%

profile of v3, /device:TPU:0, one launch (start us, length us, event | category | flops | bytes accessed | tf_op | source)
XLA Modules:
  0.0 384.2 jit_solution(7328908292906880455)
XLA Ops:
  3.5 3.1 collective-permute-start
  6.6 2.6 collective-permute-start.1
  10.3 3.7 fusion.5
  15.7 9.1 %collective-permute-done.1 = bf16[64,1664]{1,0:T(8,128)(2,1)S(1)} collective-permute-done((bf16[64,1664]{1,0:T(8,128)(2,1)S(1)}, bf16[64,1664]{1,0:T(8,128)(2,1)S(1)}, u32[]{:S(2)}, u32[]{:S(2)}) %collective-permute-start.1) | collective-permute-done | bytes 213024 | tf_op jit(solution)/shard_map/ppermute | solution.py:629
  27.9 3.8 collective-permute-start.6
  32.7 14.3 %collective-permute-done.6 = bf16[64,2560]{1,0:T(8,128)(2,1)S(1)} collective-permute-done((bf16[64,2560]{1,0:T(8,128)(2,1)S(1)}, bf16[64,2560]{1,0:T(8,128)(2,1)S(1)}, u32[]{:S(2)}, u32[]{:S(2)}) %collective-permute-start.6) | collective-permute-done | bytes 327712 | tf_op jit(solution)/shard_map/ppermute | solution.py:629
  47.0 2.5 collective-permute-done.7
  50.1 2.5 collective-permute-start.9
  53.3 8.8 %collective-permute-done.9 = bf16[64,2560]{1,0:T(8,128)(2,1)S(1)} collective-permute-done((bf16[64,2560]{1,0:T(8,128)(2,1)S(1)}, bf16[64,2560]{1,0:T(8,128)(2,1)S(1)}, u32[]{:S(2)}, u32[]{:S(2)}) %collective-permute-start.9) | collective-permute-done | bytes 327712 | tf_op jit(solution)/shard_map/ppermute | solution.py:629
  65.0 3.7 collective-permute-done.10.refs_5_
  68.7 6.1 %collective-permute-start.15 = (bf16[64,2048]{1,0:T(8,128)(2,1)}, bf16[64,2048]{1,0:T(8,128)(2,1)}, u32[]{:S(2)}, u32[]{:S(2)}) collective-permute-start(bf16[64,2048]{1,0:T(8,128)(2,1)} %convert_bitcast_fusion), channel_id=1, source_target_pairs={{0,8},{1,9},{2,10},{3,11},{4,12},{5,13},{6,14},{7,15},{8,0},{9,1},... | collective-permute-start | bytes 786440 | tf_op jit(solution)/shard_map/ppermute | solution.py:629
  77.0 13.1 %qkv.1 = (bf16[640,1024]{1,0:T(8,128)(2,1)}, bf16[1024,640]{1,0:T(8,128)(2,1)}, bf16[640,3072]{1,0:T(8,128)(2,1)}, f32[16,1024]{1,0:T(8,128)}) custom-call(s32[1]{0:T(128)} %bitcast.me_ref, f32[640,1024]{1,0:T(8,128)} %bitcast.110, bf16[4,64,1664]{2,1,0:T(8,128)(2,1)} %copy-done.43, bf16[4,64,1664]{2,1,0:T(8,128)(2,1)} %copy-done.46, ...), custom_call_target="tpu_custom_call" | custom-call | flops 1 | bytes 1 | tf_op jit(solution)/shard_map/qkv/pallas_call | solution.py:132
  90.1 3.8 collective-permute-done.13.refs_2_
  95.0 2.5 collective-permute-start.21
  101.9 11.7 %attend.1.mixed_ref.right_ref = bf16[640,1024]{1,0:T(8,128)(2,1)S(1)} custom-call(s32[1]{0:T(128)} %bitcast.me_ref, bf16[640,3072]{1,0:T(8,128)(2,1)S(1)} %copy-done.15, s32[2,1,320]{2,1,0:T(1,128)S(1)} %broadcast_in_dim.10.seen_ref), custom_call_target="tpu_custom_call" | custom-call | flops 1 | bytes 1 | tf_op jit(solution)/shard_map/attend/pallas_call | solution.py:190
  113.7 2.6 pad_maximum_fusion.2.refs_0_
  118.4 5.3 %project.1 = (f32[640,1024]{1,0:T(8,128)S(1)}, bf16[640,1024]{1,0:T(8,128)(2,1)S(1)}, bf16[1024,640]{1,0:T(8,128)(2,1)S(1)}) custom-call(s32[1]{0:T(128)} %bitcast.me_ref, bf16[640,1024]{1,0:T(8,128)(2,1)S(1)} %attend.1.mixed_ref.right_ref, f32[640,1024]{1,0:T(8,128)S(1)} %bitcast.112, f32[16,1024]{1,0:T(8,128)S(1)} %copy-done.39, ...), custom_call_target="tpu_custom_call" | custom-call | flops 1 | bytes 1 | tf_op jit(solution)/shard_map/project/pallas_call | solution.py:227
  127.3 16.2 %expand.1 = (bf16[640,4096]{1,0:T(8,128)(2,1)}, bf16[640,4096]{1,0:T(8,128)(2,1)}) custom-call(s32[1]{0:T(128)} %bitcast.me_ref, bf16[640,1024]{1,0:T(8,128)(2,1)} %copy-done.38, f32[1,4096]{1,0:T(1,128)} %reshape.119.bias_ref, bf16[4,64,2560]{2,1,0:T(8,128)(2,1)} %copy-done.4, bf16[4,64,2560]{2,1,0:T(8,128)(2,1)} %collective-permute-done.14.refs_1_, ...), custom_call_target="tpu_custom_call" | custom-call | flops 1 | bytes 1 | tf_op jit(solution)/shard_map/expand/pallas_call | solution.py:270
  146.5 2.5 copy-done.11
  149.0 5.9 %fc2_grad_far.1 = bf16[2,2,4,64,2048]{4,3,2,1,0:T(8,128)(2,1)} custom-call(s32[1]{0:T(128)} %bitcast.me_ref, bf16[1024,640]{1,0:T(8,128)(2,1)S(1)} %copy.56.turn_ref, bf16[640,4096]{1,0:T(8,128)(2,1)S(1)} %copy-done.11), custom_call_target="tpu_custom_call" | custom-call | flops 1 | bytes 1 | tf_op jit(solution)/shard_map/fc2_grad_far/pallas_call | solution.py:614
  154.9 3.8 collective-permute-done.26.refs_3_
  163.3 18.0 %contract.1 = (f32[640,1024]{1,0:T(8,128)}, bf16[640,4096]{1,0:T(8,128)(2,1)S(1)}, f32[1,4096]{1,0:T(1,128)S(1)}) custom-call(s32[1]{0:T(128)} %bitcast.me_ref, bf16[640,4096]{1,0:T(8,128)(2,1)S(1)} %copy-done.12, bf16[640,4096]{1,0:T(8,128)(2,1)} %get-tuple-element.141.slope_ref, bf16[640,1024]{1,0:T(8,128)(2,1)S(1)} %copy-done.20, ...), custom_call_target="tpu_custom_call" | custom-call | flops 1073741824000 | bytes 24117248 | tf_op jit(solution)/shard_map/contract/pallas_call | solution.py:312
  181.4 6.0 %fc1_grad_far.1 = bf16[2,2,4,64,2048]{4,3,2,1,0:T(8,128)(2,1)} custom-call(s32[1]{0:T(128)} %bitcast.me_ref, bf16[1024,640]{1,0:T(8,128)(2,1)S(1)} %copy-done.25, bf16[640,4096]{1,0:T(8,128)(2,1)S(1)} %get-tuple-element.161.right_ref.low_ref), custom_call_target="tpu_custom_call" | custom-call | flops 1 | bytes 1 | tf_op jit(solution)/shard_map/fc1_grad_far/pallas_call | solution.py:614
  187.6 5.9 %fc2_grad_near.1 = (bf16[2,4,64,2048]{3,2,1,0:T(8,128)(2,1)S(1)}, bf16[2,4,64,2048]{3,2,1,0:T(8,128)(2,1)}) custom-call(s32[1]{0:T(128)} %bitcast.me_ref, bf16[1024,640]{1,0:T(8,128)(2,1)S(1)} %copy-done.18, bf16[640,4096]{1,0:T(8,128)(2,1)S(1)} %bitcast.114, bf16[2,2,4,64,2048]{4,3,2,1,0:T(8,128)(2,1)} %collective-permute-done.30.refs_0_), custom_call_target="tpu_custom_call" | custom-call | flops 1 | bytes 1 | tf_op jit(solution)/shard_map/fc2_grad_near/pallas_call | solution.py:614
  195.0 14.1 %norm_two_back.1 = (f32[640,1024]{1,0:T(8,128)S(1)}, f32[8,1024]{1,0:T(8,128)S(1)}, bf16[640,1024]{1,0:T(8,128)(2,1)S(1)}, bf16[1024,640]{1,0:T(8,128)(2,1)S(1)}) custom-call(s32[1]{0:T(128)} %bitcast.me_ref, bf16[640,4096]{1,0:T(8,128)(2,1)} %copy-done.2, f32[640,1024]{1,0:T(8,128)S(1)} %copy-done.30, f32[640,1024]{1,0:T(8,128)S(1)} %bitcast.115, ...), custom_call_target="tpu_custom_call" | custom-call | flops 1 | bytes 1 | tf_op jit(solution)/shard_map/norm_two_back/pallas_call | solution.py:397
  209.1 4.3 %mixed_back.1.grad_ref = bf16[640,1024]{1,0:T(8,128)(2,1)S(1)} custom-call(s32[1]{0:T(128)} %bitcast.me_ref, bf16[640,1024]{1,0:T(8,128)(2,1)S(1)} %get-tuple-element.154.low_ref, bf16[4,64,2560]{2,1,0:T(8,128)(2,1)S(1)} %copy-done.5, bf16[4,64,2560]{2,1,0:T(8,128)(2,1)} %collective-permute-done.14.refs_1_, bf16[4,64,2560]{2,1,0:T(8,128)(2,1)S(1)} %copy-done.8, ...), custom_call_target="tpu_custom_call" | custom-call | flops 1 | bytes 1 | tf_op jit(solution)/shard_map/mixed_back/pallas_call | solution.py:437
  215.2 4.7 %collective-permute-done.31 = bf16[2,4,64,2048]{3,2,1,0:T(8,128)(2,1)} collective-permute-done((bf16[2,4,64,2048]{3,2,1,0:T(8,128)(2,1)}, bf16[2,4,64,2048]{3,2,1,0:T(8,128)(2,1)}, u32[]{:S(2)}, u32[]{:S(2)}) %collective-permute-start.31) | collective-permute-done | bytes 2097184 | tf_op jit(solution)/shard_map/ppermute | solution.py:629
  219.9 2.5 add_convert_fusion.1
  225.0 5.6 %fc1_grad_near.1 = (bf16[2,4,64,2048]{3,2,1,0:T(8,128)(2,1)S(1)}, bf16[2,4,64,2048]{3,2,1,0:T(8,128)(2,1)}) custom-call(s32[1]{0:T(128)} %bitcast.me_ref, bf16[1024,640]{1,0:T(8,128)(2,1)S(1)} %copy-done.26, bf16[640,4096]{1,0:T(8,128)(2,1)S(1)} %bitcast.109, bf16[2,2,4,64,2048]{4,3,2,1,0:T(8,128)(2,1)} %collective-permute-done.33.refs_0_), custom_call_target="tpu_custom_call" | custom-call | flops 1 | bytes 1 | tf_op jit(solution)/shard_map/fc1_grad_near/pallas_call | solution.py:614
  232.7 6.5 %collective-permute-done.34 = bf16[4,64,2048]{2,1,0:T(8,128)(2,1)S(1)} collective-permute-done((bf16[4,64,2048]{2,1,0:T(8,128)(2,1)S(1)}, bf16[4,64,2048]{2,1,0:T(8,128)(2,1)S(1)}, u32[]{:S(2)}, u32[]{:S(2)}) %collective-permute-start.34) | collective-permute-done | bytes 1048608 | tf_op jit(solution)/shard_map/ppermute | solution.py:629
  240.7 6.2 %collective-permute-start.36 = (bf16[64,2048]{1,0:T(8,128)(2,1)}, bf16[64,2048]{1,0:T(8,128)(2,1)}, u32[]{:S(2)}, u32[]{:S(2)}) collective-permute-start(bf16[64,2048]{1,0:T(8,128)(2,1)} %get-tuple-element.232), channel_id=1, source_target_pairs={{0,8},{1,9},{2,10},{3,11},{4,12},{5,13},{6,14},{7,15},{8,0},{9,1},... | collective-permute-start | bytes 786440 | tf_op jit(solution)/shard_map/ppermute | solution.py:629
  246.9 2.4 collective-permute-start.38
  254.6 21.1 %attend_back.1 = (bf16[640,3072]{1,0:T(8,128)(2,1)S(1)}, f32[2,2,1,1536]{3,2,1,0:T(1,128)S(1)}) custom-call(s32[1]{0:T(128)} %bitcast.me_ref, bf16[640,3072]{1,0:T(8,128)(2,1)S(1)} %copy-done.16, bf16[640,1024]{1,0:T(8,128)(2,1)S(1)} %copy-done.22, s32[2,320,1]{2,1,0:T(8,128)S(1)} %copy-done.37), custom_call_target="tpu_custom_call" | custom-call | flops 1 | bytes 1 | tf_op jit(solution)/shard_map/attend_back/pallas_call | solution.py:488
  277.4 2.4 add_convert_fusion
  281.5 4.2 %qkv_grad_far.1 = bf16[2,2,4,64,1536]{4,3,2,1,0:T(8,128)(2,1)S(1)} custom-call(s32[1]{0:T(128)} %bitcast.me_ref, bf16[1024,640]{1,0:T(8,128)(2,1)S(1)} %copy-done.23, bf16[640,3072]{1,0:T(8,128)(2,1)S(1)} %get-tuple-element.175.right_ref.low_ref), custom_call_target="tpu_custom_call" | custom-call | flops 1 | bytes 1 | tf_op jit(solution)/shard_map/qkv_grad_far/pallas_call | solution.py:614
  286.3 5.1 %collective-permute-done.40.refs_0_ = bf16[2,2,4,64,1536]{4,3,2,1,0:T(8,128)(2,1)S(1)} collective-permute-done((bf16[2,2,4,64,1536]{4,3,2,1,0:T(8,128)(2,1)S(1)}, bf16[2,2,4,64,1536]{4,3,2,1,0:T(8,128)(2,1)S(1)}, u32[]{:S(2)}, u32[]{:S(2)}) %collective-permute-start.40) | collective-permute-done | bytes 3145760 | tf_op jit(solution)/shard_map/ppermute | solution.py:629
  291.4 4.7 %qkv_grad_near.1 = (bf16[2,4,64,1536]{3,2,1,0:T(8,128)(2,1)S(1)}, bf16[2,4,64,1536]{3,2,1,0:T(8,128)(2,1)}) custom-call(s32[1]{0:T(128)} %bitcast.me_ref, bf16[1024,640]{1,0:T(8,128)(2,1)S(1)} %copy-done.23, bf16[640,3072]{1,0:T(8,128)(2,1)S(1)} %get-tuple-element.175.right_ref.low_ref, bf16[2,2,4,64,1536]{4,3,2,1,0:T(8,128)(2,1)S(1)} %collective-permute-done.40.refs_0_), custom_call_target="tpu_custom_call" | custom-call | flops 1 | bytes 1 | tf_op jit(solution)/shard_map/qkv_grad_near/pallas_call | solution.py:614
  297.3 15.1 %norm_one_back.1 = (f32[640,1024]{1,0:T(8,128)}, f32[8,1024]{1,0:T(8,128)}) custom-call(s32[1]{0:T(128)} %bitcast.me_ref, bf16[640,3072]{1,0:T(8,128)(2,1)} %copy-done.3, f32[640,1024]{1,0:T(8,128)} %bitcast.111, f32[640,1024]{1,0:T(8,128)} %copy-done.27, f32[16,1024]{1,0:T(8,128)} %get-tuple-element.118.table_ref, bf16[4,64,1664]{2,1,0:T(8,128)(2,1)} %copy-done.43, ...), custom_call_target="tpu_custom_call" | custom-call | flops 1 | bytes 1 | tf_op jit(solution)/shard_map/norm_one_back/pallas_call | solution.py:397
  314.9 5.0 %collective-permute-done.42 = bf16[2,4,64,1536]{3,2,1,0:T(8,128)(2,1)S(1)} collective-permute-done((bf16[2,4,64,1536]{3,2,1,0:T(8,128)(2,1)}, bf16[2,4,64,1536]{3,2,1,0:T(8,128)(2,1)S(1)}, u32[]{:S(2)}, u32[]{:S(2)}) %collective-permute-start.42) | collective-permute-done | bytes 1572896 | tf_op jit(solution)/shard_map/ppermute | solution.py:629
  326.0 2.4 collective-permute-start.48
  332.1 2.7 collective-permute-done.44
  335.5 3.7 collective-permute-done.45
  339.2 11.5 %collective-permute-done.47 = bf16[64,2560]{1,0:T(8,128)(2,1)} collective-permute-done((bf16[64,2560]{1,0:T(8,128)(2,1)S(1)}, bf16[64,2560]{1,0:T(8,128)(2,1)}, u32[]{:S(2)}, u32[]{:S(2)}) %collective-permute-start.47) | collective-permute-done | bytes 327712 | tf_op jit(solution)/shard_map/ppermute | solution.py:629
  352.1 6.3 %collective-permute-start.50 = (bf16[64,1536]{1,0:T(8,128)(2,1)S(1)}, bf16[64,1536]{1,0:T(8,128)(2,1)S(1)}, u32[]{:S(2)}, u32[]{:S(2)}) collective-permute-start(bf16[64,1536]{1,0:T(8,128)(2,1)S(1)} %get-tuple-element.237), channel_id=1, source_target_pairs={{0,8},{1,9},{2,10},{3,11},{4,12},{5,13},{6,14},{7,15},{8,0},{9,1},... | collective-permute-start | bytes 589832 | tf_op jit(solution)/shard_map/ppermute | solution.py:629
  358.4 2.4 collective-permute-start.55
  360.9 4.9 %collective-permute-done.50 = bf16[64,1536]{1,0:T(8,128)(2,1)S(1)} collective-permute-done((bf16[64,1536]{1,0:T(8,128)(2,1)S(1)}, bf16[64,1536]{1,0:T(8,128)(2,1)S(1)}, u32[]{:S(2)}, u32[]{:S(2)}) %collective-permute-start.50) | collective-permute-done | bytes 196640 | tf_op jit(solution)/shard_map/ppermute | solution.py:629
  367.2 3.0 collective-permute-start.53
  373.5 4.3 %collective-permute-done.54 = bf16[64,1536]{1,0:T(8,128)(2,1)S(1)} collective-permute-done((bf16[64,1536]{1,0:T(8,128)(2,1)S(1)}, bf16[64,1536]{1,0:T(8,128)(2,1)S(1)}, u32[]{:S(2)}, u32[]{:S(2)}) %collective-permute-start.54) | collective-permute-done | bytes 196640 | tf_op jit(solution)/shard_map/ppermute | solution.py:629
  (274 shorter events, 79.9 us)
Async XLA Ops:
  3.5 12.2 %collective-permute-start = (bf16[64,1664]{1,0:T(8,128)(2,1)S(1)}, bf16[64,1664]{1,0:T(8,128)(2,1)S(1)}, u32[]{:S(2)}, u32[]{:S(2)}) collective-permute-start(bf16[64,1664]{1,0:T(8,128)(2,1)S(1)} %pad_maximum_fusion.5), channel_id=1, source_target_pairs={{0,8},{1,9},{2,10},{3,11},{4,12},{5,13},{6,14},{7,15},{8,0},{9,1},... | collective-permute-start | bytes 638984 | tf_op jit(solution)/shard_map/ppermute | solution.py:629
  6.6 18.2 %collective-permute-start.1 = (bf16[64,1664]{1,0:T(8,128)(2,1)S(1)}, bf16[64,1664]{1,0:T(8,128)(2,1)S(1)}, u32[]{:S(2)}, u32[]{:S(2)}) collective-permute-start(bf16[64,1664]{1,0:T(8,128)(2,1)S(1)} %pad_maximum_fusion.5), channel_id=1, source_target_pairs={{0,16},{1,17},{2,18},{3,19},{4,20},{5,21},{6,22},{7,23},{8,24},{9,... | collective-permute-start | bytes 638984 | tf_op jit(solution)/shard_map/ppermute | solution.py:629
  9.2 15.6 %collective-permute-start.2 = (bf16[64,1664]{1,0:T(8,128)(2,1)S(1)}, bf16[64,1664]{1,0:T(8,128)(2,1)S(1)}, u32[]{:S(2)}, u32[]{:S(2)}) collective-permute-start(bf16[64,1664]{1,0:T(8,128)(2,1)S(1)} %pad_maximum_fusion.5), channel_id=1, source_target_pairs={{0,24},{1,25},{2,26},{3,27},{4,28},{5,29},{6,30},{7,31},{8,16},{9,... | collective-permute-start | bytes 638984 | tf_op jit(solution)/shard_map/ppermute | solution.py:629
  24.8 24.6 %collective-permute-start.3 = (bf16[4,64,1664]{2,1,0:T(8,128)(2,1)S(1)}, bf16[4,64,1664]{2,1,0:T(8,128)(2,1)S(1)}, u32[]{:S(2)}, u32[]{:S(2)}) collective-permute-start(bf16[4,64,1664]{2,1,0:T(8,128)(2,1)S(1)} %pad_maximum_fusion.3.refs_0_), channel_id=1, source_target_pairs={{0,1},{1,0},{2,6},{3,7},{4,5},{5,4},{6,2},{7,3},{8,9},{9,8},{10,14... | collective-permute-start | bytes 2555912 | tf_op jit(solution)/shard_map/ppermute | solution.py:629
  26.4 23.1 %collective-permute-start.4 = (bf16[4,64,1664]{2,1,0:T(8,128)(2,1)S(1)}, bf16[4,64,1664]{2,1,0:T(8,128)(2,1)S(1)}, u32[]{:S(2)}, u32[]{:S(2)}) collective-permute-start(bf16[4,64,1664]{2,1,0:T(8,128)(2,1)S(1)} %pad_maximum_fusion.3.refs_0_), channel_id=1, source_target_pairs={{0,4},{1,5},{2,3},{3,2},{4,0},{5,1},{6,7},{7,6},{8,12},{9,13},{10,... | collective-permute-start | bytes 2555912 | tf_op jit(solution)/shard_map/ppermute | solution.py:629
  27.9 21.6 %collective-permute-start.5 = (bf16[4,64,1664]{2,1,0:T(8,128)(2,1)S(1)}, bf16[4,64,1664]{2,1,0:T(8,128)(2,1)S(1)}, u32[]{:S(2)}, u32[]{:S(2)}) collective-permute-start(bf16[4,64,1664]{2,1,0:T(8,128)(2,1)S(1)} %pad_maximum_fusion.3.refs_0_), channel_id=1, source_target_pairs={{0,2},{1,3},{2,0},{3,1},{4,6},{5,7},{6,4},{7,5},{8,10},{9,11},{10,... | collective-permute-start | bytes 2555912 | tf_op jit(solution)/shard_map/ppermute | solution.py:629
  27.9 19.0 %collective-permute-start.6 = (bf16[64,2560]{1,0:T(8,128)(2,1)S(1)}, bf16[64,2560]{1,0:T(8,128)(2,1)S(1)}, u32[]{:S(2)}, u32[]{:S(2)}) collective-permute-start(bf16[64,2560]{1,0:T(8,128)(2,1)S(1)} %pad_maximum_fusion.4), channel_id=1, source_target_pairs={{0,8},{1,9},{2,10},{3,11},{4,12},{5,13},{6,14},{7,15},{8,0},{9,1},... | collective-permute-start | bytes 983048 | tf_op jit(solution)/shard_map/ppermute | solution.py:629
  31.7 17.8 %collective-permute-start.7 = (bf16[64,2560]{1,0:T(8,128)(2,1)S(1)}, bf16[64,2560]{1,0:T(8,128)(2,1)S(1)}, u32[]{:S(2)}, u32[]{:S(2)}) collective-permute-start(bf16[64,2560]{1,0:T(8,128)(2,1)S(1)} %pad_maximum_fusion.4), channel_id=1, source_target_pairs={{0,16},{1,17},{2,18},{3,19},{4,20},{5,21},{6,22},{7,23},{8,24},{9,... | collective-permute-start | bytes 983048 | tf_op jit(solution)/shard_map/ppermute | solution.py:629
  49.5 12.8 %collective-permute-start.8 = (bf16[4,64,1664]{2,1,0:T(8,128)(2,1)S(1)}, bf16[4,64,1664]{2,1,0:T(8,128)(2,1)S(1)}, u32[]{:S(2)}, u32[]{:S(2)}) collective-permute-start(bf16[4,64,1664]{2,1,0:T(8,128)(2,1)S(1)} %collective-permute-done.3.refs_2_), channel_id=1, source_target_pairs={{0,4},{1,5},{2,3},{3,2},{4,0},{5,1},{6,7},{7,6},{8,12},{9,13},{10,... | collective-permute-start | bytes 2555912 | tf_op jit(solution)/shard_map/ppermute | solution.py:629
  50.1 14.8 %collective-permute-start.11 = (bf16[4,64,1664]{2,1,0:T(8,128)(2,1)S(1)}, bf16[4,64,1664]{2,1,0:T(8,128)(2,1)S(1)}, u32[]{:S(2)}, u32[]{:S(2)}) collective-permute-start(bf16[4,64,1664]{2,1,0:T(8,128)(2,1)S(1)} %collective-permute-done.3.refs_2_), channel_id=1, source_target_pairs={{0,2},{1,3},{2,0},{3,1},{4,6},{5,7},{6,4},{7,5},{8,10},{9,11},{10,... | collective-permute-start | bytes 2555912 | tf_op jit(solution)/shard_map/ppermute | solution.py:629
  50.1 12.0 %collective-permute-start.9 = (bf16[64,2560]{1,0:T(8,128)(2,1)S(1)}, bf16[64,2560]{1,0:T(8,128)(2,1)S(1)}, u32[]{:S(2)}, u32[]{:S(2)}) collective-permute-start(bf16[64,2560]{1,0:T(8,128)(2,1)S(1)} %pad_maximum_fusion.4), channel_id=1, source_target_pairs={{0,24},{1,25},{2,26},{3,27},{4,28},{5,29},{6,30},{7,31},{8,16},{9,... | collective-permute-start | bytes 983048 | tf_op jit(solution)/shard_map/ppermute | solution.py:629
  62.5 31.4 %collective-permute-start.13 = (bf16[4,64,2560]{2,1,0:T(8,128)(2,1)S(1)}, bf16[4,64,2560]{2,1,0:T(8,128)(2,1)S(1)}, u32[]{:S(2)}, u32[]{:S(2)}) collective-permute-start(bf16[4,64,2560]{2,1,0:T(8,128)(2,1)S(1)} %pad_maximum_fusion.1.refs_0_), channel_id=1, source_target_pairs={{0,1},{1,0},{2,6},{3,7},{4,5},{5,4},{6,2},{7,3},{8,9},{9,8},{10,14... | collective-permute-start | bytes 3932168 | tf_op jit(solution)/shard_map/ppermute | solution.py:629
  63.1 30.9 %collective-permute-start.14 = (bf16[4,64,2560]{2,1,0:T(8,128)(2,1)S(1)}, bf16[4,64,2560]{2,1,0:T(8,128)(2,1)}, u32[]{:S(2)}, u32[]{:S(2)}) collective-permute-start(bf16[4,64,2560]{2,1,0:T(8,128)(2,1)S(1)} %pad_maximum_fusion.1.refs_0_), channel_id=1, source_target_pairs={{0,4},{1,5},{2,3},{3,2},{4,0},{5,1},{6,7},{7,6},{8,12},{9,13},{10,... | collective-permute-start | bytes 3932168 | tf_op jit(solution)/shard_map/ppermute | solution.py:629
  64.4 29.5 %collective-permute-start.17 = (bf16[4,64,2560]{2,1,0:T(8,128)(2,1)S(1)}, bf16[4,64,2560]{2,1,0:T(8,128)(2,1)}, u32[]{:S(2)}, u32[]{:S(2)}) collective-permute-start(bf16[4,64,2560]{2,1,0:T(8,128)(2,1)S(1)} %pad_maximum_fusion.1.refs_0_), channel_id=1, source_target_pairs={{0,2},{1,3},{2,0},{3,1},{4,6},{5,7},{6,4},{7,5},{8,10},{9,11},{10,... | collective-permute-start | bytes 3932168 | tf_op jit(solution)/shard_map/ppermute | solution.py:629
  65.0 9.8 %collective-permute-start.12 = (bf16[4,64,1664]{2,1,0:T(8,128)(2,1)S(1)}, bf16[4,64,1664]{2,1,0:T(8,128)(2,1)S(1)}, u32[]{:S(2)}, u32[]{:S(2)}) collective-permute-start(bf16[4,64,1664]{2,1,0:T(8,128)(2,1)S(1)} %collective-permute-done.8.refs_3_), channel_id=1, source_target_pairs={{0,2},{1,3},{2,0},{3,1},{4,6},{5,7},{6,4},{7,5},{8,10},{9,11},{10,... | collective-permute-start | bytes 2555912 | tf_op jit(solution)/shard_map/ppermute | solution.py:629
  68.7 21.4 %collective-permute-start.15 = (bf16[64,2048]{1,0:T(8,128)(2,1)}, bf16[64,2048]{1,0:T(8,128)(2,1)}, u32[]{:S(2)}, u32[]{:S(2)}) collective-permute-start(bf16[64,2048]{1,0:T(8,128)(2,1)} %convert_bitcast_fusion), channel_id=1, source_target_pairs={{0,8},{1,9},{2,10},{3,11},{4,12},{5,13},{6,14},{7,15},{8,0},{9,1},... | collective-permute-start | bytes 786440 | tf_op jit(solution)/shard_map/ppermute | solution.py:629
  74.8 15.3 %collective-permute-start.16 = (bf16[64,2048]{1,0:T(8,128)(2,1)}, bf16[64,2048]{1,0:T(8,128)(2,1)}, u32[]{:S(2)}, u32[]{:S(2)}) collective-permute-start(bf16[64,2048]{1,0:T(8,128)(2,1)} %convert_bitcast_fusion), channel_id=1, source_target_pairs={{0,16},{1,17},{2,18},{3,19},{4,20},{5,21},{6,22},{7,23},{8,24},{9,... | collective-permute-start | bytes 786440 | tf_op jit(solution)/shard_map/ppermute | solution.py:629
  93.9 19.7 %collective-permute-start.18 = (bf16[4,64,2560]{2,1,0:T(8,128)(2,1)S(1)}, bf16[4,64,2560]{2,1,0:T(8,128)(2,1)}, u32[]{:S(2)}, u32[]{:S(2)}) collective-permute-start(bf16[4,64,2560]{2,1,0:T(8,128)(2,1)S(1)} %collective-permute-done.13.refs_2_), channel_id=1, source_target_pairs={{0,4},{1,5},{2,3},{3,2},{4,0},{5,1},{6,7},{7,6},{8,12},{9,13},{10,... | collective-permute-start | bytes 3932168 | tf_op jit(solution)/shard_map/ppermute | solution.py:629
  94.5 19.1 %collective-permute-start.19 = (bf16[4,64,2560]{2,1,0:T(8,128)(2,1)}, bf16[4,64,2560]{2,1,0:T(8,128)(2,1)}, u32[]{:S(2)}, u32[]{:S(2)}) collective-permute-start(bf16[4,64,2560]{2,1,0:T(8,128)(2,1)} %collective-permute-done.14.refs_1_), channel_id=1, source_target_pairs={{0,2},{1,3},{2,0},{3,1},{4,6},{5,7},{6,4},{7,5},{8,10},{9,11},{10,... | collective-permute-start | bytes 3932168 | tf_op jit(solution)/shard_map/ppermute | solution.py:629
  94.5 19.1 %collective-permute-start.20 = (bf16[4,64,2560]{2,1,0:T(8,128)(2,1)S(1)}, bf16[4,64,2560]{2,1,0:T(8,128)(2,1)}, u32[]{:S(2)}, u32[]{:S(2)}) collective-permute-start(bf16[4,64,2560]{2,1,0:T(8,128)(2,1)S(1)} %collective-permute-done.13.refs_2_), channel_id=1, source_target_pairs={{0,2},{1,3},{2,0},{3,1},{4,6},{5,7},{6,4},{7,5},{8,10},{9,11},{10,... | collective-permute-start | bytes 3932168 | tf_op jit(solution)/shard_map/ppermute | solution.py:629
  95.0 18.7 %collective-permute-start.21 = (bf16[64,2048]{1,0:T(8,128)(2,1)}, bf16[64,2048]{1,0:T(8,128)(2,1)S(1)}, u32[]{:S(2)}, u32[]{:S(2)}) collective-permute-start(bf16[64,2048]{1,0:T(8,128)(2,1)} %convert_bitcast_fusion), channel_id=1, source_target_pairs={{0,24},{1,25},{2,26},{3,27},{4,28},{5,29},{6,30},{7,31},{8,16},{9,... | collective-permute-start | bytes 786440 | tf_op jit(solution)/shard_map/ppermute | solution.py:629
  116.3 27.2 %collective-permute-start.23 = (bf16[4,64,2048]{2,1,0:T(8,128)(2,1)}, bf16[4,64,2048]{2,1,0:T(8,128)(2,1)}, u32[]{:S(2)}, u32[]{:S(2)}) collective-permute-start(bf16[4,64,2048]{2,1,0:T(8,128)(2,1)} %pad_maximum_fusion.2.refs_0_), channel_id=1, source_target_pairs={{0,1},{1,0},{2,6},{3,7},{4,5},{5,4},{6,2},{7,3},{8,9},{9,8},{10,14... | collective-permute-start | bytes 3145736 | tf_op jit(solution)/shard_map/ppermute | solution.py:629
  116.7 26.7 %collective-permute-start.24 = (bf16[4,64,2048]{2,1,0:T(8,128)(2,1)}, bf16[4,64,2048]{2,1,0:T(8,128)(2,1)}, u32[]{:S(2)}, u32[]{:S(2)}) collective-permute-start(bf16[4,64,2048]{2,1,0:T(8,128)(2,1)} %pad_maximum_fusion.2.refs_0_), channel_id=1, source_target_pairs={{0,4},{1,5},{2,3},{3,2},{4,0},{5,1},{6,7},{7,6},{8,12},{9,13},{10,... | collective-permute-start | bytes 3145736 | tf_op jit(solution)/shard_map/ppermute | solution.py:629
  118.3 25.2 %collective-permute-start.25 = (bf16[4,64,2048]{2,1,0:T(8,128)(2,1)}, bf16[4,64,2048]{2,1,0:T(8,128)(2,1)}, u32[]{:S(2)}, u32[]{:S(2)}) collective-permute-start(bf16[4,64,2048]{2,1,0:T(8,128)(2,1)} %pad_maximum_fusion.2.refs_0_), channel_id=1, source_target_pairs={{0,2},{1,3},{2,0},{3,1},{4,6},{5,7},{6,4},{7,5},{8,10},{9,11},{10,... | collective-permute-start | bytes 3145736 | tf_op jit(solution)/shard_map/ppermute | solution.py:629
  143.5 15.2 %collective-permute-start.26 = (bf16[4,64,2048]{2,1,0:T(8,128)(2,1)}, bf16[4,64,2048]{2,1,0:T(8,128)(2,1)}, u32[]{:S(2)}, u32[]{:S(2)}) collective-permute-start(bf16[4,64,2048]{2,1,0:T(8,128)(2,1)} %collective-permute-done.23.refs_2_), channel_id=1, source_target_pairs={{0,4},{1,5},{2,3},{3,2},{4,0},{5,1},{6,7},{7,6},{8,12},{9,13},{10,... | collective-permute-start | bytes 3145736 | tf_op jit(solution)/shard_map/ppermute | solution.py:629
  144.8 14.4 %collective-permute-start.28 = (bf16[4,64,2048]{2,1,0:T(8,128)(2,1)}, bf16[4,64,2048]{2,1,0:T(8,128)(2,1)S(1)}, u32[]{:S(2)}, u32[]{:S(2)}) collective-permute-start(bf16[4,64,2048]{2,1,0:T(8,128)(2,1)} %collective-permute-done.23.refs_2_), channel_id=1, source_target_pairs={{0,2},{1,3},{2,0},{3,1},{4,6},{5,7},{6,4},{7,5},{8,10},{9,11},{10,... | collective-permute-start | bytes 3145736 | tf_op jit(solution)/shard_map/ppermute | solution.py:629
  146.4 12.8 %collective-permute-start.27 = (bf16[4,64,2048]{2,1,0:T(8,128)(2,1)}, bf16[4,64,2048]{2,1,0:T(8,128)(2,1)S(1)}, u32[]{:S(2)}, u32[]{:S(2)}) collective-permute-start(bf16[4,64,2048]{2,1,0:T(8,128)(2,1)} %collective-permute-done.24.refs_1_), channel_id=1, source_target_pairs={{0,2},{1,3},{2,0},{3,1},{4,6},{5,7},{6,4},{7,5},{8,10},{9,11},{10,... | collective-permute-start | bytes 3145736 | tf_op jit(solution)/shard_map/ppermute | solution.py:629
  158.7 28.8 %collective-permute-start.30 = (bf16[2,2,4,64,2048]{4,3,2,1,0:T(8,128)(2,1)}, bf16[2,2,4,64,2048]{4,3,2,1,0:T(8,128)(2,1)}, u32[]{:S(2)}, u32[]{:S(2)}) collective-permute-start(bf16[2,2,4,64,2048]{4,3,2,1,0:T(8,128)(2,1)} %fc2_grad_far.1), channel_id=1, source_target_pairs={{0,2},{1,3},{2,0},{3,1},{4,6},{5,7},{6,4},{7,5},{8,10},{9,11},{10,... | collective-permute-start | bytes 12582920 | tf_op jit(solution)/shard_map/ppermute | solution.py:629
  187.4 37.6 %collective-permute-start.33 = (bf16[2,2,4,64,2048]{4,3,2,1,0:T(8,128)(2,1)}, bf16[2,2,4,64,2048]{4,3,2,1,0:T(8,128)(2,1)}, u32[]{:S(2)}, u32[]{:S(2)}) collective-permute-start(bf16[2,2,4,64,2048]{4,3,2,1,0:T(8,128)(2,1)} %fc1_grad_far.1), channel_id=1, source_target_pairs={{0,2},{1,3},{2,0},{3,1},{4,6},{5,7},{6,4},{7,5},{8,10},{9,11},{10,... | collective-permute-start | bytes 12582920 | tf_op jit(solution)/shard_map/ppermute | solution.py:629
  193.5 26.4 %collective-permute-start.31 = (bf16[2,4,64,2048]{3,2,1,0:T(8,128)(2,1)}, bf16[2,4,64,2048]{3,2,1,0:T(8,128)(2,1)}, u32[]{:S(2)}, u32[]{:S(2)}) collective-permute-start(bf16[2,4,64,2048]{3,2,1,0:T(8,128)(2,1)} %get-tuple-element.158), channel_id=1, source_target_pairs={{0,1},{1,0},{2,6},{3,7},{4,5},{5,4},{6,2},{7,3},{8,9},{9,8},{10,14... | collective-permute-start | bytes 6291464 | tf_op jit(solution)/shard_map/ppermute | solution.py:629
  222.7 16.6 %collective-permute-start.34 = (bf16[4,64,2048]{2,1,0:T(8,128)(2,1)S(1)}, bf16[4,64,2048]{2,1,0:T(8,128)(2,1)S(1)}, u32[]{:S(2)}, u32[]{:S(2)}) collective-permute-start(bf16[4,64,2048]{2,1,0:T(8,128)(2,1)S(1)} %get-tuple-element.223), channel_id=1, source_target_pairs={{0,4},{1,5},{2,3},{3,2},{4,0},{5,1},{6,7},{7,6},{8,12},{9,13},{10,... | collective-permute-start | bytes 3145736 | tf_op jit(solution)/shard_map/ppermute | solution.py:629
  230.6 46.7 %collective-permute-start.39 = (bf16[2,4,64,2048]{3,2,1,0:T(8,128)(2,1)}, bf16[2,4,64,2048]{3,2,1,0:T(8,128)(2,1)}, u32[]{:S(2)}, u32[]{:S(2)}) collective-permute-start(bf16[2,4,64,2048]{3,2,1,0:T(8,128)(2,1)} %get-tuple-element.170), channel_id=1, source_target_pairs={{0,1},{1,0},{2,6},{3,7},{4,5},{5,4},{6,2},{7,3},{8,9},{9,8},{10,14... | collective-permute-start | bytes 6291464 | tf_op jit(solution)/shard_map/ppermute | solution.py:629
  232.2 43.5 %collective-permute-start.35 = (bf16[2,4,64,512]{3,2,1,0:T(8,128)(2,1)}, bf16[2,4,64,512]{3,2,1,0:T(8,128)(2,1)}, u32[]{:S(2)}, u32[]{:S(2)}) collective-permute-start(bf16[2,4,64,512]{3,2,1,0:T(8,128)(2,1)} %get-tuple-element.168), channel_id=1, source_target_pairs={{0,1},{1,0},{2,6},{3,7},{4,5},{5,4},{6,2},{7,3},{8,9},{9,8},{10,14... | collective-permute-start | bytes 1572872 | tf_op jit(solution)/shard_map/ppermute | solution.py:629
  240.7 35.1 %collective-permute-start.36 = (bf16[64,2048]{1,0:T(8,128)(2,1)}, bf16[64,2048]{1,0:T(8,128)(2,1)}, u32[]{:S(2)}, u32[]{:S(2)}) collective-permute-start(bf16[64,2048]{1,0:T(8,128)(2,1)} %get-tuple-element.232), channel_id=1, source_target_pairs={{0,8},{1,9},{2,10},{3,11},{4,12},{5,13},{6,14},{7,15},{8,0},{9,1},... | collective-permute-start | bytes 786440 | tf_op jit(solution)/shard_map/ppermute | solution.py:629
  246.9 28.8 %collective-permute-start.37 = (bf16[64,2048]{1,0:T(8,128)(2,1)}, bf16[64,2048]{1,0:T(8,128)(2,1)}, u32[]{:S(2)}, u32[]{:S(2)}) collective-permute-start(bf16[64,2048]{1,0:T(8,128)(2,1)} %get-tuple-element.231), channel_id=1, source_target_pairs={{0,16},{1,17},{2,18},{3,19},{4,20},{5,21},{6,22},{7,23},{8,24},{9,... | collective-permute-start | bytes 786440 | tf_op jit(solution)/shard_map/ppermute | solution.py:629
  246.9 28.9 %collective-permute-start.38 = (bf16[64,2048]{1,0:T(8,128)(2,1)}, bf16[64,2048]{1,0:T(8,128)(2,1)}, u32[]{:S(2)}, u32[]{:S(2)}) collective-permute-start(bf16[64,2048]{1,0:T(8,128)(2,1)} %get-tuple-element.230), channel_id=1, source_target_pairs={{0,24},{1,25},{2,26},{3,27},{4,28},{5,29},{6,30},{7,31},{8,16},{9,... | collective-permute-start | bytes 786440 | tf_op jit(solution)/shard_map/ppermute | solution.py:629
  285.7 26.7 %collective-permute-start.41 = (bf16[4,64,2560]{2,1,0:T(8,128)(2,1)}, bf16[4,64,2560]{2,1,0:T(8,128)(2,1)}, u32[]{:S(2)}, u32[]{:S(2)}) collective-permute-start(bf16[4,64,2560]{2,1,0:T(8,128)(2,1)} %get-tuple-element.218), channel_id=1, source_target_pairs={{0,4},{1,5},{2,3},{3,2},{4,0},{5,1},{6,7},{7,6},{8,12},{9,13},{10,... | collective-permute-start | bytes 3932168 | tf_op jit(solution)/shard_map/ppermute | solution.py:629
  297.3 22.7 %collective-permute-start.42 = (bf16[2,4,64,1536]{3,2,1,0:T(8,128)(2,1)}, bf16[2,4,64,1536]{3,2,1,0:T(8,128)(2,1)S(1)}, u32[]{:S(2)}, u32[]{:S(2)}) collective-permute-start(bf16[2,4,64,1536]{3,2,1,0:T(8,128)(2,1)} %get-tuple-element.184), channel_id=1, source_target_pairs={{0,1},{1,0},{2,6},{3,7},{4,5},{5,4},{6,2},{7,3},{8,9},{9,8},{10,14... | collective-permute-start | bytes 4718600 | tf_op jit(solution)/shard_map/ppermute | solution.py:629
  320.6 30.2 %collective-permute-start.49 = (bf16[4,64,1536]{2,1,0:T(8,128)(2,1)S(1)}, bf16[4,64,1536]{2,1,0:T(8,128)(2,1)}, u32[]{:S(2)}, u32[]{:S(2)}) collective-permute-start(bf16[4,64,1536]{2,1,0:T(8,128)(2,1)S(1)} %get-tuple-element.224), channel_id=1, source_target_pairs={{0,4},{1,5},{2,3},{3,2},{4,0},{5,1},{6,7},{7,6},{8,12},{9,13},{10,... | collective-permute-start | bytes 2359304 | tf_op jit(solution)/shard_map/ppermute | solution.py:629
  323.9 15.3 %collective-permute-start.46 = (bf16[64,2560]{1,0:T(8,128)(2,1)S(1)}, bf16[64,2560]{1,0:T(8,128)(2,1)S(1)}, u32[]{:S(2)}, u32[]{:S(2)}) collective-permute-start(bf16[64,2560]{1,0:T(8,128)(2,1)S(1)} %copy-done.54), channel_id=1, source_target_pairs={{0,8},{1,9},{2,10},{3,11},{4,12},{5,13},{6,14},{7,15},{8,0},{9,1},... | collective-permute-start | bytes 983048 | tf_op jit(solution)/shard_map/ppermute | solution.py:629
  325.1 25.6 %collective-permute-start.47 = (bf16[64,2560]{1,0:T(8,128)(2,1)S(1)}, bf16[64,2560]{1,0:T(8,128)(2,1)}, u32[]{:S(2)}, u32[]{:S(2)}) collective-permute-start(bf16[64,2560]{1,0:T(8,128)(2,1)S(1)} %get-tuple-element.227), channel_id=1, source_target_pairs={{0,16},{1,17},{2,18},{3,19},{4,20},{5,21},{6,22},{7,23},{8,24},{9,... | collective-permute-start | bytes 983048 | tf_op jit(solution)/shard_map/ppermute | solution.py:629
  326.0 24.7 %collective-permute-start.48 = (bf16[64,2560]{1,0:T(8,128)(2,1)S(1)}, bf16[64,2560]{1,0:T(8,128)(2,1)}, u32[]{:S(2)}, u32[]{:S(2)}) collective-permute-start(bf16[64,2560]{1,0:T(8,128)(2,1)S(1)} %get-tuple-element.226), channel_id=1, source_target_pairs={{0,24},{1,25},{2,26},{3,27},{4,28},{5,29},{6,30},{7,31},{8,16},{9,... | collective-permute-start | bytes 983048 | tf_op jit(solution)/shard_map/ppermute | solution.py:629
  352.1 13.7 %collective-permute-start.50 = (bf16[64,1536]{1,0:T(8,128)(2,1)S(1)}, bf16[64,1536]{1,0:T(8,128)(2,1)S(1)}, u32[]{:S(2)}, u32[]{:S(2)}) collective-permute-start(bf16[64,1536]{1,0:T(8,128)(2,1)S(1)} %get-tuple-element.237), channel_id=1, source_target_pairs={{0,8},{1,9},{2,10},{3,11},{4,12},{5,13},{6,14},{7,15},{8,0},{9,1},... | collective-permute-start | bytes 589832 | tf_op jit(solution)/shard_map/ppermute | solution.py:629
  358.4 19.3 %collective-permute-start.54 = (bf16[64,1536]{1,0:T(8,128)(2,1)S(1)}, bf16[64,1536]{1,0:T(8,128)(2,1)S(1)}, u32[]{:S(2)}, u32[]{:S(2)}) collective-permute-start(bf16[64,1536]{1,0:T(8,128)(2,1)S(1)} %get-tuple-element.236), channel_id=1, source_target_pairs={{0,16},{1,17},{2,18},{3,19},{4,20},{5,21},{6,22},{7,23},{8,24},{9,... | collective-permute-start | bytes 589832 | tf_op jit(solution)/shard_map/ppermute | solution.py:629
  358.4 19.3 %collective-permute-start.55 = (bf16[64,1536]{1,0:T(8,128)(2,1)S(1)}, bf16[64,1536]{1,0:T(8,128)(2,1)S(1)}, u32[]{:S(2)}, u32[]{:S(2)}) collective-permute-start(bf16[64,1536]{1,0:T(8,128)(2,1)S(1)} %get-tuple-element.235), channel_id=1, source_target_pairs={{0,24},{1,25},{2,26},{3,27},{4,28},{5,29},{6,30},{7,31},{8,16},{9,... | collective-permute-start | bytes 589832 | tf_op jit(solution)/shard_map/ppermute | solution.py:629
  365.8 14.7 %collective-permute-start.51 = (f32[12,1024]{1,0:T(8,128)S(1)}, f32[12,1024]{1,0:T(8,128)S(1)}, u32[]{:S(2)}, u32[]{:S(2)}) collective-permute-start(f32[12,1024]{1,0:T(8,128)S(1)} %add.92), channel_id=1, source_target_pairs={{0,8},{1,9},{2,10},{3,11},{4,12},{5,13},{6,14},{7,15},{8,0},{9,1},... | collective-permute-start | bytes 147464 | tf_op jit(solution)/shard_map/ppermute | solution.py:629
  366.2 16.1 %collective-permute-start.52 = (f32[12,1024]{1,0:T(8,128)S(1)}, f32[12,1024]{1,0:T(8,128)S(1)}, u32[]{:S(2)}, u32[]{:S(2)}) collective-permute-start(f32[12,1024]{1,0:T(8,128)S(1)} %add.92), channel_id=1, source_target_pairs={{0,16},{1,17},{2,18},{3,19},{4,20},{5,21},{6,22},{7,23},{8,24},{9,... | collective-permute-start | bytes 147464 | tf_op jit(solution)/shard_map/ppermute | solution.py:629
  367.2 15.1 %collective-permute-start.53 = (f32[12,1024]{1,0:T(8,128)S(1)}, f32[12,1024]{1,0:T(8,128)S(1)}, u32[]{:S(2)}, u32[]{:S(2)}) collective-permute-start(f32[12,1024]{1,0:T(8,128)S(1)} %add.92), channel_id=1, source_target_pairs={{0,24},{1,25},{2,26},{3,27},{4,28},{5,29},{6,30},{7,31},{8,16},{9,... | collective-permute-start | bytes 147464 | tf_op jit(solution)/shard_map/ppermute | solution.py:629
  (71 other events, 730.3 us)
